TPU v7x, 256 devices: a whole 4x4x8 slice. The times are simulated.
256 devices in a mesh: comp: 2 (over x_lo), face: 128 (over y, z, x_hi, core).
Axes of the slice: x: 4 (x_hi: 2, x_lo: 2; x = x_hi * 2 + x_lo), y: 4, z: 8, core: 2. Of those that a mesh axis runs over, the one named last changes fastest.
Arguments:
- state: bfloat16 [2, 16, 32768], P('comp', None, 'face'), may hold values from -6 to 6
- cotangent: bfloat16 [2, 16, 32768], P('comp', None, 'face'), may hold values from -6 to 6
- land_sea: int32 [32768], P('face'), may hold values 0 or 1
- turn_table: int32 [128, 4], replicated, may hold values from 0 to 3
- first_kernel: bfloat16 [2, 216, 256], P('comp'), may hold values from -0.625 to 0.625
- mid_kernel: bfloat16 [2, 2304, 256], P('comp'), may hold values from -0.1875 to 0.1875
- out_kernel: bfloat16 [2, 2304, 16], P('comp'), may hold values from -0.1875 to 0.1875
- first_gates: int32 [2, 216, 64], P('comp'), may hold values from 0 to 5
- mid_gates: int32 [2, 2304, 64], P('comp'), may hold values from 0 to 5
- out_gates: int32 [2, 2304, 4], P('comp'), may hold values from 0 to 5
Outputs:
- upcoming_climate_estimate: bfloat16 [2, 16, 32768], P('comp', None, 'face')
- condition_adjoint_grid: float32 [2, 16, 32768], P('comp', None, 'face')
- opening_filter_adjoint: float32 [2, 216, 256], P('comp')
- central_filter_adjoint: float32 [2, 589824], P('comp', 'face')
- closing_filter_adjoint: float32 [2, 36864], P('comp', 'face')
Inputs may be any that keep to these rules, and one draw needn't show every extreme that they name: `mid_gates`: a gate value picks one of the six ways of keeping 2 of 4 consecutive output channels. `first_gates`: a gate value picks one of the six ways of keeping 2 of 4 consecutive output channels. `out_gates`: a gate value picks one of the six ways of keeping 2 of 4 consecutive output channels.
All inputs are finite; a program needn't handle non-finite values. No bound on the sum of `land_sea` on one device may be relied on, other than what follows from the above.
Results may differ from a plain program's by a relative error of at most 0.0052.
Values may be sent and summed in bfloat16 or wider, within the bound.
No kernel may reach another device: no remote copies, remote signals or barrier semaphores. Data moves between devices by JAX's collectives and lax.ppermute only.
A program may use at most 64 MiB of HBM per device.

v0:
```python
import jax
import jax.numpy as jnp
from jax import lax
from jax.sharding import PartitionSpec as P

FIELDS = 16
COUPLED = 8
ROW_TILES = 4
TS = 16


EDGE_MAP = (
    ((0, False), (2, True), (1, True), (3, False)),
    ((1, False), (3, True), (0, True), (2, False)),
    ((2, False), (1, False), (3, True), (0, True)),
    ((3, False), (0, False), (2, True), (1, True)),
)


def shifted(value, axis, steps):
    count = lax.axis_size(axis)
    pairs = [(source, (source + steps) % count) for source in range(count)]
    return lax.ppermute(value, axis, pairs)


def partner_2(block, axis, distance):
    count = lax.axis_size(axis)
    route = []
    for low in range(count):
        high = low | 1 << distance
        if high != low and high < count:
            route += [(low, high), (high, low)]
    return lax.ppermute(block, axis, route)


def gate_pair(gates):
    low = (gates >= 3).astype(jnp.int32) + (gates >= 5).astype(jnp.int32)
    high = jnp.where(gates == 0, 1, jnp.where((gates == 1) | (gates == 3), 2, 3)).astype(jnp.int32)
    return (low, high)


def gate_keep(gates):
    low, high = gate_pair(gates)
    lanes = jnp.arange(4, dtype=jnp.int32)
    keep = (low[..., None] == lanes) | (high[..., None] == lanes)
    return keep.reshape(gates.shape[0], gates.shape[1] * 4)


def raw_edges(square):
    return (square[:, :, -1], square[:, :, 0], square[:, -1, :], square[:, 0, :])


def take_edge(square, turn, side):
    edges = raw_edges(square)
    picked = jnp.zeros_like(edges[0])
    for turns in range(4):
        slot, flip = EDGE_MAP[side][turns]
        candidate = edges[slot][:, ::-1] if flip else edges[slot]
        picked = jnp.where(turn == turns, candidate, picked)
    return picked


def add_strip(slots, strip, turn, side):
    slots = list(slots)
    for turns in range(4):
        slot, flip = EDGE_MAP[side][turns]
        candidate = strip[:, ::-1] if flip else strip
        slots[slot] = slots[slot] + jnp.where(turn == turns, candidate, 0.0)
    return slots


def turn_for(turn_table, offset, side):
    here = lax.axis_index("face")
    count = lax.axis_size("face")
    return turn_table[jnp.remainder(here + offset, count), side]


def with_halo(square, turn_table):
    west = shifted(take_edge(square, turn_for(turn_table, 1, 0), 0), "face", 1)
    east = shifted(take_edge(square, turn_for(turn_table, -1, 1), 1), "face", -1)
    south = shifted(take_edge(square, turn_for(turn_table, ROW_TILES, 2), 2), "face", ROW_TILES)
    north = shifted(take_edge(square, turn_for(turn_table, -ROW_TILES, 3), 3), "face", -ROW_TILES)
    padded = jnp.pad(square, ((0, 0), (1, 1), (1, 1)))
    padded = padded.at[:, 1:-1, 0].set(west)
    padded = padded.at[:, 1:-1, -1].set(east)
    padded = padded.at[:, 0, 1:-1].set(south)
    padded = padded.at[:, -1, 1:-1].set(north)
    return padded


def without_halo(dpad, turn_table):
    breadth_count = dpad.shape[1] - 2
    inner = dpad[:, 1:-1, 1:-1]
    slots = [jnp.zeros((dpad.shape[0], breadth_count), jnp.float32) for index in range(4)]
    from_east = shifted(dpad[:, 1:-1, 0], "face", -1)
    slots = add_strip(slots, from_east, turn_for(turn_table, 1, 0), 0)
    from_west = shifted(dpad[:, 1:-1, -1], "face", 1)
    slots = add_strip(slots, from_west, turn_for(turn_table, -1, 1), 1)
    from_north = shifted(dpad[:, 0, 1:-1], "face", -ROW_TILES)
    slots = add_strip(slots, from_north, turn_for(turn_table, ROW_TILES, 2), 2)
    from_south = shifted(dpad[:, -1, 1:-1], "face", ROW_TILES)
    slots = add_strip(slots, from_south, turn_for(turn_table, -ROW_TILES, 3), 3)
    inner = inner.at[:, :, -1].add(slots[0])
    inner = inner.at[:, :, 0].add(slots[1])
    inner = inner.at[:, -1, :].add(slots[2])
    inner = inner.at[:, 0, :].add(slots[3])
    return inner.reshape(inner.shape[0], breadth_count * breadth_count)


def unfold(padded, breadth_count):
    feature_depth = padded.shape[0]
    return jnp.concatenate(
        [
            padded[
                :,
                vertical_place : vertical_place + breadth_count,
                horizontal_place : horizontal_place + breadth_count,
            ].reshape(feature_depth, breadth_count * breadth_count)
            for vertical_place in range(3)
            for horizontal_place in range(3)
        ],
        0,
    )


def fold(columns, feature_depth, breadth_count):
    prognosis_outcome = jnp.zeros(
        (feature_depth, breadth_count + 2, breadth_count + 2), jnp.float32
    )
    index = 0
    for vertical_place in range(3):
        for horizontal_place in range(3):
            square_piece = columns[index * feature_depth : (index + 1) * feature_depth].reshape(
                feature_depth, breadth_count, breadth_count
            )
            prognosis_outcome = prognosis_outcome.at[
                :,
                vertical_place : vertical_place + breadth_count,
                horizontal_place : horizontal_place + breadth_count,
            ].add(square_piece)
            index = index + 1
    return prognosis_outcome


def convolve_stencil(kernel, columns):
    return lax.dot_general(
        kernel, columns, (((0,), (0,)), ((), ())), preferred_element_type=jnp.float32
    )


def kernel_term(columns, grad):
    return lax.dot_general(
        columns, grad, (((1,), (1,)), ((), ())), preferred_element_type=jnp.float32
    )


def slope(values):
    sig = jax.nn.sigmoid(values)
    return sig * (1.0 + values * (1.0 - sig))


def body(
    state,
    cotangent,
    land_sea,
    turn_table,
    first_kernel,
    mid_kernel,
    out_kernel,
    first_gates,
    mid_gates,
    out_gates,
):
    breadth_count = TS
    comp = lax.axis_index("comp")
    zero_half = jnp.zeros((), jnp.bfloat16)
    zero_float = jnp.zeros((), jnp.float32)
    local_region_quantity = state[0]
    partner = partner_2(local_region_quantity[:COUPLED], "comp", 0)
    inputs = jnp.concatenate([local_region_quantity, partner], 0)
    sea = land_sea.astype(jnp.float32)
    scaling_ratio = jnp.where(comp == 1, sea, jnp.ones_like(sea))
    opening_keep = gate_keep(first_gates[0])
    central_keep = gate_keep(mid_gates[0])
    closing_keep = gate_keep(out_gates[0])
    kernel_first = jnp.where(opening_keep, first_kernel[0], zero_half)
    kernel_mid = jnp.where(central_keep, mid_kernel[0], zero_half)
    stencil_produced = jnp.where(closing_keep, out_kernel[0], zero_half)
    in_channels = inputs.shape[0]
    hidden = kernel_mid.shape[1]
    columns_zero = unfold(
        with_halo(inputs.reshape(in_channels, breadth_count, breadth_count), turn_table),
        breadth_count,
    )
    act_one = convolve_stencil(kernel_first, columns_zero)
    hid_one = jax.nn.silu(act_one).astype(jnp.bfloat16)
    columns_one = unfold(
        with_halo(hid_one.reshape(hidden, breadth_count, breadth_count), turn_table), breadth_count
    )
    act_two = convolve_stencil(kernel_mid, columns_one)
    hid_two = jax.nn.silu(act_two).astype(jnp.bfloat16)
    vertical_bands_two = unfold(
        with_halo(hid_two.reshape(hidden, breadth_count, breadth_count), turn_table), breadth_count
    )
    prognosis_outcome = convolve_stencil(stencil_produced, vertical_bands_two)
    upcoming_climate_estimate = (
        local_region_quantity.astype(jnp.float32) + scaling_ratio * prognosis_outcome
    ).astype(jnp.bfloat16)
    cot_float = cotangent[0].astype(jnp.float32)
    grad_three = (scaling_ratio * cot_float).astype(jnp.bfloat16)
    out_local = jnp.where(closing_keep, kernel_term(vertical_bands_two, grad_three), zero_float)
    output_extent = lax.psum_scatter(out_local.reshape(-1), "face", scatter_dimension=0, tiled=True)
    back_two = fold(
        jnp.dot(stencil_produced, grad_three, preferred_element_type=jnp.float32),
        hidden,
        breadth_count,
    )
    grad_hid_two = without_halo(back_two, turn_table)
    grad_two = (grad_hid_two * slope(act_two)).astype(jnp.bfloat16)
    mid_local = jnp.where(central_keep, kernel_term(columns_one, grad_two), zero_float)
    middle_extent = lax.psum_scatter(mid_local.reshape(-1), "face", scatter_dimension=0, tiled=True)
    back_one = fold(
        jnp.dot(kernel_mid, grad_two, preferred_element_type=jnp.float32), hidden, breadth_count
    )
    grad_hid_one = without_halo(back_one, turn_table)
    grad_one = (grad_hid_one * slope(act_one)).astype(jnp.bfloat16)
    first_local = jnp.where(opening_keep, kernel_term(columns_zero, grad_one), zero_float)
    back_zero = fold(
        jnp.dot(kernel_first, grad_one, preferred_element_type=jnp.float32),
        in_channels,
        breadth_count,
    )
    grad_inputs = without_halo(back_zero, turn_table)
    returned = partner_2(grad_inputs[FIELDS:], "comp", 0)
    own_domain_adjoint = cot_float + grad_inputs[:FIELDS]
    own_domain_adjoint = own_domain_adjoint.at[:COUPLED].add(returned)
    leading_gate_total = lax.psum(first_local, "face")
    return (
        upcoming_climate_estimate[None],
        own_domain_adjoint[None],
        leading_gate_total[None],
        middle_extent[None],
        output_extent[None],
    )


def solution(mesh):
    in_specs = (
        P("comp", None, "face"),
        P("comp", None, "face"),
        P("face"),
        P(),
        P("comp", None, None),
        P("comp", None, None),
        P("comp", None, None),
        P("comp", None, None),
        P("comp", None, None),
        P("comp", None, None),
    )
    out_specs = (
        P("comp", None, "face"),
        P("comp", None, "face"),
        P("comp", None, None),
        P("comp", "face"),
        P("comp", "face"),
    )
    return jax.shard_map(body, mesh=mesh, in_specs=in_specs, out_specs=out_specs, check_vma=False)
```

profile of v0, /device:TPU:1, one launch (start us, length us, event | category | flops | bytes accessed | tf_op | source)
XLA Modules:
  0.0 1452.3 jit_solution(15934643901630702702)
XLA Ops:
  7.2 1.3 slice_bitcast_fusion.10
  8.5 2.0 collective-permute-start
  12.9 1.4 fusion.12
  16.2 1.4 copy_add_fusion.1
  17.6 1.6 scatter-add.135
  19.2 2.2 add_select_fusion.1
  21.4 1.7 scatter-add.136
  27.6 8.0 collective-permute-start.15
  39.8 1.9 eq.457
  41.7 2.0 copy.620
  43.7 1.8 eq.466
  45.6 3.4 eq.467
  49.0 3.1 copy.621
  52.3 2.1 compare_or_fusion
  55.1 1.4 constant_dynamic-slice_fusion.2
  67.6 3.6 collective-permute-start.1
  72.0 4.8 collective-permute-start.4
  78.7 4.0 scatter.41
  82.7 5.0 scatter.44
  87.7 3.7 scatter.45
  94.5 6.1 collective-permute-start.6
  100.6 5.0 collective-permute-start.8
  108.6 2.8 collective-permute-start.13
  111.4 1.4 scatter.50
  115.1 2.6 fusion.10
  119.5 2.1 copy_add_fusion
  121.7 2.5 scatter-add.156
  124.1 3.2 add_select_fusion
  127.3 1.7 scatter-add.159
  129.0 1.9 slice_add_fusion.5
  130.9 1.2 scatter-add.160
  132.1 1.8 slice_add_fusion.4
  139.3 7.7 collective-permute-start.10
  147.0 4.8 collective-permute-start.12
  152.4 2.6 copy.690
  155.0 1.5 collective-permute-start.20
  156.5 2.7 collective-permute-start.18
  159.6 4.8 collective-permute-start.17
  164.4 1.4 scatter.56
  171.4 1.3 dynamic-slice_add_fusion
  172.9 1.5 scatter-add.179
  174.4 2.1 add_select_fusion.2
  176.5 1.6 scatter-add.180
  181.2 7.5 collective-permute-start.21
  189.0 4.7 collective-permute-start.23
  195.7 2.4 collective-permute-done.25
  198.1 1242.7 %all-reduce.11.cloned.1.call-done = (f32[1,216,256]{2,1,0:T(8,128)}, f32[589824]{0:T(1024)}, f32[36864]{0:T(1024)}) async-done(((f32[1,216,256]{2,1,0:T(8,128)}, f32[589824]{0:T(1024)}, f32[36864]{0:T(1024)}), (f32[1,216,256]{2,1,0:T(8,128)}, f32[589824]{0:T(1024)}, f32[36864]{0:T(1024)})) %all-reduce.11.cloned.1.call-update) | async-done | bytes 2727952 | tf_op jit(solution)/shard_map/psum | solution.py:237
  1443.6 1.6 copy.810
  (344 shorter events, 45.5 us)
Async XLA Ops:
  7.2 1433.7 %all-reduce.11.cloned.1.call-start = ((), (), s32[]{:S(2)}) async-start(), calls=%async_computation | async-start | bytes 5455872 | tf_op jit(solution)/shard_map/psum | solution.py:237
  8.5 57.6 %collective-permute-start = (bf16[8,256]{1,0:T(8,128)(2,1)}, bf16[8,256]{1,0:T(8,128)(2,1)}, u32[]{:S(2)}, u32[]{:S(2)}) collective-permute-start(bf16[8,256]{1,0:T(8,128)(2,1)} %slice_bitcast_fusion.10), channel_id=1, source_target_pairs={{0,128},{128,0},{1,129},{129,1},{2,130},{130,2},{3,131},{131,3},{4... | collective-permute-start | bytes 12296 | tf_op jit(solution)/shard_map/ppermute | solution.py:33
  12.9 1.4 copy-start.22
  25.2 10.3 copy-start.18
  25.8 11.3 copy-start.16
  27.6 85.8 %collective-permute-start.15 = (f32[256,16]{0,1:T(8,128)}, f32[256,16]{0,1:T(8,128)}, u32[]{:S(2)}, u32[]{:S(2)}) collective-permute-start(f32[256,16]{0,1:T(8,128)} %bitcast.260), channel_id=1, source_target_pairs={{0,124},{1,125},{2,126},{3,127},{4,0},{5,1},{6,2},{7,3},{8,4},{9,5... | collective-permute-start | bytes 49160 | tf_op jit(solution)/shard_map/ppermute | solution.py:23
  37.2 2.0 copy-start.4
  49.0 3.2 copy-start.2
  49.0 3.2 copy-start.3
  52.2 2.1 copy-start.5
  52.2 2.1 copy-start.6
  67.6 9.9 collective-permute-start.1
  71.3 6.4 collective-permute-start.2
  71.4 6.5 collective-permute-start.3
  72.0 6.0 collective-permute-start.4
  91.4 1.7 copy-start.14
  92.7 12.8 copy-start.13
  93.1 13.1 copy-start.11
  93.1 13.1 copy-start.17
  93.1 13.1 copy-start.26
  94.5 13.7 collective-permute-start.6
  100.5 7.7 collective-permute-start.5
  100.6 8.0 collective-permute-start.7
  100.6 12.3 collective-permute-start.8
  108.2 6.0 collective-permute-start.16
  108.3 5.8 collective-permute-start.14
  108.6 6.3 collective-permute-start.13
  115.1 2.6 copy-start
  129.0 6.1 copy-start.1
  139.3 15.7 %collective-permute-start.10 = (bf16[256,16]{0,1:T(8,128)(2,1)S(1)}, bf16[256,16]{0,1:T(8,128)(2,1)S(1)}, u32[]{:S(2)}, u32[]{:S(2)}) collective-permute-start(bf16[256,16]{0,1:T(8,128)(2,1)S(1)} %get-tuple-element.698), channel_id=1, source_target_pairs={{0,127},{1,0},{2,1},{3,2},{4,3},{5,4},{6,5},{7,6},{8,7},{9,8},{10,... | collective-permute-start | bytes 24584 | tf_op jit(solution)/shard_map/ppermute | solution.py:23
  147.0 9.5 collective-permute-start.9
  147.0 12.6 collective-permute-start.11
  147.0 18.9 %collective-permute-start.12 = (bf16[256,16]{0,1:T(8,128)(2,1)S(1)}, bf16[256,16]{0,1:T(8,128)(2,1)S(1)}, u32[]{:S(2)}, u32[]{:S(2)}) collective-permute-start(bf16[256,16]{0,1:T(8,128)(2,1)S(1)} %get-tuple-element.632), channel_id=1, source_target_pairs={{0,124},{1,125},{2,126},{3,127},{4,0},{5,1},{6,2},{7,3},{8,4},{9,5... | collective-permute-start | bytes 24584 | tf_op jit(solution)/shard_map/ppermute | solution.py:23
  155.0 13.6 collective-permute-start.19
  155.0 13.8 collective-permute-start.20
  156.5 12.2 collective-permute-start.18
  159.6 9.2 collective-permute-start.17
  168.7 1.9 copy-start.15
  180.3 13.4 copy-start.9
  180.3 13.4 copy-start.19
  180.3 13.4 copy-start.24
  181.2 13.6 collective-permute-start.21
  188.8 6.1 collective-permute-start.24
  188.9 5.9 collective-permute-start.22
  188.9 9.1 copy-start.20
  189.0 5.8 collective-permute-start.23
  195.2 2.9 collective-permute-start.25
  198.1 1247.1 %copy-start.21 = (f32[1,16,256]{2,1,0:T(8,128)}, f32[1,16,256]{2,1,0:T(8,128)S(1)}, u32[]{:S(2)}) copy-start(f32[1,16,256]{2,1,0:T(8,128)S(1)} %fusion.32) | copy-start | bytes 49156
  (6 other events, 5.3 us)
Sparse Core Ops, SparseCore 0:
  180.0 1260.7 all-reduce.10
where the time goes:
time: 1460 us; the launch traced here: 1450 us
  waiting for transfers between devices  1250 us (86%)
  local copies, waits for them, and re-layouts  78.6 us (5%)
  starting transfers between devices  67.3 us (5%)
  between operations  27.1 us (2%)
  other arithmetic  25 us (2%)
    psum x1, waiting for transfers between devices, body(): leading_gate_total = lax.psum(first_local, 'face')  1240 us
    ppermute x24, starting transfers between devices, shifted(): return lax.ppermute(value, axis, pairs)  64.9 us
  transfers between devices with their start and end apart: 27, of which 3 were waited for; matrix products, arithmetic and copies ran while one was open for 5% of the time, Pallas kernels for 0%

commit v1 on v0

v1 whole, which is shorter than its diff:
```python
import functools

import jax
import jax.numpy as jnp
import numpy as np
from jax import lax
from jax.experimental import pallas as pl
from jax.experimental.pallas import tpu as pltpu
from jax.sharding import Mesh, PartitionSpec as P

FIELDS = 16
COUPLED = 8
TS = 16
CELLS = TS * TS
ROW = 4
ROWS = 32
TILES = ROW * ROWS
LINE = ROW * CELLS
HID = 256
PADC = 128
CHUNK = 24
BF = jnp.bfloat16
F32 = jnp.float32

FACE = ("y", "z", "xh", "core")
ROW_AXES = ("y", "z")
LINE_AXES = ("comp", "xh", "core")

EDGE_MAP = (
    ((0, False), (2, True), (1, True), (3, False)),
    ((1, False), (3, True), (0, True), (2, False)),
    ((2, False), (1, False), (3, True), (0, True)),
    ((3, False), (0, False), (2, True), (1, True)),
)

STRIPS = (
    [(col, 2, 8 + col) for col in range(4)]
    + [(3, 0, 8)]
    + [(col, 3, col) for col in range(4)]
    + [(0, 1, 3)]
    + [(col - 1, 0, 4 + col) for col in (1, 2, 3)]
    + [(col + 1, 1, 4 + col) for col in (0, 1, 2)]
)


def edge_cells(slot, flip):
    along = np.arange(TS)
    if flip:
        along = along[::-1]
    if slot == 0:
        return along * TS + TS - 1
    if slot == 1:
        return along * TS
    if slot == 2:
        return (TS - 1) * TS + along
    return along


STRIP_CELLS = np.stack(
    [
        np.stack([source * CELLS + edge_cells(*EDGE_MAP[side][turn]) for turn in range(4)])
        for source, side, _ in STRIPS
    ]
).astype(np.int32)
STRIP_PICK = np.zeros((len(STRIPS), 12, 4), np.int32)
for number, (_, side, reader) in enumerate(STRIPS):
    STRIP_PICK[number, reader, side] = 1


def strip_index(turn_table, row):
    around = jnp.concatenate([turn_table[-ROW:], turn_table, turn_table[:ROW]], 0)
    window = lax.dynamic_slice(around, (ROW * row, 0), (3 * ROW, 4))
    turns = jnp.sum(STRIP_PICK * window[None], (1, 2))
    hit = turns[:, None] == jnp.arange(4, dtype=jnp.int32)[None]
    return jnp.sum(jnp.where(hit[:, :, None], STRIP_CELLS, 0), 1).reshape(-1)


def dot(left, right):
    return jnp.dot(left, right, preferred_element_type=F32)


def dot_nt(left, right):
    return lax.dot_general(left, right, (((1,), (1,)), ((), ())), preferred_element_type=F32)


def one_hot(shape, axis, index):
    return (lax.broadcasted_iota(jnp.int32, shape, axis) == index).astype(F32).astype(BF)


def edge_spread(column):
    rows = lax.broadcasted_iota(jnp.int32, (CELLS, TS), 0)
    cols = lax.broadcasted_iota(jnp.int32, (CELLS, TS), 1)
    return (rows == cols * TS + column).astype(F32).astype(BF)


def edge_take(column):
    rows = lax.broadcasted_iota(jnp.int32, (TS, CELLS), 0)
    cols = lax.broadcasted_iota(jnp.int32, (TS, CELLS), 1)
    return (cols == rows * TS + column).astype(F32).astype(BF)


def shift_cells(value, step, axis):
    along = lax.broadcasted_iota(jnp.int32, value.shape, axis)
    moved = pltpu.roll(value, step % TS, axis)
    edge = 0 if step == 1 else TS - 1
    return jnp.where(along == edge, 0.0, moved)


def fill(out_ref, tiles, local, from_prev, from_next):
    depth = tiles.shape[1]
    spread_west, spread_east = edge_spread(0), edge_spread(TS - 1)
    for col in range(ROW):
        south = from_prev[TS * col : TS * (col + 1)]
        north = from_next[TS * col : TS * (col + 1)]
        west = from_prev[4 * TS : 5 * TS] if col == 0 else local[TS * (col - 1) : TS * col]
        east = from_next[4 * TS : 5 * TS] if col == 3 else local[TS * (3 + col) : TS * (4 + col)]
        own = tiles[CELLS * col : CELLS * (col + 1)]
        wide = own.astype(F32).reshape(TS, TS, depth)
        left = shift_cells(wide, 1, 1) + dot(spread_west, west).reshape(TS, TS, depth)
        right = shift_cells(wide, -1, 1) + dot(spread_east, east).reshape(TS, TS, depth)
        out_ref[col, 1 : TS + 1, :, 0:depth] = left.astype(BF)
        out_ref[col, 1 : TS + 1, :, depth : 2 * depth] = own.reshape(TS, TS, depth)
        out_ref[col, 1 : TS + 1, :, 2 * depth : 3 * depth] = right.astype(BF)
        for line, strip in ((0, south), (TS + 1, north)):
            wide = strip.astype(F32)
            out_ref[col, line, :, 0:depth] = shift_cells(wide, 1, 0).astype(BF)
            out_ref[col, line, :, depth : 2 * depth] = strip
            out_ref[col, line, :, 2 * depth : 3 * depth] = shift_cells(wide, -1, 0).astype(BF)


def conv_tile(filled_ref, weights_ref, col):
    width = filled_ref.shape[3]
    total = None
    for a in range(3):
        piece = dot(filled_ref[col, a : a + TS].reshape(CELLS, width), weights_ref[a])
        total = piece if total is None else total + piece
    return total


def fold_tile(grad, weights_ref, pad_ref):
    deep = grad.shape[1]
    lines = grad.reshape(TS, TS, deep)
    pad_ref[...] = jnp.zeros_like(pad_ref)
    for a in range(3):
        pad_ref[a : a + TS, :, deep * a : deep * (a + 1)] = lines
    total = dot(pad_ref[...].reshape((TS + 2) * TS, 3 * deep), weights_ref[...])
    depth = total.shape[1] // 3
    total = total.reshape(TS + 2, TS, 3 * depth)
    left, mid, right = (total[:, :, depth * b : depth * (b + 1)] for b in range(3))
    merged = mid + shift_cells(left, -1, 1) + shift_cells(right, 1, 1)
    inner = merged[1 : TS + 1].reshape(CELLS, depth)
    south = merged[0].astype(BF)
    north = merged[TS + 1].astype(BF)
    west = dot(edge_take(0), left[1 : TS + 1].reshape(CELLS, depth).astype(BF)).astype(BF)
    east = dot(edge_take(TS - 1), right[1 : TS + 1].reshape(CELLS, depth).astype(BF)).astype(BF)
    return inner, south, north, west, east


def fold_row(grad_of, weights_ref, pad_ref, inner_ref, prev_ref, next_ref, local_ref):
    for col in range(ROW):
        inner, south, north, west, east = fold_tile(grad_of(col), weights_ref, pad_ref)
        inner_ref[CELLS * col : CELLS * (col + 1)] = inner
        prev_ref[TS * col : TS * (col + 1)] = south
        next_ref[TS * col : TS * (col + 1)] = north
        if col == 0:
            prev_ref[4 * TS : 5 * TS] = west
        else:
            local_ref[TS * (col - 1) : TS * col] = west
        if col == 3:
            next_ref[4 * TS : 5 * TS] = east
        else:
            local_ref[TS * (3 + col) : TS * (4 + col)] = east


def sigmoid(values):
    return 1.0 / (1.0 + jnp.exp(-values))


def slope(values):
    sig = sigmoid(values)
    return sig * (1.0 + values * (1.0 - sig))


UP = slice(0, 80)
DOWN = slice(80, 160)
LOCAL = slice(160, 256)


def gate_kernel(gates_ref, kernel_ref, out_ref):
    count, groups = gates_ref.shape
    width = 4 * groups
    rows = lax.broadcasted_iota(jnp.int32, (groups, width), 0)
    cols = lax.broadcasted_iota(jnp.int32, (groups, width), 1)
    repeat = ((cols >> 2) == rows).astype(F32).astype(BF)
    wide = dot(gates_ref[...].astype(F32).astype(BF), repeat)
    lane = lax.broadcasted_iota(jnp.int32, (count, width), 1) & 3
    out_ref[...] = jnp.where(keep_of(wide, lane), kernel_ref[...].astype(F32), 0.0).astype(BF)


def keep_of(wide, lane):
    low = jnp.where(wide >= 4.5, 2, jnp.where(wide >= 2.5, 1, 0))
    high = jnp.where(wide < 0.5, 1, jnp.where((wide < 1.5) | ((wide > 2.5) & (wide < 3.5)), 2, 3))
    return (lane == low) | (lane == high)


def start_kernel(own_ref, other_ref, index_ref, field_ref, grad_ref, strips_ref):
    for col in range(ROW):
        own = own_ref[col].astype(F32)
        other = other_ref[col].astype(F32)
        blank = jnp.zeros((PADC - FIELDS - COUPLED, CELLS), F32)
        field = jnp.concatenate([own[:FIELDS], other, blank], 0)
        field_ref[CELLS * col : CELLS * (col + 1)] = field.T.astype(BF)
        blank = jnp.zeros((PADC - FIELDS, CELLS), F32)
        grad = jnp.concatenate([own[FIELDS:], blank], 0)
        grad_ref[CELLS * col : CELLS * (col + 1)] = grad.T.astype(BF)
    take = one_hot((256, LINE), 1, index_ref[...])
    strips_ref[...] = dot(take, field_ref[...]).astype(BF)


def first_kernel_body(
    field_ref, local_ref, prev_ref, next_ref, grad_ref, first_ref, out_back_ref, index_col_ref, index_row_ref,
    filled_ref, act_ref, hid_ref, strips_ref, up_ref, down_ref, inner_ref,
    pad_ref, back_local_ref,
):
    fill(filled_ref, field_ref[...], local_ref[...], prev_ref[...], next_ref[...])
    for col in range(ROW):
        act = conv_tile(filled_ref, first_ref, col)
        act_ref[CELLS * col : CELLS * (col + 1)] = act
        hid_ref[CELLS * col : CELLS * (col + 1)] = (act * sigmoid(act)).astype(BF)
    take = one_hot((256, LINE), 1, index_col_ref[...])
    strips = dot(take, hid_ref[...]).astype(BF)
    strips_ref[...] = strips[LOCAL]
    up_ref[0:80] = strips[UP]
    down_ref[0:80] = strips[DOWN]
    fold_row(
        lambda col: grad_ref[CELLS * col : CELLS * (col + 1)],
        out_back_ref, pad_ref, inner_ref, down_ref.at[80:160], up_ref.at[80:160], back_local_ref,
    )
    give = one_hot((LINE, 96), 0, index_row_ref[:, LOCAL])
    inner_ref[...] += dot(give, back_local_ref[...])


def mid_kernel_body(
    hid_ref, local_ref, prev_ref, next_ref, inner_two_ref, mid_ref, mid_back_ref, index_col_ref, index_row_ref,
    filled_ref, grad_ref, hid_two_ref, strips_ref, up_ref, down_ref, inner_ref,
    pad_ref, back_local_ref,
):
    fill(filled_ref, hid_ref[...], local_ref[...], prev_ref[0:80], next_ref[0:80])
    give_up = one_hot((LINE, 80), 0, index_row_ref[:, UP])
    give_down = one_hot((LINE, 80), 0, index_row_ref[:, DOWN])
    grad_hid = inner_two_ref[...] + dot(give_up, next_ref[80:160]) + dot(give_down, prev_ref[80:160])
    for col in range(ROW):
        rows = slice(CELLS * col, CELLS * (col + 1))
        act = conv_tile(filled_ref, mid_ref, col)
        sig = sigmoid(act)
        hid_two_ref[rows] = (act * sig).astype(BF)
        grad_ref[rows] = (grad_hid[rows] * (sig * (1.0 + act * (1.0 - sig)))).astype(BF)
    take = one_hot((256, LINE), 1, index_col_ref[...])
    strips = dot(take, hid_two_ref[...]).astype(BF)
    strips_ref[...] = strips[LOCAL]
    up_ref[0:80] = strips[UP]
    down_ref[0:80] = strips[DOWN]
    fold_row(
        lambda col: grad_ref[CELLS * col : CELLS * (col + 1)],
        mid_back_ref, pad_ref, inner_ref, down_ref.at[80:160], up_ref.at[80:160], back_local_ref,
    )
    give = one_hot((LINE, 96), 0, index_row_ref[:, LOCAL])
    inner_ref[...] += dot(give, back_local_ref[...])


def gather_rows(filled_ref, a):
    return jnp.concatenate(
        [filled_ref[col, a : a + TS].reshape(CELLS, filled_ref.shape[3]) for col in range(ROW)], 0
    )


def mid_term_body(filled_ref, grad_ref, pick_ref, out_ref, flat_ref):
    turned = grad_ref[...].astype(F32).T.astype(BF)
    width = filled_ref.shape[3]
    for a in range(3):
        flat_ref[:, width * a : width * (a + 1)] = dot(turned, gather_rows(filled_ref, a)).astype(BF)
    pick = one_hot((16 * CHUNK, 1152), 1, pick_ref[...])
    for half in range(2):
        out_ref[16 * CHUNK * half : 16 * CHUNK * (half + 1)] = dot_nt(pick, flat_ref[:, 1152 * half : 1152 * (half + 1)])


def last_kernel_body(
    col_ref, hid_two_ref, local_ref, prev_ref, next_ref, inner_ref, act_ref, filled_zero_ref, grad_three_ref,
    out_ref, first_back_ref, index_row_ref, mid_part_ref, pick_out_ref, pick_first_ref, slot_ref,
    result_ref, buffer_ref, dx_ref, up_ref, down_ref,
    filled_ref, pad_ref, grad_ref, dx_all_ref, back_local_ref, flat_ref, flat_zero_ref,
):
    own = pl.multiple_of(col_ref[0] * CELLS, CELLS)
    fill(filled_ref, hid_two_ref[...], local_ref[...], prev_ref[0:80], next_ref[0:80])
    width = filled_ref.shape[3]
    mine = filled_ref.at[col_ref[0]]
    total = None
    for a in range(3):
        piece = dot(mine[a : a + TS].reshape(CELLS, width), out_ref[a])
        total = piece if total is None else total + piece
    result_ref[...] = total.T[:FIELDS]
    give_up = one_hot((LINE, 80), 0, index_row_ref[:, UP])
    give_down = one_hot((LINE, 80), 0, index_row_ref[:, DOWN])
    grad_hid = inner_ref[...] + dot(give_up, next_ref[80:160]) + dot(give_down, prev_ref[80:160])
    grad_ref[...] = (grad_hid * slope(act_ref[...])).astype(BF)
    fold_row(
        lambda col: grad_ref[CELLS * col : CELLS * (col + 1)],
        first_back_ref, pad_ref, dx_all_ref, down_ref, up_ref, back_local_ref,
    )
    give = one_hot((LINE, 96), 0, index_row_ref[:, LOCAL])
    dx_all_ref[...] += dot(give, back_local_ref[...])
    dx_ref[...] = dx_all_ref[pl.ds(own, CELLS)]
    three = grad_three_ref[...].astype(F32).T
    repeated = jnp.concatenate([three[:FIELDS]] * 9 + [jnp.zeros((HID - 9 * FIELDS, LINE), F32)], 0).astype(BF)
    slots = lax.broadcasted_iota(jnp.int32, (HID, width), 0) >> 4
    for a in range(3):
        term = dot(repeated, gather_rows(filled_ref, a))
        flat_ref[:, width * a : width * (a + 1)] = jnp.where(
            slots == slot_ref[:, width * a : width * (a + 1)], term, 0.0
        ).astype(BF)
    turned = grad_ref[...].astype(F32).T.astype(BF)
    zero_width = filled_zero_ref.shape[3]
    for a in range(3):
        flat_zero_ref[:, zero_width * a : zero_width * (a + 1)] = dot(
            turned, gather_rows(filled_zero_ref, a)
        ).astype(BF)
    along = lax.broadcasted_iota(jnp.int32, (16 * CHUNK, 1152), 1)
    low = pick_out_ref[...]
    pick_out = ((along >= low) & (along < low + 9)).astype(F32).astype(BF)
    for half in range(2):
        rows = slice(16 * CHUNK * half, 16 * CHUNK * (half + 1))
        pick_first = one_hot((16 * CHUNK, 1152), 1, pick_first_ref[rows])
        buffer_ref[rows] = (
            mid_part_ref[rows]
            + dot_nt(pick_out, flat_ref[:, 1152 * half : 1152 * (half + 1)])
            + dot_nt(pick_first, flat_zero_ref[...])
        ).astype(BF)


def finish_kernel(dx_ref, next_ref, prev_ref, index_row_ref, base_ref, out_ref):
    base = base_ref[0]
    rows = lax.broadcasted_iota(jnp.int32, (CELLS, 80), 0) + base
    give_up = (rows == index_row_ref[:, UP]).astype(F32).astype(BF)
    give_down = (rows == index_row_ref[:, DOWN]).astype(F32).astype(BF)
    total = dx_ref[...] + dot(give_up, next_ref[...]) + dot(give_down, prev_ref[...])
    out_ref[...] = total.T[: FIELDS + COUPLED]


VMEM = pl.BlockSpec(memory_space=pltpu.VMEM)
SMEM = pl.BlockSpec(memory_space=pltpu.SMEM)


def call(body, out, args, scratch=(), scalars=(), name=None, flops=0):
    specs = [SMEM if position in scalars else VMEM for position in range(len(args))]
    size = sum(int(np.prod(item.shape)) * item.dtype.itemsize for item in list(args) + list(out))
    return pl.pallas_call(
        body,
        out_shape=[jax.ShapeDtypeStruct(item.shape, item.dtype) for item in out],
        in_specs=specs,
        out_specs=[VMEM] * len(out),
        scratch_shapes=list(scratch),
        compiler_params=pltpu.CompilerParams(vmem_limit_bytes=60 * 1024 * 1024),
        cost_estimate=pl.CostEstimate(flops=flops, bytes_accessed=size, transcendentals=0),
        name=name,
    )(*args)


def sds(shape, kind):
    return jax.ShapeDtypeStruct(shape, kind)


def row_shift(value, step):
    pairs = [(face, (face + ROW * step) % TILES) for face in range(TILES)]
    return lax.ppermute(value, FACE, pairs)


def body(
    state, cotangent, land_sea, turn_table, first_kernel, mid_kernel, out_kernel, first_gates, mid_gates, out_gates
):
    comp = lax.axis_index("comp")
    row = lax.axis_index(ROW_AXES)
    col = lax.axis_index(("xh", "core"))
    tile = row * ROW + col
    own_state = state[0]
    sea = land_sea.astype(F32)
    weight = jnp.where(comp == 1, sea, jnp.ones_like(sea))
    cot = cotangent[0].astype(F32)
    grad_three = (weight * cot).astype(BF)

    packed = jnp.concatenate([own_state, grad_three], 0)
    line = lax.all_to_all(jnp.broadcast_to(packed[None], (8, 32, CELLS)), LINE_AXES, 0, 0)
    line = line.reshape(2, ROW, 32, CELLS)
    own = jnp.where(comp == 0, line[0], line[1])
    other = jnp.where(comp == 0, line[1, :, :COUPLED], line[0, :, :COUPLED])

    index = strip_index(turn_table, row)
    index_col, index_row = index.reshape(256, 1), index.reshape(1, 256)
    field, grad_cells, strips_zero = call(
        start_kernel,
        [sds((LINE, PADC), BF), sds((LINE, PADC), BF), sds((256, PADC), BF)],
        [own, other, index_col], name="start",
    )
    prev_zero = row_shift(strips_zero[UP], 1)
    next_zero = row_shift(strips_zero[DOWN], -1)

    def gated(gates, kernel, name):
        return call(gate_kernel, [sds(kernel.shape, BF)], [gates, kernel], name=name)[0]

    gated_first = gated(first_gates[0], first_kernel[0], "gate_first")
    gated_mid = gated(mid_gates[0], mid_kernel[0], "gate_mid")
    gated_out = gated(out_gates[0], out_kernel[0], "gate_out")
    pad_in = PADC - FIELDS - COUPLED
    first_w = jnp.pad(gated_first.reshape(3, 3, FIELDS + COUPLED, HID), ((0, 0), (0, 0), (0, pad_in), (0, 0)))
    first_w = first_w.reshape(3, 3 * PADC, HID)
    first_back = first_w.transpose(0, 2, 1).reshape(3 * HID, 3 * PADC)
    mid_w = gated_mid.reshape(3, 3 * HID, HID)
    mid_back = mid_w.transpose(0, 2, 1).reshape(3 * HID, 3 * HID)
    out_w = jnp.pad(gated_out, ((0, 0), (0, PADC - FIELDS))).reshape(3, 3 * HID, PADC)
    out_back = out_w.transpose(0, 2, 1).reshape(3 * PADC, 3 * HID)

    exchange = [sds((160, HID), BF), sds((160, HID), BF)]
    filled_zero, act_one, hid_one, local_one, up_one, down_one, inner_two = call(
        first_kernel_body,
        [sds((ROW, TS + 2, TS, 3 * PADC), BF), sds((LINE, HID), F32), sds((LINE, HID), BF), sds((96, HID), BF)]
        + exchange + [sds((LINE, HID), F32)],
        [field, strips_zero[LOCAL], prev_zero, next_zero, grad_cells, first_w, out_back, index_col, index_row],
        scratch=[pltpu.VMEM((TS + 2, TS, 3 * PADC), BF), pltpu.VMEM((96, HID), BF)],
        name="layer_one",
    )
    prev_one = row_shift(up_one, 1)
    next_one = row_shift(down_one, -1)

    filled_one, grad_two, hid_two, local_two, up_two, down_two, inner_one = call(
        mid_kernel_body,
        [sds((ROW, TS + 2, TS, 3 * HID), BF), sds((LINE, HID), BF), sds((LINE, HID), BF), sds((96, HID), BF)]
        + exchange + [sds((LINE, HID), F32)],
        [hid_one, local_one, prev_one, next_one, inner_two, mid_w, mid_back, index_col, index_row],
        scratch=[pltpu.VMEM((TS + 2, TS, 3 * HID), BF), pltpu.VMEM((96, HID), BF)],
        name="layer_two",
    )
    prev_two = row_shift(up_two, 1)
    next_two = row_shift(down_two, -1)

    place = jnp.arange(16 * CHUNK, dtype=jnp.int32)
    block, inside = place // CHUNK, place % CHUNK
    begin = 72 * block + 18 * col
    pick_mid = jnp.where(inside < 18, begin + inside, -1).reshape(-1, 1)
    pick_out = jnp.where((inside >= 18) & (inside < 20), begin + 9 * (inside - 18), -100).reshape(-1, 1)
    place = jnp.arange(32 * CHUNK, dtype=jnp.int32)
    block, inside = place // CHUNK, place % CHUNK
    wanted = 8 * block + 2 * col + inside - 20
    real = (inside >= 20) & (inside < 22) & (wanted < 9 * (FIELDS + COUPLED))
    depth = FIELDS + COUPLED
    pick_first = jnp.where(real, (wanted // depth) * PADC + wanted % depth, -1).reshape(-1, 1)
    kernel_row = jnp.arange(9 * HID, dtype=jnp.int32)
    slot = ((kernel_row % 72 - 18 * col + 72) % 9).reshape(1, -1)

    mid_part = call(
        mid_term_body,
        [sds((32 * CHUNK, HID), F32)],
        [filled_one, grad_two, pick_mid],
        scratch=[pltpu.VMEM((HID, 9 * HID), BF)],
        name="mid_term", flops=2 * 10**9,
    )[0]

    result, buffer, dx_own, up_three, down_three = call(
        last_kernel_body,
        [sds((FIELDS, CELLS), F32), sds((32 * CHUNK, HID), BF), sds((CELLS, PADC), F32), sds((80, PADC), BF),
         sds((80, PADC), BF)],
        [col.reshape(1), hid_two, local_two, prev_two, next_two, inner_one, act_one, filled_zero, grad_cells,
         out_w, first_back, index_row, mid_part, pick_out, pick_first, slot],
        scratch=[
            pltpu.VMEM((ROW, TS + 2, TS, 3 * HID), BF), pltpu.VMEM((TS + 2, TS, 3 * HID), BF),
            pltpu.VMEM((LINE, HID), BF), pltpu.VMEM((LINE, PADC), F32), pltpu.VMEM((96, PADC), BF),
            pltpu.VMEM((HID, 9 * HID), BF), pltpu.VMEM((HID, 9 * PADC), BF),
        ],
        scalars=(0,), name="layer_three",
    )
    prev_three = row_shift(up_three, 1)
    next_three = row_shift(down_three, -1)
    estimate = (own_state.astype(F32) + weight * result).astype(BF)

    spread = lax.all_to_all(buffer.reshape(ROWS, CHUNK, HID), ROW_AXES, 0, 0)
    summed = jnp.sum(spread.astype(F32), 0)

    dx = call(
        finish_kernel, [sds((FIELDS + COUPLED, CELLS), F32)],
        [dx_own, next_three, prev_three, index_row, (col * CELLS).reshape(1)], scalars=(4,), name="finish",
    )[0]
    returned = lax.ppermute(dx[FIELDS:], "comp", [(0, 1), (1, 0)])
    adjoint = cot + dx[:FIELDS] + jnp.pad(returned, ((0, FIELDS - COUPLED), (0, 0)))

    shared = jnp.broadcast_to(summed[20:22].astype(BF)[None], (TILES, 2, HID))
    opening = lax.all_to_all(shared, FACE, 0, 0).reshape(2 * TILES, HID)[: 9 * depth].astype(F32)

    def keep_mask(gates):
        groups = gates.shape[1]
        repeat = (np.arange(4 * groups)[None] // 4 == np.arange(groups)[:, None]).astype(np.float32)
        wide = dot(gates.astype(BF), jnp.asarray(repeat, BF))
        return keep_of(wide, jnp.arange(4 * groups, dtype=jnp.int32)[None] & 3)

    opening = jnp.where(keep_mask(first_gates[0]), opening, 0.0)
    rows_mid = lax.dynamic_slice(mid_gates[0], (18 * tile, 0), (18, HID // 4))
    central = jnp.where(keep_mask(rows_mid), summed[:18], 0.0).reshape(1, 18 * HID)
    rows_out = lax.dynamic_slice(out_gates[0], (18 * tile, 0), (18, FIELDS // 4))
    closing = summed[18:20, : 9 * FIELDS].reshape(18, FIELDS)
    closing = jnp.where(keep_mask(rows_out), closing, 0.0).reshape(1, 18 * FIELDS)
    return estimate[None], adjoint[None], opening[None], central, closing


def solution(mesh):
    fine = Mesh(mesh.devices.reshape(2, 4, 8, 2, 2), ("comp",) + FACE)
    whole = P("comp", None, None)
    in_specs = (P("comp", None, FACE), P("comp", None, FACE), P(FACE), P()) + (whole,) * 6
    out_specs = (P("comp", None, FACE), P("comp", None, FACE), whole, P("comp", FACE), P("comp", FACE))
    return jax.shard_map(body, mesh=fine, in_specs=in_specs, out_specs=out_specs, check_vma=False)
```

time: 1460 us -> 145 us (0.10)
  waiting for transfers between devices: 1250 us -> 20.4 us
  local copies, waits for them, and re-layouts: 78.6 us -> 22.2 us
  Pallas kernels: 0 us -> 41.1 us
  between operations: 27.1 us -> 0.84 us
  starting transfers between devices: 67.3 us -> 45.8 us
    psum x1 -> x0, waiting for transfers between devices: 1240 us -> none  [body(): leading_gate_total = lax.psum(first_local, 'face')]
    ppermute x26 -> x9, starting transfers between devices: 67.3 us -> 22.7 us  [the longest x8 21.6 us: row_shift(): return lax.ppermute(value, FACE, pairs)]
    pallas_call x0 -> x9, Pallas kernels: none -> 41.1 us  [call(): pl.pallas_call(body, out_shape=[jax.ShapeDtypeStruct(item.shape, item.dty...]
    all_to_all x0 -> x3, starting transfers between devices: none -> 23.1 us  [the longest x1 12.5 us: body(): lax.all_to_all(shared, FACE, 0, 0).reshape(2 * TILES, HID)[:9 * depth]]
    scatter-add x33 -> x0, local copies, waits for them, and re-layouts: 19 us -> none  [the longest x27 18.4 us: fold(): prognosis_outcome = prognosis_outcome.at[:, vertical_place:vertical_place...]
    scatter x12 -> x0, local copies, waits for them, and re-layouts: 17 us -> none  [the longest x3 7.85 us: with_halo(): padded = padded.at[:, 0, 1:-1].set(south)]
    eq x22 -> x0, local copies, waits for them, and re-layouts: 16.4 us -> none  [gate_keep(): keep = (low[..., None] == lanes) | (high[..., None] == lanes)]
  transfers between devices with their start and end apart: 27 -> 12, of which waited for: 3 -> 5; matrix products, arithmetic and copies ran while one was open for 5% -> 18% of each run, Pallas kernels for 0% -> 11%
where the time goes in v1:
time: 145 us; the launch traced here: 144 us
  starting transfers between devices  45.8 us (32%)
  Pallas kernels  41.1 us (28%)
  local copies, waits for them, and re-layouts  22.2 us (15%)
  waiting for transfers between devices  20.4 us (14%)
  other arithmetic  12.3 us (8%)
    pallas_call x9, Pallas kernels, call(): pl.pallas_call(body, out_shape=[jax.ShapeDtypeStruct(item.shape, item.dty...  41.1 us
    ppermute x8, starting transfers between devices, row_shift(): return lax.ppermute(value, FACE, pairs)  21.6 us
    all_to_all x1, starting transfers between devices, body(): lax.all_to_all(shared, FACE, 0, 0).reshape(2 * TILES, HID)[:9 * depth]  12.5 us
    all_to_all x1, waiting for transfers between devices, body(): lax.all_to_all(shared, FACE, 0, 0).reshape(2 * TILES, HID)[:9 * depth]  11.2 us
    ppermute x8, waiting for transfers between devices, row_shift(): return lax.ppermute(value, FACE, pairs)  9.05 us
    unnamed x43, local copies, waits for them, and re-layouts  7.84 us
    all_to_all x1, starting transfers between devices, body(): lax.all_to_all(jnp.broadcast_to(packed[None], (8, 32, CELLS)), LINE_AXES,...  6.47 us
    all_to_all x1, starting transfers between devices, body(): spread = lax.all_to_all(buffer.reshape(ROWS, CHUNK, HID), ROW_AXES, 0, 0)  4.09 us
  transfers between devices with their start and end apart: 12, of which 5 were waited for; matrix products, arithmetic and copies ran while one was open for 18% of the time, Pallas kernels for 11%

profile of v1, /device:TPU:1, one launch (start us, length us, event | category | flops | bytes accessed | tf_op | source)
XLA Modules:
  0.0 144.0 jit_solution(13642030897146015017)
XLA Ops:
  0.7 0.7 convert_select_fusion
  1.4 0.7 fusion.33
  2.1 0.7 pad_maximum_fusion
  3.4 6.5 %all-to-all-start = ((bf16[8,32,256]{2,1,0:T(8,128)(2,1)}), bf16[8,32,256]{2,1,0:T(8,128)(2,1)S(1)}, u32[]{:S(2)}, u32[]{:S(2)}) async-start(bf16[8,32,256]{2,1,0:T(8,128)(2,1)} %broadcast_in_dim.116), calls=%async_computation | async-start | bytes 262144 | tf_op jit(solution)/shard_map/all_to_all | solution.py:391
  9.9 0.8 fusion.56
  10.7 0.8 fusion.49
  11.6 0.8 multiply_reduce_fusion
  12.4 0.8 select_reduce_fusion
  13.3 0.8 reshape_reshape.8.index_ref.index_col_ref
  14.7 1.4 fusion.7.pick_first_ref
  17.4 2.1 %start.1 = (bf16[1024,128]{1,0:T(8,128)(2,1)}, bf16[1024,128]{1,0:T(8,128)(2,1)}, bf16[256,128]{1,0:T(8,128)(2,1)}) custom-call(bf16[4,32,256]{2,1,0:T(8,128)(2,1)} %slice_select_fusion.own_ref, bf16[4,8,256]{2,1,0:T(8,128)(2,1)} %fusion.41.other_ref, s32[256,1]{1,0:T(8,128)} %reshape_reshape.8.index_ref.index_col_ref), custom_call_target="tpu_custom_call" | custom-call | bytes 672768 | tf_op jit(solution)/shard_map/start/pallas_call | solution.py:356
  19.5 0.7 fusion.55
  20.3 1.0 collective-permute-start
  21.2 6.4 %collective-permute-start.1 = (bf16[80,128]{1,0:T(8,128)(2,1)S(1)}, bf16[80,128]{1,0:T(8,128)(2,1)S(1)}, u32[]{:S(2)}, u32[]{:S(2)}) collective-permute-start(bf16[80,128]{1,0:T(8,128)(2,1)S(1)} %get-tuple-element.49), channel_id=1, source_target_pairs={{0,124},{1,125},{2,126},{3,127},{4,0},{5,1},{6,2},{7,3},{8,4},{9,5... | collective-permute-start | bytes 61448 | tf_op jit(solution)/shard_map/ppermute | solution.py:374
  27.6 0.8 add_select_fusion.7.pick_ref
  29.0 0.8 copy.43
  29.8 1.4 copy.44
  31.2 1.1 copy.45
  32.3 1.8 %gate_first.1 = bf16[216,256]{1,0:T(8,128)(2,1)} custom-call(s32[216,64]{1,0:T(8,128)} %bitcast.77, bf16[216,256]{1,0:T(8,128)(2,1)} %bitcast.80), custom_call_target="tpu_custom_call" | custom-call | bytes 276480 | tf_op jit(solution)/shard_map/gate_first/pallas_call | solution.py:356
  34.1 0.9 pad.12
  35.1 3.2 %gate_out.1 = bf16[2304,16]{1,0:T(8,128)(2,1)} custom-call(s32[2304,4]{1,0:T(8,128)} %bitcast.71, bf16[2304,16]{1,0:T(8,128)(2,1)} %bitcast.74), custom_call_target="tpu_custom_call" | custom-call | bytes 184320 | tf_op jit(solution)/shard_map/gate_out/pallas_call | solution.py:356
  38.3 1.2 pad.13
  39.5 1.1 copy.46
  40.6 1.4 copy.48
  42.0 3.9 %gate_mid.1 = bf16[2304,256]{1,0:T(8,128)(2,1)} custom-call(s32[2304,64]{1,0:T(8,128)} %bitcast.70, bf16[2304,256]{1,0:T(8,128)(2,1)} %bitcast.75), custom_call_target="tpu_custom_call" | custom-call | bytes 2949120 | tf_op jit(solution)/shard_map/gate_mid/pallas_call | solution.py:356
  45.9 2.4 %copy.49 = bf16[3,256,768]{2,1,0:T(8,128)(2,1)} copy(bf16[3,256,768]{1,2,0:T(8,128)(2,1)} %bitcast.63) | data formatting | bytes 2359296 | tf_op jit(solution)/shard_map/transpose | solution.py:417
  48.3 1.1 copy.51
  49.4 1.3 slice.55.local_ref
  51.3 5.8 %layer_one.1 = (bf16[4,18,16,384]{3,2,1,0:T(8,128)(2,1)}, f32[1024,256]{1,0:T(8,128)}, bf16[1024,256]{1,0:T(8,128)(2,1)}, bf16[96,256]{1,0:T(8,128)(2,1)}, bf16[...) custom-call(bf16[1024,128]{1,0:T(8,128)(2,1)} %get-tuple-element.27.field_ref, ...), custom_call_target="tpu_custom_call" | custom-call | bytes 5490688 | tf_op jit(solution)/shard_map/layer_one/pallas_call | solution.py:356
  57.2 4.8 %collective-permute-start.3 = (bf16[160,256]{1,0:T(8,128)(2,1)}, bf16[160,256]{1,0:T(8,128)(2,1)S(1)}, u32[]{:S(2)}, u32[]{:S(2)}) collective-permute-start(bf16[160,256]{1,0:T(8,128)(2,1)} %get-tuple-element.33), channel_id=1, source_target_pairs={{0,124},{1,125},{2,126},{3,127},{4,0},{5,1},{6,2},{7,3},{8,4},{9,5... | collective-permute-start | bytes 245768 | tf_op jit(solution)/shard_map/ppermute | solution.py:374
  61.9 0.8 add_select_fusion.6.pick_out_ref
  62.7 1.6 %collective-permute-done.2.prev_ref = bf16[160,256]{1,0:T(8,128)(2,1)S(1)} collective-permute-done((bf16[160,256]{1,0:T(8,128)(2,1)}, bf16[160,256]{1,0:T(8,128)(2,1)S(1)}, u32[]{:S(2)}, u32[]{:S(2)}) %collective-permute-start.2) | collective-permute-done | bytes 81952 | tf_op jit(solution)/shard_map/ppermute | solution.py:374
  65.1 8.1 %layer_two.1 = (bf16[4,18,16,768]{3,2,1,0:T(8,128)(2,1)}, bf16[1024,256]{1,0:T(8,128)(2,1)}, bf16[1024,256]{1,0:T(8,128)(2,1)}, bf16[96,256]{1,0:T(8,128)(2,1)},...) custom-call(bf16[1024,256]{1,0:T(8,128)(2,1)} %get-tuple-element.30.hid_ref, ...), custom_call_target="tpu_custom_call" | custom-call | bytes 8226816 | tf_op jit(solution)/shard_map/layer_two/pallas_call | solution.py:356
  73.1 4.8 %collective-permute-start.5 = (bf16[160,256]{1,0:T(8,128)(2,1)}, bf16[160,256]{1,0:T(8,128)(2,1)S(1)}, u32[]{:S(2)}, u32[]{:S(2)}) collective-permute-start(bf16[160,256]{1,0:T(8,128)(2,1)} %get-tuple-element.38), channel_id=1, source_target_pairs={{0,124},{1,125},{2,126},{3,127},{4,0},{5,1},{6,2},{7,3},{8,4},{9,5... | collective-permute-start | bytes 245768 | tf_op jit(solution)/shard_map/ppermute | solution.py:374
  77.9 4.5 %mid_term.1.mid_part_ref = f32[768,256]{1,0:T(8,128)} custom-call(bf16[4,18,16,768]{3,2,1,0:T(8,128)(2,1)} %get-tuple-element.42.filled_ref, bf16[1024,256]{1,0:T(8,128)(2,1)} %get-tuple-element.43.grad_ref, s32[384,1]{1,0:T(8,128)} %add_select_fusion.7.pick_ref), custom_call_target="tpu_custom_call" | custom-call | flops 2000000000 | bytes 3081728 | tf_op jit(solution)/shard_map/mid_term/pallas_call | solution.py:356
  83.1 9.9 %layer_three.1 = (f32[16,256]{1,0:T(8,128)}, bf16[768,256]{1,0:T(8,128)(2,1)}, f32[256,128]{1,0:T(8,128)}, bf16[80,128]{1,0:T(8,128)(2,1)}, bf16[80,128]{1,0:T(8,128)(2,1)}) custom-call(s32[1]{0:T(128)} %bitcast.1.col_ref, bf16[1024,256]{1,0:T(8,128)(2,1)} %get-tuple-element.35.hid_two_ref, bf16[96,256]{1,0:T(8,128)(2,1)} %get-tuple-element.36.local_ref, ...), custom_call_target="tpu_custom_call" | custom-call | bytes 6543876 | tf_op jit(solution)/shard_map/layer_three/pallas_call | solution.py:356
  93.0 4.1 %all-to-all-start.1 = ((bf16[32,24,256]{2,1,0:T(8,128)(2,1)}), bf16[32,24,256]{2,1,0:T(8,128)(2,1)S(1)}, u32[]{:S(2)}, u32[]{:S(2)}) async-start(bf16[32,24,256]{2,1,0:T(8,128)(2,1)} %bitcast.79), calls=%async_computation.1 | async-start | bytes 786432 | tf_op jit(solution)/shard_map/all_to_all | solution.py:483
  97.1 4.7 %collective-permute-start.6 = (bf16[80,128]{1,0:T(8,128)(2,1)}, bf16[80,128]{1,0:T(8,128)(2,1)S(1)}, u32[]{:S(2)}, u32[]{:S(2)}) collective-permute-start(bf16[80,128]{1,0:T(8,128)(2,1)} %get-tuple-element.46), channel_id=1, source_target_pairs={{0,124},{1,125},{2,126},{3,127},{4,0},{5,1},{6,2},{7,3},{8,4},{9,5... | collective-permute-start | bytes 61448 | tf_op jit(solution)/shard_map/ppermute | solution.py:374
  101.8 3.5 %collective-permute-done.6.next_ref = bf16[80,128]{1,0:T(8,128)(2,1)S(1)} collective-permute-done((bf16[80,128]{1,0:T(8,128)(2,1)}, bf16[80,128]{1,0:T(8,128)(2,1)S(1)}, u32[]{:S(2)}, u32[]{:S(2)}) %collective-permute-start.6) | collective-permute-done | bytes 20512 | tf_op jit(solution)/shard_map/ppermute | solution.py:374
  105.4 3.9 %collective-permute-done.7.prev_ref = bf16[80,128]{1,0:T(8,128)(2,1)S(1)} collective-permute-done((bf16[80,128]{1,0:T(8,128)(2,1)}, bf16[80,128]{1,0:T(8,128)(2,1)S(1)}, u32[]{:S(2)}, u32[]{:S(2)}) %collective-permute-start.7) | collective-permute-done | bytes 20512 | tf_op jit(solution)/shard_map/ppermute | solution.py:374
  109.8 1.8 %finish.1 = f32[24,256]{1,0:T(8,128)} custom-call(f32[256,128]{1,0:T(8,128)} %get-tuple-element.45.dx_ref, bf16[80,128]{1,0:T(8,128)(2,1)} %copy-done.15, bf16[80,128]{1,0:T(8,128)(2,1)} %copy-done.16, s32[1,256]{1,0:T(1,128)} %reshape_reshape.7.index_row_ref, s32[1]{0:T(128)} %bitcast.23.base_ref), custom_call_target="tpu_custom_call" | custom-call | bytes 197636 | tf_op jit(solution)/shard_map/finish/pallas_call | solution.py:356
  112.4 1.1 collective-permute-start.8
  113.4 1.3 fusion.45
  114.9 1.3 fusion.35
  116.3 0.7 broadcast_in_dim.126
  117.0 12.5 %all-to-all-start.2 = ((bf16[128,2,256]{2,1,0:T(2,128)(2,1)}), bf16[128,2,256]{2,1,0:T(2,128)(2,1)S(1)}, u32[]{:S(2)}, u32[]{:S(2)}) async-start(bf16[128,2,256]{2,1,0:T(2,128)(2,1)} %broadcast_in_dim.126), calls=%async_computation.2 | async-start | bytes 262144 | tf_op jit(solution)/shard_map/all_to_all | solution.py:494
  131.6 11.2 %all-to-all-done.2 = bf16[128,2,256]{2,1,0:T(2,128)(2,1)S(1)} async-done(((bf16[128,2,256]{2,1,0:T(2,128)(2,1)}), bf16[128,2,256]{2,1,0:T(2,128)(2,1)S(1)}, u32[]{:S(2)}, u32[]{:S(2)}) %all-to-all-start.2) | async-done | bytes 131104 | tf_op jit(solution)/shard_map/all_to_all | solution.py:494
  143.0 1.0 select_bitcast_fusion
  (71 shorter events, 9.0 us)
Async XLA Ops:
  0.6 28.4 %copy-start.9 = (s32[1,216,64]{1,2,0:T(8,128)S(1)}, s32[1,216,64]{1,2,0:T(8,128)}, u32[]{:S(2)}) copy-start(s32[1,216,64]{1,2,0:T(8,128)} %param.22) | copy-start | bytes 165892
  0.6 29.1 %copy-start.10 = (s32[1,2304,4]{1,2,0:T(4,128)S(1)}, s32[1,2304,4]{1,2,0:T(4,128)}, u32[]{:S(2)}) copy-start(s32[1,2304,4]{1,2,0:T(4,128)} %param.24) | copy-start | bytes 110596
  3.4 12.7 %all-to-all-start = ((bf16[8,32,256]{2,1,0:T(8,128)(2,1)}), bf16[8,32,256]{2,1,0:T(8,128)(2,1)S(1)}, u32[]{:S(2)}, u32[]{:S(2)}) async-start(bf16[8,32,256]{2,1,0:T(8,128)(2,1)} %broadcast_in_dim.116), calls=%async_computation | async-start | bytes 262144 | tf_op jit(solution)/shard_map/all_to_all | solution.py:391
  14.7 16.5 %copy-start.8 = (bf16[1,2304,16]{1,2,0:T(8,128)(2,1)S(1)}, bf16[1,2304,16]{1,2,0:T(8,128)(2,1)}, u32[]{:S(2)}) copy-start(bf16[1,2304,16]{1,2,0:T(8,128)(2,1)} %param.21) | copy-start | bytes 221188
  20.3 30.4 %collective-permute-start = (bf16[80,128]{1,0:T(8,128)(2,1)S(1)}, bf16[80,128]{1,0:T(8,128)(2,1)S(1)}, u32[]{:S(2)}, u32[]{:S(2)}) collective-permute-start(bf16[80,128]{1,0:T(8,128)(2,1)S(1)} %get-tuple-element.50), channel_id=1, source_target_pairs={{0,4},{1,5},{2,6},{3,7},{4,8},{5,9},{6,10},{7,11},{8,12},{9,13},{1... | collective-permute-start | bytes 61448 | tf_op jit(solution)/shard_map/ppermute | solution.py:374
  21.2 29.5 %collective-permute-start.1 = (bf16[80,128]{1,0:T(8,128)(2,1)S(1)}, bf16[80,128]{1,0:T(8,128)(2,1)S(1)}, u32[]{:S(2)}, u32[]{:S(2)}) collective-permute-start(bf16[80,128]{1,0:T(8,128)(2,1)S(1)} %get-tuple-element.49), channel_id=1, source_target_pairs={{0,124},{1,125},{2,126},{3,127},{4,0},{5,1},{6,2},{7,3},{8,4},{9,5... | collective-permute-start | bytes 61448 | tf_op jit(solution)/shard_map/ppermute | solution.py:374
  35.1 13.2 %copy-start.1 = (bf16[3,3,128,256]{3,2,1,0:T(8,128)(2,1)}, bf16[3,3,128,256]{3,2,1,0:T(8,128)(2,1)S(1)}, u32[]{:S(2)}) copy-start(bf16[3,3,128,256]{3,2,1,0:T(8,128)(2,1)S(1)} %pad.12) | copy-start | bytes 1769476
  38.2 2.4 %copy-start.2 = (s32[1,2304,64]{1,2,0:T(8,128)S(1)}, s32[1,2304,64]{1,2,0:T(8,128)}, u32[]{:S(2)}) copy-start(s32[1,2304,64]{1,2,0:T(8,128)} %param.23) | copy-start | bytes 1769476
  39.5 2.5 %copy-start = (bf16[2304,128]{1,0:T(8,128)(2,1)}, bf16[2304,128]{1,0:T(8,128)(2,1)S(1)}, u32[]{:S(2)}) copy-start(bf16[2304,128]{1,0:T(8,128)(2,1)S(1)} %pad.13) | copy-start | bytes 1769476
  50.7 0.6 copy-start.13
  50.7 0.6 copy-start.14
  57.1 7.2 %collective-permute-start.2 = (bf16[160,256]{1,0:T(8,128)(2,1)}, bf16[160,256]{1,0:T(8,128)(2,1)S(1)}, u32[]{:S(2)}, u32[]{:S(2)}) collective-permute-start(bf16[160,256]{1,0:T(8,128)(2,1)} %get-tuple-element.32), channel_id=1, source_target_pairs={{0,4},{1,5},{2,6},{3,7},{4,8},{5,9},{6,10},{7,11},{8,12},{9,13},{1... | collective-permute-start | bytes 245768 | tf_op jit(solution)/shard_map/ppermute | solution.py:374
  57.2 7.2 %collective-permute-start.3 = (bf16[160,256]{1,0:T(8,128)(2,1)}, bf16[160,256]{1,0:T(8,128)(2,1)S(1)}, u32[]{:S(2)}, u32[]{:S(2)}) collective-permute-start(bf16[160,256]{1,0:T(8,128)(2,1)} %get-tuple-element.33), channel_id=1, source_target_pairs={{0,124},{1,125},{2,126},{3,127},{4,0},{5,1},{6,2},{7,3},{8,4},{9,5... | collective-permute-start | bytes 245768 | tf_op jit(solution)/shard_map/ppermute | solution.py:374
  64.4 0.6 copy-start.6
  64.4 0.7 copy-start.7
  73.1 9.3 %collective-permute-start.4 = (bf16[160,256]{1,0:T(8,128)(2,1)}, bf16[160,256]{1,0:T(8,128)(2,1)S(1)}, u32[]{:S(2)}, u32[]{:S(2)}) collective-permute-start(bf16[160,256]{1,0:T(8,128)(2,1)} %get-tuple-element.37), channel_id=1, source_target_pairs={{0,4},{1,5},{2,6},{3,7},{4,8},{5,9},{6,10},{7,11},{8,12},{9,13},{1... | collective-permute-start | bytes 245768 | tf_op jit(solution)/shard_map/ppermute | solution.py:374
  73.1 9.3 %collective-permute-start.5 = (bf16[160,256]{1,0:T(8,128)(2,1)}, bf16[160,256]{1,0:T(8,128)(2,1)S(1)}, u32[]{:S(2)}, u32[]{:S(2)}) collective-permute-start(bf16[160,256]{1,0:T(8,128)(2,1)} %get-tuple-element.38), channel_id=1, source_target_pairs={{0,124},{1,125},{2,126},{3,127},{4,0},{5,1},{6,2},{7,3},{8,4},{9,5... | collective-permute-start | bytes 245768 | tf_op jit(solution)/shard_map/ppermute | solution.py:374
  82.4 0.6 copy-start.4
  82.4 0.7 copy-start.5
  83.1 30.4 %copy-start.12 = (bf16[1,16,256]{2,1,0:T(8,128)(2,1)S(1)}, bf16[1,16,256]{2,1,0:T(8,128)(2,1)}, u32[]{:S(2)}) copy-start(bf16[1,16,256]{2,1,0:T(8,128)(2,1)} %param.15) | copy-start | bytes 24580
  83.1 31.8 %copy-start.11 = (bf16[1,16,256]{2,1,0:T(8,128)(2,1)S(1)}, bf16[1,16,256]{2,1,0:T(8,128)(2,1)}, u32[]{:S(2)}) copy-start(bf16[1,16,256]{2,1,0:T(8,128)(2,1)} %param.16) | copy-start | bytes 24580
  93.0 36.7 %copy-start.18 = (bf16[4,16]{1,0:T(4,128)(2,1)S(1)}, bf16[4,16]{1,0:T(4,128)(2,1)}, u32[]{:S(2)}) copy-start(bf16[4,16]{1,0:T(4,128)(2,1)} %constant.157.clone) | copy-start | bytes 388
  93.0 37.7 %copy-start.17 = (bf16[64,256]{1,0:T(8,128)(2,1)S(1)}, bf16[64,256]{1,0:T(8,128)(2,1)}, u32[]{:S(2)}) copy-start(bf16[64,256]{1,0:T(8,128)(2,1)} %constant.156.clone) | copy-start | bytes 98308
  93.0 23.2 %all-to-all-start.1 = ((bf16[32,24,256]{2,1,0:T(8,128)(2,1)}), bf16[32,24,256]{2,1,0:T(8,128)(2,1)S(1)}, u32[]{:S(2)}, u32[]{:S(2)}) async-start(bf16[32,24,256]{2,1,0:T(8,128)(2,1)} %bitcast.79), calls=%async_computation.1 | async-start | bytes 786432 | tf_op jit(solution)/shard_map/all_to_all | solution.py:483
  97.1 45.9 %copy-start.3 = (s32[1,216,64]{2,1,0:T(8,128)S(1)}, s32[1,216,64]{2,1,0:T(8,128)}, u32[]{:S(2)}) copy-start(s32[1,216,64]{2,1,0:T(8,128)} %copy.43) | copy-start | bytes 165892
  97.1 8.2 %collective-permute-start.6 = (bf16[80,128]{1,0:T(8,128)(2,1)}, bf16[80,128]{1,0:T(8,128)(2,1)S(1)}, u32[]{:S(2)}, u32[]{:S(2)}) collective-permute-start(bf16[80,128]{1,0:T(8,128)(2,1)} %get-tuple-element.46), channel_id=1, source_target_pairs={{0,124},{1,125},{2,126},{3,127},{4,0},{5,1},{6,2},{7,3},{8,4},{9,5... | collective-permute-start | bytes 61448 | tf_op jit(solution)/shard_map/ppermute | solution.py:374
  101.8 7.4 %collective-permute-start.7 = (bf16[80,128]{1,0:T(8,128)(2,1)}, bf16[80,128]{1,0:T(8,128)(2,1)S(1)}, u32[]{:S(2)}, u32[]{:S(2)}) collective-permute-start(bf16[80,128]{1,0:T(8,128)(2,1)} %get-tuple-element.47), channel_id=1, source_target_pairs={{0,4},{1,5},{2,6},{3,7},{4,8},{5,9},{6,10},{7,11},{8,12},{9,13},{1... | collective-permute-start | bytes 61448 | tf_op jit(solution)/shard_map/ppermute | solution.py:374
  105.4 3.9 %copy-start.15 = (bf16[80,128]{1,0:T(8,128)(2,1)}, bf16[80,128]{1,0:T(8,128)(2,1)S(1)}, u32[]{:S(2)}) copy-start(bf16[80,128]{1,0:T(8,128)(2,1)S(1)} %collective-permute-done.6.next_ref) | copy-start | bytes 61444
  109.2 0.6 copy-start.16
  112.4 2.5 %collective-permute-start.8 = (f32[8,256]{1,0:T(8,128)S(1)}, f32[8,256]{1,0:T(8,128)S(1)}, u32[]{:S(2)}, u32[]{:S(2)}) collective-permute-start(f32[8,256]{1,0:T(8,128)S(1)} %slice.69), channel_id=1, source_target_pairs={{0,128},{128,0},{1,129},{129,1},{2,130},{130,2},{3,131},{131,3},{4... | collective-permute-start | bytes 24584 | tf_op jit(solution)/shard_map/ppermute | solution.py:490
  117.0 25.8 %all-to-all-start.2 = ((bf16[128,2,256]{2,1,0:T(2,128)(2,1)}), bf16[128,2,256]{2,1,0:T(2,128)(2,1)S(1)}, u32[]{:S(2)}, u32[]{:S(2)}) async-start(bf16[128,2,256]{2,1,0:T(2,128)(2,1)} %broadcast_in_dim.126), calls=%async_computation.2 | async-start | bytes 262144 | tf_op jit(solution)/shard_map/all_to_all | solution.py:494

commit v2 on v1

v2 whole, which is shorter than its diff:
```python
import jax
import jax.numpy as jnp
import numpy as np
from jax import lax
from jax.experimental import pallas as pl
from jax.experimental.pallas import tpu as pltpu
from jax.sharding import Mesh, PartitionSpec as P


FIELDS = 16
COUPLED = 8
TS = 16
CELLS = TS * TS
ROW = 4
ROWS = 32
TILES = ROW * ROWS
LINE = ROW * CELLS
HID = 256
PADC = 128
CHUNK = 24
SHARE = 16
BF = jnp.bfloat16
F32 = jnp.float32

FACE = ("y", "z", "xh", "core")
ROW_AXES = ("y", "z")
LINE_AXES = ("comp", "xh", "core")

EDGE_MAP = (
    ((0, False), (2, True), (1, True), (3, False)),
    ((1, False), (3, True), (0, True), (2, False)),
    ((2, False), (1, False), (3, True), (0, True)),
    ((3, False), (0, False), (2, True), (1, True)),
)

STRIPS = (
    [(col, 2, 8 + col) for col in range(4)]
    + [(3, 0, 8)]
    + [(col, 3, col) for col in range(4)]
    + [(0, 1, 3)]
    + [(col - 1, 0, 4 + col) for col in (1, 2, 3)]
    + [(col + 1, 1, 4 + col) for col in (0, 1, 2)]
)


def edge_line(slot, flip):
    first, step = ((TS - 1, TS), (0, TS), ((TS - 1) * TS, 1), (0, 1))[slot]
    if flip:
        first, step = first + (TS - 1) * step, -step
    return first, step


def dot(left, right):
    return jnp.dot(left, right, preferred_element_type=F32)


def dot_nt(left, right):
    return lax.dot_general(left, right, (((1,), (1,)), ((), ())), preferred_element_type=F32)


def dot_tn(left, right):
    return lax.dot_general(left, right, (((0,), (0,)), ((), ())), preferred_element_type=F32)


def dot_exact(left, right):
    high = right.astype(BF)
    rest = right - high.astype(F32)
    mid = rest.astype(BF)
    low = (rest - mid.astype(F32)).astype(BF)
    return dot(left, high) + (dot(left, mid) + dot(left, low))


def dot_exact_right(left, right):
    high = left.astype(BF)
    rest = left - high.astype(F32)
    mid = rest.astype(BF)
    low = (rest - mid.astype(F32)).astype(BF)
    return dot(high, right) + (dot(mid, right) + dot(low, right))


def fetch(sources, buffers, sems):
    copies = [
        pltpu.make_async_copy(source, buffer, sems.at[place])
        for place, (source, buffer) in enumerate(zip(sources, buffers))
    ]
    for copy in copies:
        copy.start()
    return copies


def one_hot(shape, axis, index):
    return (lax.broadcasted_iota(jnp.int32, shape, axis) == index).astype(F32).astype(BF)


def edge_spread(column):
    rows = lax.broadcasted_iota(jnp.int32, (CELLS, TS), 0)
    cols = lax.broadcasted_iota(jnp.int32, (CELLS, TS), 1)
    return (rows == cols * TS + column).astype(F32).astype(BF)


def edge_take(column):
    rows = lax.broadcasted_iota(jnp.int32, (TS, CELLS), 0)
    cols = lax.broadcasted_iota(jnp.int32, (TS, CELLS), 1)
    return (cols == rows * TS + column).astype(F32).astype(BF)


def shift_cells(value, step, axis):
    along = lax.broadcasted_iota(jnp.int32, value.shape, axis)
    moved = pltpu.roll(value, step % TS, axis)
    edge = 0 if step == 1 else TS - 1
    return jnp.where(along == edge, 0.0, moved)


def fill(out_ref, tiles, local, from_prev, from_next):
    depth = tiles.shape[1]
    spread_west, spread_east = edge_spread(0), edge_spread(TS - 1)
    for col in range(ROW):
        south = from_prev[TS * col : TS * (col + 1)]
        north = from_next[TS * col : TS * (col + 1)]
        west = from_prev[4 * TS : 5 * TS] if col == 0 else local[TS * (col - 1) : TS * col]
        east = from_next[4 * TS : 5 * TS] if col == 3 else local[TS * (3 + col) : TS * (4 + col)]
        own = tiles[CELLS * col : CELLS * (col + 1)]
        wide = own.astype(F32).reshape(TS, TS, depth)
        left = shift_cells(wide, 1, 1) + dot(spread_west, west).reshape(TS, TS, depth)
        right = shift_cells(wide, -1, 1) + dot(spread_east, east).reshape(TS, TS, depth)
        out_ref[col, 1 : TS + 1, :, 0:depth] = left.astype(BF)
        out_ref[col, 1 : TS + 1, :, depth : 2 * depth] = own.reshape(TS, TS, depth)
        out_ref[col, 1 : TS + 1, :, 2 * depth : 3 * depth] = right.astype(BF)
        for line, strip in ((0, south), (TS + 1, north)):
            wide = strip.astype(F32)
            out_ref[col, line, :, 0:depth] = shift_cells(wide, 1, 0).astype(BF)
            out_ref[col, line, :, depth : 2 * depth] = strip
            out_ref[col, line, :, 2 * depth : 3 * depth] = shift_cells(wide, -1, 0).astype(BF)


def conv_tile(filled_ref, weights_ref, col):
    width = filled_ref.shape[3]
    total = None
    for a in range(3):
        piece = dot(filled_ref[col, a : a + TS].reshape(CELLS, width), weights_ref[a])
        total = piece if total is None else total + piece
    return total


def fold_tile(grad, weights_ref, pad_ref):
    deep = grad.shape[1]
    lines = grad.reshape(TS, TS, deep)
    for a in range(3):
        pad_ref[a : a + TS, :, deep * a : deep * (a + 1)] = lines
    total = dot(pad_ref[...].reshape((TS + 2) * TS, 3 * deep), weights_ref[...])
    depth = total.shape[1] // 3
    total = total.reshape(TS + 2, TS, 3 * depth)
    left, mid, right = (total[:, :, depth * b : depth * (b + 1)] for b in range(3))
    merged = mid + shift_cells(left, -1, 1) + shift_cells(right, 1, 1)
    inner = merged[1 : TS + 1].reshape(CELLS, depth)
    south = merged[0].astype(BF)
    north = merged[TS + 1].astype(BF)
    west = dot(edge_take(0), left[1 : TS + 1].reshape(CELLS, depth).astype(BF)).astype(BF)
    east = dot(edge_take(TS - 1), right[1 : TS + 1].reshape(CELLS, depth).astype(BF)).astype(BF)
    return inner, south, north, west, east


def fold_row(grad_of, weights_ref, pad_ref, inner_ref, prev_ref, next_ref, local_ref):
    pad_ref[...] = jnp.zeros_like(pad_ref)
    for col in range(ROW):
        inner, south, north, west, east = fold_tile(grad_of(col), weights_ref, pad_ref)
        inner_ref[CELLS * col : CELLS * (col + 1)] = inner
        prev_ref[TS * col : TS * (col + 1)] = south
        next_ref[TS * col : TS * (col + 1)] = north
        if col == 0:
            prev_ref[4 * TS : 5 * TS] = west
        else:
            local_ref[TS * (col - 1) : TS * col] = west
        if col == 3:
            next_ref[4 * TS : 5 * TS] = east
        else:
            local_ref[TS * (3 + col) : TS * (4 + col)] = east


def sigmoid(values):
    return 1.0 / (1.0 + jnp.exp(-values))


def slope(values):
    sig = sigmoid(values)
    return sig * (1.0 + values * (1.0 - sig))


UP = slice(0, 80)
DOWN = slice(80, 160)
LOCAL = slice(160, 256)


def keep_of(wide, lane):
    low = jnp.where(wide >= 4.5, 2, jnp.where(wide >= 2.5, 1, 0))
    high = jnp.where(wide < 0.5, 1, jnp.where((wide < 1.5) | ((wide > 2.5) & (wide < 3.5)), 2, 3))
    return lane == low, lane == high


def kept_pair(planes, gates):
    one, two, three, four = planes
    low = jnp.where(gates >= 4.5, three, jnp.where(gates >= 2.5, two, one))
    high = jnp.where(gates < 0.5, two, jnp.where((gates < 1.5) | ((gates > 2.5) & (gates < 3.5)), three, four))
    return low, high


def eye(rows, cols):
    return one_hot((rows, cols), 1, lax.broadcasted_iota(jnp.int32, (rows, cols), 0))


def repeat_four(groups, width):
    rows = lax.broadcasted_iota(jnp.int32, (groups, width), 0)
    cols = lax.broadcasted_iota(jnp.int32, (groups, width), 1)
    return ((cols >> 2) == rows).astype(F32).astype(BF)


def plane_order():
    rows = lax.broadcasted_iota(jnp.int32, (HID, HID), 0)
    return one_hot((HID, HID), 1, 4 * (rows & 63) + (rows >> 6))


def pack_kernel(state_hbm, cot_hbm, sea_hbm, out_ref, state_ref, cot_ref, sea_ref, sems):
    copies = fetch((state_hbm, cot_hbm, sea_hbm), (state_ref, cot_ref, sea_ref), sems)
    for copy in copies:
        copy.wait()
    comp = lax.axis_index("comp")
    weight = jnp.where(comp == 1, sea_ref[...].astype(F32), 1.0)
    grad = (weight * cot_ref[...].astype(F32)).astype(BF)
    for place in range(8):
        out_ref[place, 0:FIELDS] = state_ref[...]
        out_ref[place, FIELDS : 2 * FIELDS] = grad


def kept_rows(gates, kernel):
    outputs = kernel.shape[0]
    rows = lax.broadcasted_iota(jnp.int32, (outputs, outputs // 4), 0) >> 2
    wide = dot(one_hot((outputs, outputs // 4), 1, rows), gates)
    low, high = keep_of(wide, lax.broadcasted_iota(jnp.int32, wide.shape, 0) & 3)
    return jnp.where(low | high, kernel, 0.0)


def prepare_kernel(
    turn_ref, first_gates_hbm, mid_gates_hbm, out_gates_hbm, first_hbm, mid_hbm, out_hbm,
    take_ref, give_ref, first_w_ref, first_back_ref, mid_w_ref, mid_back_ref, out_w_ref, out_back_ref,
    first_turned_ref, mid_turned_ref, out_turned_ref, first_wide_ref,
    first_gates_ref, mid_gates_ref, out_gates_ref, first_ref, mid_ref, out_ref, sems,
):
    copies = fetch(
        (first_gates_hbm, mid_gates_hbm, out_gates_hbm, first_hbm, mid_hbm, out_hbm),
        (first_gates_ref, mid_gates_ref, out_gates_ref, first_ref, mid_ref, out_ref), sems,
    )
    row = lax.axis_index(ROW_AXES)
    strip_of = lax.broadcasted_iota(jnp.int32, (8, 256), 1) >> 4
    along = lax.broadcasted_iota(jnp.int32, (8, 256), 1) & 15
    cells = jnp.zeros((8, 256), jnp.int32)
    for number, (source, side, reader) in enumerate(STRIPS):
        turn = turn_ref[side, lax.rem(ROW * row + reader - ROW + TILES, TILES)]
        first, step = edge_line(*EDGE_MAP[side][3])
        for turns in range(3):
            one, two = edge_line(*EDGE_MAP[side][turns])
            first, step = jnp.where(turn == turns, one, first), jnp.where(turn == turns, two, step)
        first = first + source * CELLS
        cells = jnp.where(strip_of == number, first + step * along, cells)
        place = lax.broadcasted_iota(jnp.int32, (TS, LINE), 1)
        wanted = first + step * lax.broadcasted_iota(jnp.int32, (TS, LINE), 0)
        take_ref[TS * number : TS * (number + 1)] = (place == wanted).astype(F32).astype(BF)
    give_ref[...] = one_hot((LINE, 256), 0, cells[0:1])
    for copy in copies:
        copy.wait()
    depth = FIELDS + COUPLED
    count = 9 * depth
    gates = first_gates_ref[...].astype(F32).astype(BF)
    wide = dot_tn(gates, repeat_four(HID // 4, HID))
    first_wide_ref[...] = wide.astype(BF)
    low, high = keep_of(wide, lax.broadcasted_iota(jnp.int32, (count, HID), 1) & 3)
    kernel = jnp.where(low | high, first_ref[...].astype(F32), 0.0)
    blank = jnp.zeros((PADC - depth, HID), F32)
    for a in range(3):
        for b in range(3):
            rows = slice(depth * (3 * a + b), depth * (3 * a + b + 1))
            first_w_ref[a, PADC * b : PADC * (b + 1)] = jnp.concatenate([kernel[rows], blank], 0).astype(BF)
        first_back_ref[HID * a : HID * (a + 1)] = dot_nt(eye(HID, HID), first_w_ref[a]).astype(BF)
    place = lax.broadcasted_iota(jnp.int32, (count, 9 * PADC), 0)
    tap = (place * 2731) >> 16
    first_turned_ref[...] = dot(gates, one_hot((count, 9 * PADC), 1, tap * PADC + place - depth * tap)).astype(BF)
    for a in range(3):
        cols = slice(3 * HID * a, 3 * HID * (a + 1))
        gates = mid_gates_ref[:, cols].astype(F32).astype(BF)
        mid_turned_ref[:, cols] = gates
        mid_back_ref[HID * a : HID * (a + 1)] = kept_rows(gates, dot_nt(eye(HID, HID), mid_ref[cols])).astype(BF)
        mid_w_ref[a] = dot_tn(mid_back_ref[HID * a : HID * (a + 1)], eye(HID, HID)).astype(BF)
        gates = out_gates_ref[:, cols].astype(F32).astype(BF)
        out_turned_ref[:, cols] = dot(eye(8, 4), gates).astype(BF)
        kernel = kept_rows(gates, out_ref[:, cols].astype(F32))
        kernel = jnp.concatenate([kernel, jnp.zeros((PADC - FIELDS, 3 * HID), F32)], 0)
        out_back_ref[PADC * a : PADC * (a + 1)] = kernel.astype(BF)
        out_w_ref[a] = kernel.T.astype(BF)


def start_kernel(line_ref, take_ref, field_ref, grad_ref, strips_ref):
    comp = lax.axis_index("comp")
    for col in range(ROW):
        own = line_ref[comp, col].astype(F32)
        other = line_ref[1 - comp, col][:FIELDS].astype(F32)[:COUPLED]
        blank = jnp.zeros((PADC - FIELDS - COUPLED, CELLS), F32)
        field = jnp.concatenate([own[:FIELDS], other, blank], 0)
        field_ref[CELLS * col : CELLS * (col + 1)] = field.T.astype(BF)
        blank = jnp.zeros((PADC - FIELDS, CELLS), F32)
        grad = jnp.concatenate([own[FIELDS:], blank], 0)
        grad_ref[CELLS * col : CELLS * (col + 1)] = grad.T.astype(BF)
    strips_ref[...] = dot(take_ref[...], field_ref[...]).astype(BF)


def send_strips(strips, up_ref, down_ref, local_ref):
    up_ref[0:80] = strips[UP]
    down_ref[0:80] = strips[DOWN]
    local_ref[0:96] = strips[LOCAL]


def back_strips(prev_ref, next_ref, local_ref):
    return jnp.concatenate([next_ref[80:160], prev_ref[80:160], local_ref[96:192]], 0)


def layer_one_kernel(
    field_ref, strips_ref, prev_ref, next_ref, grad_ref, first_ref, out_back_ref, take_ref,
    filled_ref, act_ref, hid_ref, local_ref, up_ref, down_ref, inner_ref,
    pad_ref,
):
    fill(filled_ref, field_ref[...], strips_ref[LOCAL], prev_ref[...], next_ref[...])
    for col in range(ROW):
        act = conv_tile(filled_ref, first_ref, col)
        act_ref[CELLS * col : CELLS * (col + 1)] = act
        hid_ref[CELLS * col : CELLS * (col + 1)] = (act * sigmoid(act)).astype(BF)
    send_strips(dot(take_ref[...], hid_ref[...]).astype(BF), up_ref, down_ref, local_ref)
    fold_row(
        lambda col: grad_ref[CELLS * col : CELLS * (col + 1)],
        out_back_ref, pad_ref, inner_ref, down_ref.at[80:160], up_ref.at[80:160], local_ref.at[96:192],
    )


def layer_two_kernel(
    hid_ref, local_in_ref, prev_ref, next_ref, inner_two_ref, mid_ref, mid_back_ref, take_ref, give_ref,
    filled_ref, grad_ref, hid_two_ref, local_ref, up_ref, down_ref, inner_ref,
    pad_ref,
):
    fill(filled_ref, hid_ref[...], local_in_ref[0:96], prev_ref[0:80], next_ref[0:80])
    strips = back_strips(prev_ref, next_ref, local_in_ref)
    for col in range(ROW):
        rows = slice(CELLS * col, CELLS * (col + 1))
        grad_hid = inner_two_ref[rows] + dot(give_ref[rows], strips)
        act = conv_tile(filled_ref, mid_ref, col)
        sig = sigmoid(act)
        hid_two_ref[rows] = (act * sig).astype(BF)
        grad_ref[rows] = (grad_hid * (sig * (1.0 + act * (1.0 - sig)))).astype(BF)
    send_strips(dot(take_ref[...], hid_two_ref[...]).astype(BF), up_ref, down_ref, local_ref)
    fold_row(
        lambda col: grad_ref[CELLS * col : CELLS * (col + 1)],
        mid_back_ref, pad_ref, inner_ref, down_ref.at[80:160], up_ref.at[80:160], local_ref.at[96:192],
    )


def gather_rows(filled_ref, a):
    return jnp.concatenate(
        [filled_ref[col, a : a + TS].reshape(CELLS, filled_ref.shape[3]) for col in range(ROW)], 0
    )


def term_pairs(filled_ref, grad, gates_ref, flat_ref):
    turned = dot_nt(plane_order(), grad).astype(BF)
    width = filled_ref.shape[3]
    for a in range(3):
        cols = slice(width * a, width * (a + 1))
        term = dot(turned, gather_rows(filled_ref, a))
        low, high = kept_pair([term[64 * m : 64 * (m + 1)] for m in range(4)], gates_ref[:, cols].astype(F32))
        flat_ref[0:64, cols] = low.astype(BF)
        flat_ref[64:128, cols] = high.astype(BF)


def mid_term_kernel(filled_ref, grad_ref, gates_ref, part_ref, pick_out_ref, pick_first_ref, flat_ref):
    col = lax.axis_index(("xh", "core"))
    term_pairs(filled_ref, grad_ref[...], gates_ref, flat_ref)
    shape = (16 * CHUNK, 1152)
    place = lax.broadcasted_iota(jnp.int32, shape, 0)
    block = (place * 2731) >> 16
    inside = place - CHUNK * block
    ahead = lax.broadcasted_iota(jnp.int32, shape, 1) - (72 * block + 18 * col)
    pick = ((ahead == inside) & (inside < 18)).astype(F32).astype(BF)
    late = ahead - 9 * (inside - 18)
    pick_out_ref[...] = ((late >= 0) & (late < 9) & (inside >= 18) & (inside < 20)).astype(F32).astype(BF)
    shape = (4 * SHARE, 1152)
    place = lax.broadcasted_iota(jnp.int32, shape, 0)
    inside = place & 15
    wanted = 14 * (4 * (place >> 4) + col) + inside
    tap = (wanted * 2731) >> 16
    target = tap * PADC + wanted - (FIELDS + COUPLED) * tap
    real = (inside < 14) & (wanted < 9 * (FIELDS + COUPLED))
    pick_first_ref[...] = ((lax.broadcasted_iota(jnp.int32, shape, 1) == target) & real).astype(F32).astype(BF)
    for half in range(2):
        part_ref[16 * CHUNK * half : 16 * CHUNK * (half + 1)] = dot_nt(
            pick, flat_ref[:, 1152 * half : 1152 * (half + 1)]
        )


def terms_kernel(
    hid_two_ref, local_ref, prev_ref, next_ref, inner_ref, act_ref, filled_zero_ref, grad_three_ref, give_ref,
    part_ref, pick_out_ref, pick_first_ref, first_gates_ref, out_gates_ref,
    buffer_ref, filled_ref, grad_ref,
    flat_ref, flat_zero_ref,
):
    fill(filled_ref, hid_two_ref[...], local_ref[0:96], prev_ref[0:80], next_ref[0:80])
    strips = back_strips(prev_ref, next_ref, local_ref)
    for col in range(ROW):
        rows = slice(CELLS * col, CELLS * (col + 1))
        grad_hid = inner_ref[rows] + dot(give_ref[rows], strips)
        grad_ref[rows] = (grad_hid * slope(act_ref[rows])).astype(BF)
    place = lax.broadcasted_iota(jnp.int32, (32, PADC), 0)
    group = place & 7
    wanted = jnp.where(group < 4, 4 * group + (place >> 3), -1)
    turned = dot_nt(one_hot((32, PADC), 1, wanted), grad_three_ref[...]).astype(BF)
    width = filled_ref.shape[3]
    for a in range(3):
        cols = slice(width * a, width * (a + 1))
        term = dot(turned, gather_rows(filled_ref, a))
        low, high = kept_pair([term[8 * m : 8 * (m + 1)] for m in range(4)], out_gates_ref[:, cols].astype(F32))
        pair = low + pltpu.roll(high, 4, 0)
        wide = jnp.broadcast_to(pair[None], (16, 8, width)).reshape(128, width)
        kernel_row = lax.broadcasted_iota(jnp.int32, (128, width), 1) + width * a
        slot = kernel_row - 9 * ((kernel_row * 7282) >> 16)
        mine = (lax.broadcasted_iota(jnp.int32, (128, width), 0) >> 3) == slot
        flat_ref[:, cols] = jnp.where(mine, wide, 0.0).astype(BF)
    term_pairs(filled_zero_ref, grad_ref[...], first_gates_ref, flat_zero_ref)
    for half in range(2):
        rows = slice(16 * CHUNK * half, 16 * CHUNK * (half + 1))
        part = part_ref[rows] + dot_nt(pick_out_ref[...], flat_ref[:, 1152 * half : 1152 * (half + 1)])
        buffer_ref[16 * half : 16 * (half + 1), 0:CHUNK] = part.astype(BF).reshape(16, CHUNK, PADC)
    share = dot_nt(pick_first_ref[...], flat_zero_ref[...]).astype(BF)
    for place in range(ROWS):
        kind = place // 8
        buffer_ref[place, CHUNK : CHUNK + SHARE] = share[SHARE * kind : SHARE * (kind + 1)]


def last_kernel(
    filled_ref, grad_ref, out_ref, first_back_ref, state_ref, sea_ref,
    estimate_ref, dx_ref, up_ref, down_ref, local_ref,
    pad_ref, dx_all_ref,
):
    comp = lax.axis_index("comp")
    col = lax.axis_index(("xh", "core"))
    width = filled_ref.shape[3]
    fold_row(
        lambda col: grad_ref[CELLS * col : CELLS * (col + 1)],
        first_back_ref, pad_ref, dx_all_ref, down_ref, up_ref, local_ref,
    )
    dx_ref[...] = dx_all_ref[pl.ds(pl.multiple_of(col * CELLS, CELLS), CELLS)]
    mine = filled_ref.at[col]
    total = None
    for a in range(3):
        piece = dot(mine[a : a + TS].reshape(CELLS, width), out_ref[a])
        total = piece if total is None else total + piece
    weight = jnp.where(comp == 1, sea_ref[...].astype(F32), 1.0)
    estimate_ref[...] = (state_ref[...].astype(F32) + weight * total.T[:FIELDS]).astype(BF)


def sum_kernel(spread_ref, share_ref, sum_ref):
    total = spread_ref[0].astype(F32)
    for place in range(1, ROWS):
        total = total + spread_ref[place].astype(F32)
    sum_ref[...] = total[:CHUNK]
    share = total[CHUNK:].astype(BF)
    for place in range(16):
        share_ref[place] = share


def finish_kernel(
    dx_ref, next_ref, prev_ref, local_ref, give_ref, cot_ref, sum_ref, mid_gates_ref, out_gates_ref,
    own_ref, send_ref, central_ref, closing_ref,
):
    col = lax.axis_index(("xh", "core"))
    give = give_ref[pl.ds(pl.multiple_of(col * CELLS, CELLS), CELLS)]
    strips = jnp.concatenate([next_ref[...], prev_ref[...], local_ref[...]], 0)
    total = (dx_ref[...] + dot(give, strips)).T
    own_ref[...] = cot_ref[...].astype(F32) + total[:FIELDS]
    send_ref[...] = total[FIELDS : FIELDS + COUPLED]
    tile = lax.axis_index(FACE)
    place = lax.broadcasted_iota(jnp.int32, (CHUNK, 9 * HID), 0)
    mine = one_hot((CHUNK, 9 * HID), 1, jnp.where(place < 18, 18 * tile + place, -1))
    sums = sum_ref[...]
    repeat = repeat_four(HID // 4, HID)
    wide = dot(dot_nt(mine, mid_gates_ref[...]).astype(BF), repeat)
    low, high = keep_of(wide, lax.broadcasted_iota(jnp.int32, (CHUNK, HID), 1) & 3)
    lows, highs = dot_exact_right(sums[:, :64], repeat), dot_exact_right(sums[:, 64:], repeat)
    central = jnp.where(low, lows, jnp.where(high, highs, 0.0))
    for line in range(18):
        central_ref[:, HID * line : HID * (line + 1)] = central[line : line + 1]
    place = lax.broadcasted_iota(jnp.int32, (CHUNK, CHUNK), 0)
    late = (place >= 9).astype(jnp.int32)
    spread = dot_exact(one_hot((CHUNK, CHUNK), 1, 18 + late), sums)
    place = lax.broadcasted_iota(jnp.int32, (CHUNK, PADC), 0)
    slot = place - 9 * (place >= 9).astype(jnp.int32)
    lane = lax.broadcasted_iota(jnp.int32, (CHUNK, PADC), 1)
    spread = jnp.where((lane >> 3) == slot, spread, 0.0)
    flat = 3 * PADC
    from_lane = lax.broadcasted_iota(jnp.int32, (PADC, flat), 0) & 7
    group = (lax.broadcasted_iota(jnp.int32, (PADC, flat), 1) & 15) >> 2
    lows = dot_exact_right(spread, (from_lane == group).astype(F32).astype(BF))
    highs = dot_exact_right(spread, (from_lane == group + 4).astype(F32).astype(BF))
    group = (lax.broadcasted_iota(jnp.int32, (8, flat), 1) & 15) >> 2
    wide = dot(dot_nt(mine, out_gates_ref[...]).astype(BF), one_hot((8, flat), 0, group))
    lane = lax.broadcasted_iota(jnp.int32, (CHUNK, flat), 1)
    low, high = keep_of(wide, lane & 3)
    closing = jnp.where(low, lows, jnp.where(high, highs, 0.0))
    here = lax.broadcasted_iota(jnp.int32, (CHUNK, flat), 0) == (lane >> 4)
    closing_ref[...] = jnp.sum(jnp.where(here, closing, 0.0), 0, keepdims=True)[:, : 18 * FIELDS]


def opening_kernel(share_ref, wide_ref, out_ref):
    count = 9 * (FIELDS + COUPLED)
    wanted = lax.broadcasted_iota(jnp.int32, (count, 16 * SHARE), 0)
    block = (wanted * 4682) >> 16
    pick = one_hot((count, 16 * SHARE), 1, SHARE * block + wanted - 14 * block)
    pairs = dot(pick, share_ref[...]).astype(BF)
    repeat = repeat_four(HID // 4, HID)
    low, high = keep_of(wide_ref[...].astype(F32), lax.broadcasted_iota(jnp.int32, (count, HID), 1) & 3)
    out_ref[...] = jnp.where(low, dot(pairs[:, :64], repeat), jnp.where(high, dot(pairs[:, 64:], repeat), 0.0))


VMEM = pl.BlockSpec(memory_space=pltpu.VMEM)
SMEM = pl.BlockSpec(memory_space=pltpu.SMEM)
HBM = pl.BlockSpec(memory_space=pltpu.HBM)


def call(body, out, args, scratch=(), scalars=(), far=(), flops=0, limit=10):
    specs = [SMEM if place in scalars else HBM if place in far else VMEM for place in range(len(args))]
    size = sum(int(np.prod(item.shape)) * item.dtype.itemsize for item in list(args) + list(out))
    return pl.pallas_call(
        body,
        out_shape=[jax.ShapeDtypeStruct(item.shape, item.dtype) for item in out],
        in_specs=specs,
        out_specs=[VMEM] * len(out),
        scratch_shapes=list(scratch),
        compiler_params=pltpu.CompilerParams(vmem_limit_bytes=limit * 1024 * 1024),
        cost_estimate=pl.CostEstimate(flops=flops, bytes_accessed=size, transcendentals=0),
    )(*args)


def sds(shape, kind):
    return jax.ShapeDtypeStruct(shape, kind)


def row_shift(value, step):
    pairs = [(face, (face + ROW * step) % TILES) for face in range(TILES)]
    return lax.ppermute(value, FACE, pairs)


def body(
    state, cotangent, land_sea, turn_table, first_kernel, mid_kernel, out_kernel, first_gates, mid_gates, out_gates
):
    sea = land_sea.reshape(1, CELLS)
    depth = FIELDS + COUPLED

    packed = call(pack_kernel, [sds((8, 2 * FIELDS, CELLS), BF)], [state[0], cotangent[0], sea],
        scratch=[
            pltpu.VMEM((FIELDS, CELLS), BF), pltpu.VMEM((FIELDS, CELLS), BF), pltpu.VMEM((1, CELLS), jnp.int32),
            pltpu.SemaphoreType.DMA((3,)),
        ],
        far=(0, 1, 2),
    )[0]
    line = lax.all_to_all(packed, LINE_AXES, 0, 0).reshape(2, ROW, 2 * FIELDS, CELLS)

    (
        take, give, first_w, first_back, mid_w, mid_back, out_w, out_back, first_turned, mid_turned, out_turned,
        first_wide,
    ) = call(
        prepare_kernel,
        [
            sds((256, LINE), BF), sds((LINE, 256), BF), sds((3, 3 * PADC, HID), BF), sds((3 * HID, 3 * PADC), BF),
            sds((3, 3 * HID, HID), BF), sds((3 * HID, 3 * HID), BF), sds((3, 3 * HID, PADC), BF),
            sds((3 * PADC, 3 * HID), BF), sds((64, 9 * PADC), BF), sds((64, 9 * HID), BF), sds((8, 9 * HID), BF),
            sds((9 * depth, HID), BF),
        ],
        [turn_table.T, first_gates[0].T, mid_gates[0].T, out_gates[0].T, first_kernel[0], mid_kernel[0],
         out_kernel[0].T],
        scratch=[
            pltpu.VMEM((64, 9 * depth), jnp.int32), pltpu.VMEM((64, 9 * HID), jnp.int32),
            pltpu.VMEM((4, 9 * HID), jnp.int32), pltpu.VMEM((9 * depth, HID), BF), pltpu.VMEM((9 * HID, HID), BF),
            pltpu.VMEM((FIELDS, 9 * HID), BF), pltpu.SemaphoreType.DMA((6,)),
        ],
        scalars=(0,), far=(1, 2, 3, 4, 5, 6), flops=5 * 10**9,
    )

    field, grad_cells, strips_zero = call(
        start_kernel,
        [sds((LINE, PADC), BF), sds((LINE, PADC), BF), sds((256, PADC), BF)], [line, take],
    )
    prev_zero = row_shift(strips_zero[UP], 1)
    next_zero = row_shift(strips_zero[DOWN], -1)

    exchange = [sds((192, HID), BF), sds((160, HID), BF), sds((160, HID), BF), sds((LINE, HID), F32)]
    filled_zero, act_one, hid_one, local_one, up_one, down_one, inner_two = call(
        layer_one_kernel,
        [sds((ROW, TS + 2, TS, 3 * PADC), BF), sds((LINE, HID), F32), sds((LINE, HID), BF)] + exchange,
        [field, strips_zero, prev_zero, next_zero, grad_cells, first_w, out_back, take],
        scratch=[pltpu.VMEM((TS + 2, TS, 3 * PADC), BF)],
    )
    prev_one = row_shift(up_one, 1)
    next_one = row_shift(down_one, -1)

    filled_one, grad_two, hid_two, local_two, up_two, down_two, inner_one = call(
        layer_two_kernel,
        [sds((ROW, TS + 2, TS, 3 * HID), BF), sds((LINE, HID), BF), sds((LINE, HID), BF)] + exchange,
        [hid_one, local_one, prev_one, next_one, inner_two, mid_w, mid_back, take, give],
        scratch=[pltpu.VMEM((TS + 2, TS, 3 * HID), BF)],
    )
    prev_two = row_shift(up_two, 1)
    next_two = row_shift(down_two, -1)

    part, pick_out, pick_first = call(
        mid_term_kernel,
        [sds((32 * CHUNK, PADC), F32), sds((16 * CHUNK, 1152), BF), sds((4 * SHARE, 1152), BF)],
        [filled_one, grad_two, mid_turned],
        scratch=[pltpu.VMEM((PADC, 9 * HID), BF)], flops=2 * 10**9,
    )

    buffer, filled_two, grad_one = call(
        terms_kernel,
        [sds((ROWS, CHUNK + SHARE, PADC), BF), sds((ROW, TS + 2, TS, 3 * HID), BF), sds((LINE, HID), BF)],
        [hid_two, local_two, prev_two, next_two, inner_one, act_one, filled_zero, grad_cells, give,
         part, pick_out, pick_first, first_turned, out_turned],
        scratch=[pltpu.VMEM((PADC, 9 * HID), BF), pltpu.VMEM((PADC, 9 * PADC), BF)],
    )
    spread = lax.all_to_all(buffer, ROW_AXES, 0, 0)

    estimate, dx_own, up_three, down_three, local_three = call(
        last_kernel,
        [sds((FIELDS, CELLS), BF), sds((CELLS, PADC), F32), sds((80, PADC), BF), sds((80, PADC), BF),
         sds((96, PADC), BF)],
        [filled_two, grad_one, out_w, first_back, state[0], sea],
        scratch=[pltpu.VMEM((TS + 2, TS, 3 * HID), BF), pltpu.VMEM((LINE, PADC), F32)], flops=2 * 10**9,
    )
    prev_three = row_shift(up_three, 1)
    next_three = row_shift(down_three, -1)

    shared, summed = call(sum_kernel, [sds((16, SHARE, PADC), BF), sds((CHUNK, PADC), F32)], [spread])
    opened = lax.all_to_all(shared, ("y", "xh", "core"), 0, 0).reshape(16 * SHARE, PADC)

    own, send, central, closing = call(
        finish_kernel,
        [sds((FIELDS, CELLS), F32), sds((COUPLED, CELLS), F32), sds((1, 18 * HID), F32), sds((1, 18 * FIELDS), F32)],
        [dx_own, next_three, prev_three, local_three, give, cotangent[0], summed, mid_turned, out_turned],
    )
    returned = lax.ppermute(send, "comp", [(0, 1), (1, 0)])
    adjoint = own + jnp.pad(returned, ((0, FIELDS - COUPLED), (0, 0)))
    opening = call(opening_kernel, [sds((9 * depth, HID), F32)], [opened, first_wide])[0]
    return estimate[None], adjoint[None], opening[None], central, closing


def solution(mesh):
    fine = Mesh(mesh.devices.reshape(2, 4, 8, 2, 2), ("comp",) + FACE)
    whole = P("comp", None, None)
    in_specs = (P("comp", None, FACE), P("comp", None, FACE), P(FACE), P()) + (whole,) * 6
    out_specs = (P("comp", None, FACE), P("comp", None, FACE), whole, P("comp", FACE), P("comp", FACE))

    return jax.shard_map(body, mesh=fine, in_specs=in_specs, out_specs=out_specs, check_vma=False)
```

time: 145 us -> 114 us (0.79)
  Pallas kernels: 41.1 us -> 25.4 us
  other arithmetic: 12.3 us -> 0.61 us
  local copies, waits for them, and re-layouts: 22.2 us -> 20.5 us
    pallas_call x9 -> x11, Pallas kernels: 41.1 us -> 25.4 us  [call(): pl.pallas_call(body, out_shape=[jax.ShapeDtypeStruct(item.shape, item.dty...]
    unnamed x43 -> x64, local copies, waits for them, and re-layouts: 7.84 us -> 20.5 us
    select_n x7 -> x0, other arithmetic: 5.64 us -> none  [the longest x1 1.41 us: body(): jnp.where(real, wanted // depth * PADC + wanted % depth, -1).reshape(-1, 1)]
    transpose x3 -> x0, local copies, waits for them, and re-layouts: 4.53 us -> none  [the longest x1 2.37 us: body(): mid_back = mid_w.transpose(0, 2, 1).reshape(3 * HID, 3 * HID)]
    all_to_all x3, waiting for transfers between devices: 11.2 us -> 6.72 us  [the longest x1 6.71 us: body(): lax.all_to_all(shared, ('y', 'xh', 'core'), 0, 0).reshape(16 * SHARE, PADC)]
    ppermute x8, waiting for transfers between devices: 9.05 us -> 13.1 us  [row_shift(): return lax.ppermute(value, FACE, pairs)]
    slice x5 -> x0, local copies, waits for them, and re-layouts: 2.88 us -> none  [the longest x1 1.34 us: body(): strips_zero[LOCAL]]
    pad x2 -> x0, local copies, waits for them, and re-layouts: 2.18 us -> none  [the longest x1 1.24 us: body(): jnp.pad(gated_out, ((0, 0), (0, PADC - FIELDS))).reshape(3, 3 * HID, PADC)]
  transfers between devices with their start and end apart: 12 -> 12, of which waited for: 5 -> 6; matrix products, arithmetic and copies ran while one was open for 18% -> 1% of each run, Pallas kernels for 11% -> 9%
where the time goes in v2:
time: 114 us; the launch traced here: 113 us
  starting transfers between devices  46 us (40%)
  Pallas kernels  25.4 us (22%)
  local copies, waits for them, and re-layouts  20.5 us (18%)
  waiting for transfers between devices  19.8 us (17%)
    pallas_call x11, Pallas kernels, call(): pl.pallas_call(body, out_shape=[jax.ShapeDtypeStruct(item.shape, item.dty...  25.4 us
    ppermute x8, starting transfers between devices, row_shift(): return lax.ppermute(value, FACE, pairs)  21.5 us
    unnamed x64, local copies, waits for them, and re-layouts  20.5 us
    ppermute x8, waiting for transfers between devices, row_shift(): return lax.ppermute(value, FACE, pairs)  13.1 us
    all_to_all x1, starting transfers between devices, body(): lax.all_to_all(shared, ('y', 'xh', 'core'), 0, 0).reshape(16 * SHARE, PADC)  10.6 us
    all_to_all x1, waiting for transfers between devices, body(): lax.all_to_all(shared, ('y', 'xh', 'core'), 0, 0).reshape(16 * SHARE, PADC)  6.71 us
    all_to_all x1, starting transfers between devices, body(): lax.all_to_all(packed, LINE_AXES, 0, 0).reshape(2, ROW, 2 * FIELDS, CELLS)  6.48 us
    all_to_all x1, starting transfers between devices, body(): spread = lax.all_to_all(buffer, ROW_AXES, 0, 0)  6.01 us
  transfers between devices with their start and end apart: 12, of which 6 were waited for; matrix products, arithmetic and copies ran while one was open for 1% of the time, Pallas kernels for 9%

profile of v2, /device:TPU:1, one launch (start us, length us, event | category | flops | bytes accessed | tf_op | source)
XLA Modules:
  0.0 113.1 jit_solution(10215162721271069662)
XLA Ops:
  0.6 0.7 copy-done.13
  1.3 0.7 copy-done.15
  2.0 0.7 copy-done.17
  2.7 0.7 shard_map.137
  3.4 6.5 %all-to-all-start = ((bf16[8,32,256]{2,1,0:T(8,128)(2,1)}), bf16[8,32,256]{2,1,0:T(8,128)(2,1)S(1)}, u32[]{:S(2)}, u32[]{:S(2)}) async-start(bf16[8,32,256]{2,1,0:T(8,128)(2,1)} %shard_map.137), calls=%async_computation | async-start | bytes 262144 | tf_op jit(solution)/shard_map/all_to_all | solution.py:568
  9.9 1.3 %copy-done.19 = bf16[1,2304,256]{2,1,0:T(8,128)(2,1)S(1)} copy-done((bf16[1,2304,256]{2,1,0:T(8,128)(2,1)S(1)}, bf16[1,2304,256]{2,1,0:T(8,128)(2,1)}, u32[]{:S(2)}) %copy-start.19) | copy-done | bytes 1179672
  11.2 1.1 copy-done.20
  12.2 0.9 copy-done.23
  13.1 0.9 copy-done.24
  14.0 0.8 copy-done.25
  14.9 0.8 copy-done.26
  15.6 0.7 copy-done.27
  16.3 4.4 %shard_map.138 = (bf16[256,1024]{1,0:T(8,128)(2,1)S(1)}, bf16[1024,256]{1,0:T(8,128)(2,1)S(1)}, bf16[3,384,256]{2,1,0:T(8,128)(2,1)S(1)}, bf16[768,384]{1,0:T(8,...) custom-call(s32[4,128]{1,0:T(4,128)S(1)} %bitcast.38, ...), custom_call_target="tpu_custom_call" | custom-call | flops 5000000000 | bytes 8404992 | tf_op jit(solution)/shard_map/pallas_call | solution.py:535
  20.7 0.8 copy-done
  21.5 0.8 copy-done.2
  22.3 0.7 copy-done.4
  23.1 0.7 copy-done.7
  23.7 0.6 copy-done.9
  24.3 0.6 copy-done.11
  25.0 0.8 copy-done.28
  25.8 0.8 copy-done.30
  27.1 7.4 %collective-permute-start.1 = (bf16[80,128]{1,0:T(8,128)(2,1)S(1)}, bf16[80,128]{1,0:T(8,128)(2,1)S(1)}, u32[]{:S(2)}, u32[]{:S(2)}) collective-permute-start(bf16[80,128]{1,0:T(8,128)(2,1)S(1)} %get-tuple-element.97), channel_id=1, source_target_pairs={{0,124},{1,125},{2,126},{3,127},{4,0},{5,1},{6,2},{7,3},{8,4},{9,5... | collective-permute-start | bytes 61448 | tf_op jit(solution)/shard_map/ppermute | solution.py:552
  34.5 0.9 collective-permute-done.1.next_ref
  35.4 5.0 %collective-permute-done.prev_ref = bf16[80,128]{1,0:T(8,128)(2,1)S(1)} collective-permute-done((bf16[80,128]{1,0:T(8,128)(2,1)S(1)}, bf16[80,128]{1,0:T(8,128)(2,1)S(1)}, u32[]{:S(2)}, u32[]{:S(2)}) %collective-permute-start) | collective-permute-done | bytes 20512 | tf_op jit(solution)/shard_map/ppermute | solution.py:552
  40.5 1.1 copy-done.1
  41.5 1.1 copy-done.3
  42.6 3.2 %shard_map.140 = (bf16[4,18,16,384]{3,2,1,0:T(8,128)(2,1)S(1)}, f32[1024,256]{1,0:T(8,128)S(1)}, bf16[1024,256]{1,0:T(8,128)(2,1)S(1)}, bf16[192,256]{1,0:T(8,12...) custom-call(bf16[1024,128]{1,0:T(8,128)(2,1)S(1)} %get-tuple-element.52.field_ref, ...), custom_call_target="tpu_custom_call" | custom-call | bytes 6103040 | tf_op jit(solution)/shard_map/pallas_call | solution.py:535
  45.8 4.8 %collective-permute-start.3 = (bf16[160,256]{1,0:T(8,128)(2,1)S(1)}, bf16[160,256]{1,0:T(8,128)(2,1)S(1)}, u32[]{:S(2)}, u32[]{:S(2)}) collective-permute-start(bf16[160,256]{1,0:T(8,128)(2,1)S(1)} %get-tuple-element.60), channel_id=1, source_target_pairs={{0,124},{1,125},{2,126},{3,127},{4,0},{5,1},{6,2},{7,3},{8,4},{9,5... | collective-permute-start | bytes 245768 | tf_op jit(solution)/shard_map/ppermute | solution.py:552
  50.6 1.8 %collective-permute-done.2.prev_ref = bf16[160,256]{1,0:T(8,128)(2,1)S(1)} collective-permute-done((bf16[160,256]{1,0:T(8,128)(2,1)S(1)}, bf16[160,256]{1,0:T(8,128)(2,1)S(1)}, u32[]{:S(2)}, u32[]{:S(2)}) %collective-permute-start.2) | collective-permute-done | bytes 81952 | tf_op jit(solution)/shard_map/ppermute | solution.py:552
  52.4 4.4 %shard_map.141 = (bf16[4,18,16,768]{3,2,1,0:T(8,128)(2,1)S(1)}, bf16[1024,256]{1,0:T(8,128)(2,1)S(1)}, bf16[1024,256]{1,0:T(8,128)(2,1)S(1)}, bf16[192,256]{1,0:...) custom-call(bf16[1024,256]{1,0:T(8,128)(2,1)S(1)} %get-tuple-element.57.hid_r, ...), custom_call_target="tpu_custom_call" | custom-call | bytes 9371648 | tf_op jit(solution)/shard_map/pallas_call | solution.py:535
  56.8 4.9 %collective-permute-start.5 = (bf16[160,256]{1,0:T(8,128)(2,1)S(1)}, bf16[160,256]{1,0:T(8,128)(2,1)S(1)}, u32[]{:S(2)}, u32[]{:S(2)}) collective-permute-start(bf16[160,256]{1,0:T(8,128)(2,1)S(1)} %get-tuple-element.68), channel_id=1, source_target_pairs={{0,124},{1,125},{2,126},{3,127},{4,0},{5,1},{6,2},{7,3},{8,4},{9,5... | collective-permute-start | bytes 245768 | tf_op jit(solution)/shard_map/ppermute | solution.py:552
  61.7 2.4 %shard_map.142 = (f32[768,128]{1,0:T(8,128)S(1)}, bf16[384,1152]{1,0:T(8,128)(2,1)S(1)}, bf16[64,1152]{1,0:T(8,128)(2,1)S(1)}) custom-call(bf16[4,18,16,768]{3,2,1,0:T(8,128)(2,1)S(1)} %get-tuple-element.72.filled_ref, bf16[1024,256]{1,0:T(8,128)(2,1)S(1)} %get-tuple-element.73.grad_ref, bf16[64,2304]{1,0:T(8,128)(2,1)S(1)} %copy-done.5), custom_call_target="tpu_custom_call" | custom-call | flops 2000000000 | bytes 4014080 | tf_op jit(solution)/shard_map/pallas_call | solution.py:535
  64.2 4.0 %shard_map.143 = (bf16[32,40,128]{2,1,0:T(8,128)(2,1)}, bf16[4,18,16,768]{3,2,1,0:T(8,128)(2,1)S(1)}, bf16[1024,256]{1,0:T(8,128)(2,1)S(1)}) custom-call(bf16[1024,256]{1,0:T(8,128)(2,1)S(1)} %get-tuple-element.65.hid_two_ref, bf16[192,256]{1,0:T(8,128)(2,1)S(1)} %get-tuple-element.66.local_ref, bf16[160,256]{1,0:T(8,128)(2,1)S(1)} %collective-permute-done.4.prev_ref, ...), custom_call_target="tpu_custom_call" | custom-call | bytes 8785920 | tf_op jit(solution)/shard_map/pallas_call | solution.py:535
  68.2 0.8 copy-done.21
  69.0 6.0 %all-to-all-start.1 = ((bf16[32,40,128]{2,1,0:T(8,128)(2,1)}), bf16[32,40,128]{2,1,0:T(8,128)(2,1)S(1)}, u32[]{:S(2)}, u32[]{:S(2)}) async-start(bf16[32,40,128]{2,1,0:T(8,128)(2,1)} %get-tuple-element.89), calls=%async_computation.1 | async-start | bytes 655360 | tf_op jit(solution)/shard_map/all_to_all | solution.py:631
  75.0 1.0 copy-done.22
  76.1 1.1 copy-done.29
  77.1 1.1 copy-done.31
  78.2 2.6 %shard_map.144 = (bf16[16,256]{1,0:T(8,128)(2,1)}, f32[256,128]{1,0:T(8,128)S(1)}, bf16[80,128]{1,0:T(8,128)(2,1)S(1)}, bf16[80,128]{1,0:T(8,128)(2,1)S(1)}, bf16[96,128]{1,0:T(8,128)(2,1)S(1)}) custom-call(bf16[4,18,16,768]{3,2,1,0:T(8,128)(2,1)S(1)} %get-tuple-element.80.filled_ref, bf16[1024,256]{1,0:T(8,128)(2,1)S(1)} %copy-done.22, ...), custom_call_target="tpu_custom_call" | custom-call | flops 2000000000 | bytes 3687424 | tf_op jit(solution)/shard_map/pallas_call | solution.py:535
  80.9 4.4 %collective-permute-start.6 = (bf16[80,128]{1,0:T(8,128)(2,1)S(1)}, bf16[80,128]{1,0:T(8,128)(2,1)S(1)}, u32[]{:S(2)}, u32[]{:S(2)}) collective-permute-start(bf16[80,128]{1,0:T(8,128)(2,1)S(1)} %get-tuple-element.86), channel_id=1, source_target_pairs={{0,124},{1,125},{2,126},{3,127},{4,0},{5,1},{6,2},{7,3},{8,4},{9,5... | collective-permute-start | bytes 61448 | tf_op jit(solution)/shard_map/ppermute | solution.py:552
  85.3 0.7 shard_map.145
  86.2 5.0 %collective-permute-done.7.prev_ref = bf16[80,128]{1,0:T(8,128)(2,1)S(1)} collective-permute-done((bf16[80,128]{1,0:T(8,128)(2,1)S(1)}, bf16[80,128]{1,0:T(8,128)(2,1)S(1)}, u32[]{:S(2)}, u32[]{:S(2)}) %collective-permute-start.7) | collective-permute-done | bytes 20512 | tf_op jit(solution)/shard_map/ppermute | solution.py:552
  91.3 1.5 %shard_map.146 = (f32[16,256]{1,0:T(8,128)S(1)}, f32[8,256]{1,0:T(8,128)S(1)}, f32[1,4608]{1,0:T(1,128)}, f32[1,288]{1,0:T(1,128)}) custom-call(f32[256,128]{1,0:T(8,128)S(1)} %get-tuple-element.85.dx_ref, bf16[80,128]{1,0:T(8,128)(2,1)S(1)} %collective-permute-done.6.next_ref, bf16[80,128]{1,0:T(8,128)(2,1)S(1)} %collective-permute-done.7.prev_ref, ...), custom_call_target="tpu_custom_call" | custom-call | bytes 1117312 | tf_op jit(solution)/shard_map/pallas_call | solution.py:535
  92.7 1.4 %collective-permute-start.8 = (f32[8,256]{1,0:T(8,128)S(1)}, f32[8,256]{1,0:T(8,128)S(1)}, u32[]{:S(2)}, u32[]{:S(2)}) collective-permute-start(f32[8,256]{1,0:T(8,128)S(1)} %get-tuple-element.92), channel_id=1, source_target_pairs={{0,128},{128,0},{1,129},{129,1},{2,130},{130,2},{3,131},{131,3},{4... | collective-permute-start | bytes 24584 | tf_op jit(solution)/shard_map/ppermute | solution.py:651
  94.2 10.6 %all-to-all-start.2 = ((bf16[16,16,128]{2,1,0:T(8,128)(2,1)}), bf16[16,16,128]{2,1,0:T(8,128)(2,1)S(1)}, u32[]{:S(2)}, u32[]{:S(2)}) async-start(bf16[16,16,128]{2,1,0:T(8,128)(2,1)} %get-tuple-element.93), calls=%async_computation.2 | async-start | bytes 131072 | tf_op jit(solution)/shard_map/all_to_all | solution.py:644
  104.7 0.6 add_bitcast_fusion
  105.3 6.7 %all-to-all-done.2 = bf16[16,16,128]{2,1,0:T(8,128)(2,1)S(1)} async-done(((bf16[16,16,128]{2,1,0:T(8,128)(2,1)}), bf16[16,16,128]{2,1,0:T(8,128)(2,1)S(1)}, u32[]{:S(2)}, u32[]{:S(2)}) %all-to-all-start.2) | async-done | bytes 65568 | tf_op jit(solution)/shard_map/all_to_all | solution.py:644
  112.0 1.1 shard_map.147
  (53 shorter events, 0.8 us)
Async XLA Ops:
  0.6 0.7 copy-start.13
  1.3 0.7 copy-start.15
  2.0 0.7 copy-start.17
  3.4 23.2 %all-to-all-start = ((bf16[8,32,256]{2,1,0:T(8,128)(2,1)}), bf16[8,32,256]{2,1,0:T(8,128)(2,1)S(1)}, u32[]{:S(2)}, u32[]{:S(2)}) async-start(bf16[8,32,256]{2,1,0:T(8,128)(2,1)} %shard_map.137), calls=%async_computation | async-start | bytes 262144 | tf_op jit(solution)/shard_map/all_to_all | solution.py:568
  9.9 1.3 %copy-start.19 = (bf16[1,2304,256]{2,1,0:T(8,128)(2,1)S(1)}, bf16[1,2304,256]{2,1,0:T(8,128)(2,1)}, u32[]{:S(2)}) copy-start(bf16[1,2304,256]{2,1,0:T(8,128)(2,1)} %param.15) | copy-start | bytes 3538948
  11.2 1.1 copy-start.20
  12.2 0.9 copy-start.23
  13.1 0.9 copy-start.24
  14.0 0.8 copy-start.25
  14.9 0.8 copy-start.26
  15.6 0.7 copy-start.27
  20.7 0.8 copy-start
  21.5 0.8 copy-start.2
  22.3 0.7 copy-start.4
  23.1 0.7 copy-start.7
  23.7 0.6 copy-start.9
  24.3 0.6 copy-start.11
  25.0 0.8 copy-start.28
  25.8 0.8 copy-start.30
  27.1 8.3 %collective-permute-start.1 = (bf16[80,128]{1,0:T(8,128)(2,1)S(1)}, bf16[80,128]{1,0:T(8,128)(2,1)S(1)}, u32[]{:S(2)}, u32[]{:S(2)}) collective-permute-start(bf16[80,128]{1,0:T(8,128)(2,1)S(1)} %get-tuple-element.97), channel_id=1, source_target_pairs={{0,124},{1,125},{2,126},{3,127},{4,0},{5,1},{6,2},{7,3},{8,4},{9,5... | collective-permute-start | bytes 61448 | tf_op jit(solution)/shard_map/ppermute | solution.py:552
  34.5 6.0 %collective-permute-start = (bf16[80,128]{1,0:T(8,128)(2,1)S(1)}, bf16[80,128]{1,0:T(8,128)(2,1)S(1)}, u32[]{:S(2)}, u32[]{:S(2)}) collective-permute-start(bf16[80,128]{1,0:T(8,128)(2,1)S(1)} %get-tuple-element.98), channel_id=1, source_target_pairs={{0,4},{1,5},{2,6},{3,7},{4,8},{5,9},{6,10},{7,11},{8,12},{9,13},{1... | collective-permute-start | bytes 61448 | tf_op jit(solution)/shard_map/ppermute | solution.py:552
  40.5 1.1 copy-start.1
  41.5 1.1 copy-start.3
  45.8 6.6 %collective-permute-start.2 = (bf16[160,256]{1,0:T(8,128)(2,1)S(1)}, bf16[160,256]{1,0:T(8,128)(2,1)S(1)}, u32[]{:S(2)}, u32[]{:S(2)}) collective-permute-start(bf16[160,256]{1,0:T(8,128)(2,1)S(1)} %get-tuple-element.59), channel_id=1, source_target_pairs={{0,4},{1,5},{2,6},{3,7},{4,8},{5,9},{6,10},{7,11},{8,12},{9,13},{1... | collective-permute-start | bytes 245768 | tf_op jit(solution)/shard_map/ppermute | solution.py:552
  45.8 6.6 %collective-permute-start.3 = (bf16[160,256]{1,0:T(8,128)(2,1)S(1)}, bf16[160,256]{1,0:T(8,128)(2,1)S(1)}, u32[]{:S(2)}, u32[]{:S(2)}) collective-permute-start(bf16[160,256]{1,0:T(8,128)(2,1)S(1)} %get-tuple-element.60), channel_id=1, source_target_pairs={{0,124},{1,125},{2,126},{3,127},{4,0},{5,1},{6,2},{7,3},{8,4},{9,5... | collective-permute-start | bytes 245768 | tf_op jit(solution)/shard_map/ppermute | solution.py:552
  52.4 9.3 %copy-start.5 = (bf16[64,2304]{1,0:T(8,128)(2,1)S(1)}, bf16[64,2304]{1,0:T(8,128)(2,1)}, u32[]{:S(2)}) copy-start(bf16[64,2304]{1,0:T(8,128)(2,1)} %copy-done.4) | copy-start | bytes 884740
  56.8 7.3 %collective-permute-start.4 = (bf16[160,256]{1,0:T(8,128)(2,1)S(1)}, bf16[160,256]{1,0:T(8,128)(2,1)S(1)}, u32[]{:S(2)}, u32[]{:S(2)}) collective-permute-start(bf16[160,256]{1,0:T(8,128)(2,1)S(1)} %get-tuple-element.67), channel_id=1, source_target_pairs={{0,4},{1,5},{2,6},{3,7},{4,8},{5,9},{6,10},{7,11},{8,12},{9,13},{1... | collective-permute-start | bytes 245768 | tf_op jit(solution)/shard_map/ppermute | solution.py:552
  56.8 7.3 %collective-permute-start.5 = (bf16[160,256]{1,0:T(8,128)(2,1)S(1)}, bf16[160,256]{1,0:T(8,128)(2,1)S(1)}, u32[]{:S(2)}, u32[]{:S(2)}) collective-permute-start(bf16[160,256]{1,0:T(8,128)(2,1)S(1)} %get-tuple-element.68), channel_id=1, source_target_pairs={{0,124},{1,125},{2,126},{3,127},{4,0},{5,1},{6,2},{7,3},{8,4},{9,5... | collective-permute-start | bytes 245768 | tf_op jit(solution)/shard_map/ppermute | solution.py:552
  61.7 2.5 %copy-start.8 = (bf16[64,1152]{1,0:T(8,128)(2,1)S(1)}, bf16[64,1152]{1,0:T(8,128)(2,1)}, u32[]{:S(2)}) copy-start(bf16[64,1152]{1,0:T(8,128)(2,1)} %copy-done.7) | copy-start | bytes 442372
  61.7 2.5 %copy-start.10 = (bf16[8,2304]{1,0:T(8,128)(2,1)S(1)}, bf16[8,2304]{1,0:T(8,128)(2,1)}, u32[]{:S(2)}) copy-start(bf16[8,2304]{1,0:T(8,128)(2,1)} %copy-done.9) | copy-start | bytes 110596
  64.1 10.9 %copy-start.16 = (bf16[1,16,256]{2,1,0:T(8,128)(2,1)S(1)}, bf16[1,16,256]{2,1,0:T(8,128)(2,1)}, u32[]{:S(2)}) copy-start(bf16[1,16,256]{2,1,0:T(8,128)(2,1)} %param.10) | copy-start | bytes 24580
  64.2 10.9 %copy-start.18 = (s32[256]{0:T(256)S(1)}, s32[256]{0:T(256)}, u32[]{:S(2)}) copy-start(s32[256]{0:T(256)} %param.12) | copy-start | bytes 3076
  68.2 0.8 copy-start.21
  69.0 16.3 %all-to-all-start.1 = ((bf16[32,40,128]{2,1,0:T(8,128)(2,1)}), bf16[32,40,128]{2,1,0:T(8,128)(2,1)S(1)}, u32[]{:S(2)}, u32[]{:S(2)}) async-start(bf16[32,40,128]{2,1,0:T(8,128)(2,1)} %get-tuple-element.89), calls=%async_computation.1 | async-start | bytes 655360 | tf_op jit(solution)/shard_map/all_to_all | solution.py:631
  75.0 1.0 copy-start.22
  76.1 1.1 copy-start.29
  77.1 1.1 copy-start.31
  78.2 13.0 %copy-start.6 = (bf16[64,2304]{1,0:T(8,128)(2,1)S(1)}, bf16[64,2304]{1,0:T(8,128)(2,1)}, u32[]{:S(2)}) copy-start(bf16[64,2304]{1,0:T(8,128)(2,1)} %copy-done.4) | copy-start | bytes 884740
  78.2 13.0 %copy-start.14 = (bf16[1,16,256]{2,1,0:T(8,128)(2,1)S(1)}, bf16[1,16,256]{2,1,0:T(8,128)(2,1)}, u32[]{:S(2)}) copy-start(bf16[1,16,256]{2,1,0:T(8,128)(2,1)} %param.11) | copy-start | bytes 24580
  80.9 31.2 %copy-start.12 = (bf16[216,256]{1,0:T(8,128)(2,1)S(1)}, bf16[216,256]{1,0:T(8,128)(2,1)}, u32[]{:S(2)}) copy-start(bf16[216,256]{1,0:T(8,128)(2,1)} %copy-done.11) | copy-start | bytes 331780
  80.9 5.3 %collective-permute-start.6 = (bf16[80,128]{1,0:T(8,128)(2,1)S(1)}, bf16[80,128]{1,0:T(8,128)(2,1)S(1)}, u32[]{:S(2)}, u32[]{:S(2)}) collective-permute-start(bf16[80,128]{1,0:T(8,128)(2,1)S(1)} %get-tuple-element.86), channel_id=1, source_target_pairs={{0,124},{1,125},{2,126},{3,127},{4,0},{5,1},{6,2},{7,3},{8,4},{9,5... | collective-permute-start | bytes 61448 | tf_op jit(solution)/shard_map/ppermute | solution.py:552
  85.3 6.0 %collective-permute-start.7 = (bf16[80,128]{1,0:T(8,128)(2,1)S(1)}, bf16[80,128]{1,0:T(8,128)(2,1)S(1)}, u32[]{:S(2)}, u32[]{:S(2)}) collective-permute-start(bf16[80,128]{1,0:T(8,128)(2,1)S(1)} %get-tuple-element.87), channel_id=1, source_target_pairs={{0,4},{1,5},{2,6},{3,7},{4,8},{5,9},{6,10},{7,11},{8,12},{9,13},{1... | collective-permute-start | bytes 61448 | tf_op jit(solution)/shard_map/ppermute | solution.py:552
  92.7 12.0 %collective-permute-start.8 = (f32[8,256]{1,0:T(8,128)S(1)}, f32[8,256]{1,0:T(8,128)S(1)}, u32[]{:S(2)}, u32[]{:S(2)}) collective-permute-start(f32[8,256]{1,0:T(8,128)S(1)} %get-tuple-element.92), channel_id=1, source_target_pairs={{0,128},{128,0},{1,129},{129,1},{2,130},{130,2},{3,131},{131,3},{4... | collective-permute-start | bytes 24584 | tf_op jit(solution)/shard_map/ppermute | solution.py:651
  94.2 17.9 %all-to-all-start.2 = ((bf16[16,16,128]{2,1,0:T(8,128)(2,1)}), bf16[16,16,128]{2,1,0:T(8,128)(2,1)S(1)}, u32[]{:S(2)}, u32[]{:S(2)}) async-start(bf16[16,16,128]{2,1,0:T(8,128)(2,1)} %get-tuple-element.93), calls=%async_computation.2 | async-start | bytes 131072 | tf_op jit(solution)/shard_map/all_to_all | solution.py:644

commit v3 on v2

--- a/solution.py
+++ b/solution.py
@@ -19,6 +19,24 @@
 PADC = 128
 CHUNK = 24
 SHARE = 16
+DEPTH = FIELDS + COUPLED
+
+GIVE = 0
+TAKE = GIVE + LINE
+FIRST_W = TAKE + LINE
+OUT_BACK = FIRST_W + 9 * PADC
+BANK_ONE = OUT_BACK + 9 * PADC
+MID_W = 0
+MID_BACK = MID_W + 9 * HID
+MID_GATES = MID_BACK + 9 * HID
+FIRST_GATES = MID_GATES + 9 * 64
+OUT_GATES = FIRST_GATES + 5 * 64
+BANK_TWO = OUT_GATES + 9 * 16
+NARROW = 0
+FIRST_WIDE = NARROW + 9 * HID
+GIVE_OWN = FIRST_WIDE + 224
+OWN_GATES = GIVE_OWN + CELLS
+BANK_THREE = OWN_GATES + 32
 BF = jnp.bfloat16
 F32 = jnp.float32
 
@@ -133,24 +151,36 @@
             out_ref[col, line, :, 2 * depth : 3 * depth] = shift_cells(wide, -1, 0).astype(BF)
 
 
-def conv_tile(filled_ref, weights_ref, col):
+def take_strips(bank_ref, cells_ref):
+    total = None
+    for col in range(ROW):
+        block = slice(TAKE + CELLS * col, TAKE + CELLS * (col + 1))
+        piece = dot(bank_ref[block], cells_ref[CELLS * col : CELLS * (col + 1)])
+        total = piece if total is None else total + piece
+    return total.astype(BF)
+
+
+def conv_tile(filled_ref, bank_ref, base, col, lanes=slice(None)):
     width = filled_ref.shape[3]
     total = None
     for a in range(3):
-        piece = dot(filled_ref[col, a : a + TS].reshape(CELLS, width), weights_ref[a])
+        weights = bank_ref[base + width * a : base + width * (a + 1), lanes]
+        piece = dot(filled_ref[col, a : a + TS].reshape(CELLS, width), weights)
         total = piece if total is None else total + piece
     return total
 
 
-def fold_tile(grad, weights_ref, pad_ref):
+def fold_tile(grad, bank_ref, base, lanes, pad_ref):
     deep = grad.shape[1]
     lines = grad.reshape(TS, TS, deep)
     for a in range(3):
         pad_ref[a : a + TS, :, deep * a : deep * (a + 1)] = lines
-    total = dot(pad_ref[...].reshape((TS + 2) * TS, 3 * deep), weights_ref[...])
-    depth = total.shape[1] // 3
-    total = total.reshape(TS + 2, TS, 3 * depth)
-    left, mid, right = (total[:, :, depth * b : depth * (b + 1)] for b in range(3))
+    padded = pad_ref[...].reshape((TS + 2) * TS, 3 * deep)
+    left, mid, right = (
+        dot(padded, bank_ref[base + 3 * deep * b : base + 3 * deep * (b + 1), lanes]) for b in range(3)
+    )
+    depth = mid.shape[1]
+    left, mid, right = (part.reshape(TS + 2, TS, depth) for part in (left, mid, right))
     merged = mid + shift_cells(left, -1, 1) + shift_cells(right, 1, 1)
     inner = merged[1 : TS + 1].reshape(CELLS, depth)
     south = merged[0].astype(BF)
@@ -160,10 +190,10 @@
     return inner, south, north, west, east
 
 
-def fold_row(grad_of, weights_ref, pad_ref, inner_ref, prev_ref, next_ref, local_ref):
+def fold_row(grad_of, bank_ref, base, lanes, pad_ref, inner_ref, prev_ref, next_ref, local_ref):
     pad_ref[...] = jnp.zeros_like(pad_ref)
     for col in range(ROW):
-        inner, south, north, west, east = fold_tile(grad_of(col), weights_ref, pad_ref)
+        inner, south, north, west, east = fold_tile(grad_of(col), bank_ref, base, lanes, pad_ref)
         inner_ref[CELLS * col : CELLS * (col + 1)] = inner
         prev_ref[TS * col : TS * (col + 1)] = south
         next_ref[TS * col : TS * (col + 1)] = north
@@ -239,16 +269,16 @@
     return jnp.where(low | high, kernel, 0.0)
 
 
-def prepare_kernel(
-    turn_ref, first_gates_hbm, mid_gates_hbm, out_gates_hbm, first_hbm, mid_hbm, out_hbm,
-    take_ref, give_ref, first_w_ref, first_back_ref, mid_w_ref, mid_back_ref, out_w_ref, out_back_ref,
-    first_turned_ref, mid_turned_ref, out_turned_ref, first_wide_ref,
-    first_gates_ref, mid_gates_ref, out_gates_ref, first_ref, mid_ref, out_ref, sems,
+def prepare_early_kernel(
+    turn_hbm, first_gates_hbm, out_gates_hbm, first_hbm, out_hbm, bank_ref,
+    turn_ref, first_gates_ref, out_gates_ref, first_ref, out_ref, sems,
 ):
     copies = fetch(
-        (first_gates_hbm, mid_gates_hbm, out_gates_hbm, first_hbm, mid_hbm, out_hbm),
-        (first_gates_ref, mid_gates_ref, out_gates_ref, first_ref, mid_ref, out_ref), sems,
-    )
+        (turn_hbm, first_gates_hbm, out_gates_hbm, first_hbm, out_hbm),
+        (turn_ref, first_gates_ref, out_gates_ref, first_ref, out_ref), sems,
+    )
+    for copy in copies:
+        copy.wait()
     row = lax.axis_index(ROW_AXES)
     strip_of = lax.broadcasted_iota(jnp.int32, (8, 256), 1) >> 4
     along = lax.broadcasted_iota(jnp.int32, (8, 256), 1) & 15
@@ -263,41 +293,85 @@
         cells = jnp.where(strip_of == number, first + step * along, cells)
         place = lax.broadcasted_iota(jnp.int32, (TS, LINE), 1)
         wanted = first + step * lax.broadcasted_iota(jnp.int32, (TS, LINE), 0)
-        take_ref[TS * number : TS * (number + 1)] = (place == wanted).astype(F32).astype(BF)
-    give_ref[...] = one_hot((LINE, 256), 0, cells[0:1])
+        hit = (place == wanted).astype(F32).astype(BF)
+        for col in range(ROW):
+            at = TAKE + CELLS * col + TS * number
+            bank_ref[at : at + TS] = hit[:, CELLS * col : CELLS * (col + 1)]
+    bank_ref[GIVE : GIVE + LINE] = one_hot((LINE, 256), 0, cells[0:1])
+    count = 9 * DEPTH
+    wide = dot_tn(first_gates_ref[...].astype(F32).astype(BF), repeat_four(HID // 4, HID))
+    low, high = keep_of(wide, lax.broadcasted_iota(jnp.int32, (count, HID), 1) & 3)
+    kernel = jnp.where(low | high, first_ref[...].astype(F32), 0.0)
+    blank = jnp.zeros((PADC - DEPTH, HID), F32)
+    for tap in range(9):
+        block = jnp.concatenate([kernel[DEPTH * tap : DEPTH * (tap + 1)], blank], 0)
+        bank_ref[FIRST_W + PADC * tap : FIRST_W + PADC * (tap + 1)] = block.astype(BF)
+        cols = slice(HID * tap, HID * (tap + 1))
+        kernel_out = kept_rows(out_gates_ref[:, cols].astype(F32).astype(BF), out_ref[:, cols].astype(F32))
+        kernel_out = jnp.concatenate([kernel_out, jnp.zeros((PADC - FIELDS, HID), F32)], 0)
+        at = OUT_BACK + PADC * (3 * (tap % 3) + tap // 3)
+        bank_ref[at : at + PADC] = kernel_out.astype(BF)
+
+
+def prepare_late_kernel(
+    early_ref, first_gates_hbm, mid_gates_hbm, out_gates_hbm, mid_hbm, two_ref, three_ref,
+    first_gates_ref, mid_gates_ref, out_gates_ref, mid_ref, sems,
+):
+    copies = fetch(
+        (first_gates_hbm, mid_gates_hbm, out_gates_hbm, mid_hbm),
+        (first_gates_ref, mid_gates_ref, out_gates_ref, mid_ref), sems,
+    )
+    col = lax.axis_index(("xh", "core"))
+    tile = lax.axis_index(FACE)
+    three_ref[GIVE_OWN : GIVE_OWN + CELLS] = early_ref[pl.ds(pl.multiple_of(GIVE + CELLS * col, CELLS), CELLS)]
+    for a in range(3):
+        for b in range(3):
+            tap = 3 * a + b
+            block = early_ref[FIRST_W + PADC * tap : FIRST_W + PADC * (tap + 1)]
+            at = NARROW + HID * (3 * b + a)
+            three_ref[at : at + HID, :PADC] = dot_nt(eye(HID, HID), block).astype(BF)
+            at = OUT_BACK + PADC * (3 * b + a)
+            block = early_ref[at : at + PADC]
+            at = NARROW + HID * tap
+            three_ref[at : at + HID, PADC:] = dot_tn(block, eye(PADC, PADC)).astype(BF)
     for copy in copies:
         copy.wait()
-    depth = FIELDS + COUPLED
-    count = 9 * depth
+    count = 9 * DEPTH
     gates = first_gates_ref[...].astype(F32).astype(BF)
-    wide = dot_tn(gates, repeat_four(HID // 4, HID))
-    first_wide_ref[...] = wide.astype(BF)
-    low, high = keep_of(wide, lax.broadcasted_iota(jnp.int32, (count, HID), 1) & 3)
-    kernel = jnp.where(low | high, first_ref[...].astype(F32), 0.0)
-    blank = jnp.zeros((PADC - depth, HID), F32)
+    three_ref[FIRST_WIDE : FIRST_WIDE + count] = dot_tn(gates, repeat_four(HID // 4, HID)).astype(BF)
+    place = lax.broadcasted_iota(jnp.int32, (count, 9 * PADC), 0)
+    tap = (place * 2731) >> 16
+    spread = dot(gates, one_hot((count, 9 * PADC), 1, tap * PADC + place - DEPTH * tap)).astype(BF)
+    for b in range(4):
+        two_ref[FIRST_GATES + 64 * b : FIRST_GATES + 64 * (b + 1)] = spread[:, HID * b : HID * (b + 1)]
+    two_ref[FIRST_GATES + 256 : FIRST_GATES + 320, :PADC] = spread[:, 4 * HID :]
+    place = lax.broadcasted_iota(jnp.int32, (32, 9 * HID), 0)
+    mine = one_hot((32, 9 * HID), 1, jnp.where(place < 18, 18 * tile + place, -1))
+    gates = mid_gates_ref[...].astype(F32).astype(BF)
+    three_ref[OWN_GATES : OWN_GATES + 32, :64] = dot_nt(mine, gates).astype(BF)
+    out_gates = dot(eye(PADC, 4), out_gates_ref[...].astype(F32).astype(BF)).astype(BF)
+    three_ref[OWN_GATES : OWN_GATES + 32, PADC:] = dot_nt(mine, out_gates).astype(BF)
     for a in range(3):
         for b in range(3):
-            rows = slice(depth * (3 * a + b), depth * (3 * a + b + 1))
-            first_w_ref[a, PADC * b : PADC * (b + 1)] = jnp.concatenate([kernel[rows], blank], 0).astype(BF)
-        first_back_ref[HID * a : HID * (a + 1)] = dot_nt(eye(HID, HID), first_w_ref[a]).astype(BF)
-    place = lax.broadcasted_iota(jnp.int32, (count, 9 * PADC), 0)
-    tap = (place * 2731) >> 16
-    first_turned_ref[...] = dot(gates, one_hot((count, 9 * PADC), 1, tap * PADC + place - depth * tap)).astype(BF)
-    for a in range(3):
-        cols = slice(3 * HID * a, 3 * HID * (a + 1))
-        gates = mid_gates_ref[:, cols].astype(F32).astype(BF)
-        mid_turned_ref[:, cols] = gates
-        mid_back_ref[HID * a : HID * (a + 1)] = kept_rows(gates, dot_nt(eye(HID, HID), mid_ref[cols])).astype(BF)
-        mid_w_ref[a] = dot_tn(mid_back_ref[HID * a : HID * (a + 1)], eye(HID, HID)).astype(BF)
-        gates = out_gates_ref[:, cols].astype(F32).astype(BF)
-        out_turned_ref[:, cols] = dot(eye(8, 4), gates).astype(BF)
-        kernel = kept_rows(gates, out_ref[:, cols].astype(F32))
-        kernel = jnp.concatenate([kernel, jnp.zeros((PADC - FIELDS, 3 * HID), F32)], 0)
-        out_back_ref[PADC * a : PADC * (a + 1)] = kernel.astype(BF)
-        out_w_ref[a] = kernel.T.astype(BF)
-
-
-def start_kernel(line_ref, take_ref, field_ref, grad_ref, strips_ref):
+            tap = 3 * a + b
+            cols = slice(HID * tap, HID * (tap + 1))
+            two_ref[MID_GATES + 64 * tap : MID_GATES + 64 * (tap + 1)] = gates[:, cols]
+            turned = kept_rows(gates[:, cols], dot_nt(eye(HID, HID), mid_ref[cols])).astype(BF)
+            at = MID_BACK + HID * (3 * b + a)
+            two_ref[at : at + HID] = turned
+            at = MID_W + HID * tap
+            two_ref[at : at + HID] = dot_tn(turned, eye(HID, HID)).astype(BF)
+            two_ref[OUT_GATES + 16 * tap : OUT_GATES + 16 * (tap + 1)] = out_gates[:16, cols]
+
+
+def bank_gates(bank_ref, base, rows, blocks):
+    step = max(rows, 16)
+    return jnp.concatenate(
+        [bank_ref[base + step * b : base + step * (b + 1)][:rows] for b in blocks], 1
+    )
+
+
+def start_kernel(line_ref, bank_ref, field_ref, grad_ref, strips_ref):
     comp = lax.axis_index("comp")
     for col in range(ROW):
         own = line_ref[comp, col].astype(F32)
@@ -308,7 +382,7 @@
         blank = jnp.zeros((PADC - FIELDS, CELLS), F32)
         grad = jnp.concatenate([own[FIELDS:], blank], 0)
         grad_ref[CELLS * col : CELLS * (col + 1)] = grad.T.astype(BF)
-    strips_ref[...] = dot(take_ref[...], field_ref[...]).astype(BF)
+    strips_ref[...] = take_strips(bank_ref, field_ref)
 
 
 def send_strips(strips, up_ref, down_ref, local_ref):
@@ -322,24 +396,24 @@
 
 
 def layer_one_kernel(
-    field_ref, strips_ref, prev_ref, next_ref, grad_ref, first_ref, out_back_ref, take_ref,
+    field_ref, strips_ref, prev_ref, next_ref, grad_ref, bank_ref,
     filled_ref, act_ref, hid_ref, local_ref, up_ref, down_ref, inner_ref,
     pad_ref,
 ):
     fill(filled_ref, field_ref[...], strips_ref[LOCAL], prev_ref[...], next_ref[...])
     for col in range(ROW):
-        act = conv_tile(filled_ref, first_ref, col)
+        act = conv_tile(filled_ref, bank_ref, FIRST_W, col)
         act_ref[CELLS * col : CELLS * (col + 1)] = act
         hid_ref[CELLS * col : CELLS * (col + 1)] = (act * sigmoid(act)).astype(BF)
-    send_strips(dot(take_ref[...], hid_ref[...]).astype(BF), up_ref, down_ref, local_ref)
+    send_strips(take_strips(bank_ref, hid_ref), up_ref, down_ref, local_ref)
     fold_row(
         lambda col: grad_ref[CELLS * col : CELLS * (col + 1)],
-        out_back_ref, pad_ref, inner_ref, down_ref.at[80:160], up_ref.at[80:160], local_ref.at[96:192],
+        bank_ref, OUT_BACK, slice(None), pad_ref, inner_ref, down_ref.at[80:160], up_ref.at[80:160], local_ref.at[96:192],
     )
 
 
 def layer_two_kernel(
-    hid_ref, local_in_ref, prev_ref, next_ref, inner_two_ref, mid_ref, mid_back_ref, take_ref, give_ref,
+    hid_ref, local_in_ref, prev_ref, next_ref, inner_two_ref, early_ref, bank_ref,
     filled_ref, grad_ref, hid_two_ref, local_ref, up_ref, down_ref, inner_ref,
     pad_ref,
 ):
@@ -347,15 +421,15 @@
     strips = back_strips(prev_ref, next_ref, local_in_ref)
     for col in range(ROW):
         rows = slice(CELLS * col, CELLS * (col + 1))
-        grad_hid = inner_two_ref[rows] + dot(give_ref[rows], strips)
-        act = conv_tile(filled_ref, mid_ref, col)
+        grad_hid = inner_two_ref[rows] + dot(early_ref[rows], strips)
+        act = conv_tile(filled_ref, bank_ref, MID_W, col)
         sig = sigmoid(act)
         hid_two_ref[rows] = (act * sig).astype(BF)
         grad_ref[rows] = (grad_hid * (sig * (1.0 + act * (1.0 - sig)))).astype(BF)
-    send_strips(dot(take_ref[...], hid_two_ref[...]).astype(BF), up_ref, down_ref, local_ref)
+    send_strips(take_strips(early_ref, hid_two_ref), up_ref, down_ref, local_ref)
     fold_row(
         lambda col: grad_ref[CELLS * col : CELLS * (col + 1)],
-        mid_back_ref, pad_ref, inner_ref, down_ref.at[80:160], up_ref.at[80:160], local_ref.at[96:192],
+        bank_ref, MID_BACK, slice(None), pad_ref, inner_ref, down_ref.at[80:160], up_ref.at[80:160], local_ref.at[96:192],
     )
 
 
@@ -365,20 +439,22 @@
     )
 
 
-def term_pairs(filled_ref, grad, gates_ref, flat_ref):
+def term_pairs(filled_ref, grad, gates_of, flat_ref):
     turned = dot_nt(plane_order(), grad).astype(BF)
     width = filled_ref.shape[3]
     for a in range(3):
         cols = slice(width * a, width * (a + 1))
         term = dot(turned, gather_rows(filled_ref, a))
-        low, high = kept_pair([term[64 * m : 64 * (m + 1)] for m in range(4)], gates_ref[:, cols].astype(F32))
+        low, high = kept_pair([term[64 * m : 64 * (m + 1)] for m in range(4)], gates_of(a).astype(F32))
         flat_ref[0:64, cols] = low.astype(BF)
         flat_ref[64:128, cols] = high.astype(BF)
 
 
-def mid_term_kernel(filled_ref, grad_ref, gates_ref, part_ref, pick_out_ref, pick_first_ref, flat_ref):
+def mid_term_kernel(filled_ref, grad_ref, bank_ref, part_ref, pick_out_ref, pick_first_ref, flat_ref):
     col = lax.axis_index(("xh", "core"))
-    term_pairs(filled_ref, grad_ref[...], gates_ref, flat_ref)
+    term_pairs(
+        filled_ref, grad_ref[...], lambda a: bank_gates(bank_ref, MID_GATES, 64, range(3 * a, 3 * a + 3)), flat_ref
+    )
     shape = (16 * CHUNK, 1152)
     place = lax.broadcasted_iota(jnp.int32, shape, 0)
     block = (place * 2731) >> 16
@@ -402,16 +478,16 @@
 
 
 def terms_kernel(
-    hid_two_ref, local_ref, prev_ref, next_ref, inner_ref, act_ref, filled_zero_ref, grad_three_ref, give_ref,
-    part_ref, pick_out_ref, pick_first_ref, first_gates_ref, out_gates_ref,
-    buffer_ref, filled_ref, grad_ref,
-    flat_ref, flat_zero_ref,
+    hid_two_ref, local_ref, prev_ref, next_ref, inner_ref, act_ref, filled_zero_ref, grad_three_ref, early_ref, bank_ref,
+    part_ref, pick_out_ref, pick_first_ref,
+    buffer_ref, mine_ref, grad_ref,
+    filled_ref, flat_ref, flat_zero_ref,
 ):
     fill(filled_ref, hid_two_ref[...], local_ref[0:96], prev_ref[0:80], next_ref[0:80])
     strips = back_strips(prev_ref, next_ref, local_ref)
     for col in range(ROW):
         rows = slice(CELLS * col, CELLS * (col + 1))
-        grad_hid = inner_ref[rows] + dot(give_ref[rows], strips)
+        grad_hid = inner_ref[rows] + dot(early_ref[rows], strips)
         grad_ref[rows] = (grad_hid * slope(act_ref[rows])).astype(BF)
     place = lax.broadcasted_iota(jnp.int32, (32, PADC), 0)
     group = place & 7
@@ -421,18 +497,26 @@
     for a in range(3):
         cols = slice(width * a, width * (a + 1))
         term = dot(turned, gather_rows(filled_ref, a))
-        low, high = kept_pair([term[8 * m : 8 * (m + 1)] for m in range(4)], out_gates_ref[:, cols].astype(F32))
+        gates = bank_gates(bank_ref, OUT_GATES, 16, range(3 * a, 3 * a + 3)).astype(F32)[:8]
+        low, high = kept_pair([term[8 * m : 8 * (m + 1)] for m in range(4)], gates)
         pair = low + pltpu.roll(high, 4, 0)
         wide = jnp.broadcast_to(pair[None], (16, 8, width)).reshape(128, width)
         kernel_row = lax.broadcasted_iota(jnp.int32, (128, width), 1) + width * a
         slot = kernel_row - 9 * ((kernel_row * 7282) >> 16)
         mine = (lax.broadcasted_iota(jnp.int32, (128, width), 0) >> 3) == slot
         flat_ref[:, cols] = jnp.where(mine, wide, 0.0).astype(BF)
-    term_pairs(filled_zero_ref, grad_ref[...], first_gates_ref, flat_zero_ref)
+    gates = jnp.concatenate(
+        [bank_ref[FIRST_GATES + 64 * b : FIRST_GATES + 64 * (b + 1)] for b in range(4)]
+        + [bank_ref[FIRST_GATES + 256 : FIRST_GATES + 320, :PADC]], 1,
+    )
+    term_pairs(
+        filled_zero_ref, grad_ref[...], lambda a: gates[:, 3 * PADC * a : 3 * PADC * (a + 1)], flat_zero_ref
+    )
     for half in range(2):
         rows = slice(16 * CHUNK * half, 16 * CHUNK * (half + 1))
         part = part_ref[rows] + dot_nt(pick_out_ref[...], flat_ref[:, 1152 * half : 1152 * (half + 1)])
         buffer_ref[16 * half : 16 * (half + 1), 0:CHUNK] = part.astype(BF).reshape(16, CHUNK, PADC)
+    mine_ref[...] = filled_ref[lax.axis_index(("xh", "core"))]
     share = dot_nt(pick_first_ref[...], flat_zero_ref[...]).astype(BF)
     for place in range(ROWS):
         kind = place // 8
@@ -440,22 +524,22 @@
 
 
 def last_kernel(
-    filled_ref, grad_ref, out_ref, first_back_ref, state_ref, sea_ref,
+    mine_ref, grad_ref, bank_ref, state_ref, sea_ref,
     estimate_ref, dx_ref, up_ref, down_ref, local_ref,
     pad_ref, dx_all_ref,
 ):
     comp = lax.axis_index("comp")
     col = lax.axis_index(("xh", "core"))
-    width = filled_ref.shape[3]
+    width = mine_ref.shape[2]
     fold_row(
         lambda col: grad_ref[CELLS * col : CELLS * (col + 1)],
-        first_back_ref, pad_ref, dx_all_ref, down_ref, up_ref, local_ref,
+        bank_ref, NARROW, slice(0, PADC), pad_ref, dx_all_ref, down_ref, up_ref, local_ref,
     )
     dx_ref[...] = dx_all_ref[pl.ds(pl.multiple_of(col * CELLS, CELLS), CELLS)]
-    mine = filled_ref.at[col]
     total = None
     for a in range(3):
-        piece = dot(mine[a : a + TS].reshape(CELLS, width), out_ref[a])
+        weights = bank_ref[NARROW + width * a : NARROW + width * (a + 1), PADC:]
+        piece = dot(mine_ref[a : a + TS].reshape(CELLS, width), weights)
         total = piece if total is None else total + piece
     weight = jnp.where(comp == 1, sea_ref[...].astype(F32), 1.0)
     estimate_ref[...] = (state_ref[...].astype(F32) + weight * total.T[:FIELDS]).astype(BF)
@@ -472,21 +556,17 @@
 
 
 def finish_kernel(
-    dx_ref, next_ref, prev_ref, local_ref, give_ref, cot_ref, sum_ref, mid_gates_ref, out_gates_ref,
+    dx_ref, next_ref, prev_ref, local_ref, bank_ref, cot_ref, sum_ref,
     own_ref, send_ref, central_ref, closing_ref,
 ):
-    col = lax.axis_index(("xh", "core"))
-    give = give_ref[pl.ds(pl.multiple_of(col * CELLS, CELLS), CELLS)]
+    give = bank_ref[GIVE_OWN : GIVE_OWN + CELLS]
     strips = jnp.concatenate([next_ref[...], prev_ref[...], local_ref[...]], 0)
     total = (dx_ref[...] + dot(give, strips)).T
     own_ref[...] = cot_ref[...].astype(F32) + total[:FIELDS]
     send_ref[...] = total[FIELDS : FIELDS + COUPLED]
-    tile = lax.axis_index(FACE)
-    place = lax.broadcasted_iota(jnp.int32, (CHUNK, 9 * HID), 0)
-    mine = one_hot((CHUNK, 9 * HID), 1, jnp.where(place < 18, 18 * tile + place, -1))
     sums = sum_ref[...]
     repeat = repeat_four(HID // 4, HID)
-    wide = dot(dot_nt(mine, mid_gates_ref[...]).astype(BF), repeat)
+    wide = dot(bank_ref[OWN_GATES : OWN_GATES + 32, :64], repeat)[:CHUNK]
     low, high = keep_of(wide, lax.broadcasted_iota(jnp.int32, (CHUNK, HID), 1) & 3)
     lows, highs = dot_exact_right(sums[:, :64], repeat), dot_exact_right(sums[:, 64:], repeat)
     central = jnp.where(low, lows, jnp.where(high, highs, 0.0))
@@ -504,8 +584,8 @@
     group = (lax.broadcasted_iota(jnp.int32, (PADC, flat), 1) & 15) >> 2
     lows = dot_exact_right(spread, (from_lane == group).astype(F32).astype(BF))
     highs = dot_exact_right(spread, (from_lane == group + 4).astype(F32).astype(BF))
-    group = (lax.broadcasted_iota(jnp.int32, (8, flat), 1) & 15) >> 2
-    wide = dot(dot_nt(mine, out_gates_ref[...]).astype(BF), one_hot((8, flat), 0, group))
+    group = (lax.broadcasted_iota(jnp.int32, (PADC, flat), 1) & 15) >> 2
+    wide = dot(bank_ref[OWN_GATES : OWN_GATES + 32, PADC:], one_hot((PADC, flat), 0, group))[:CHUNK]
     lane = lax.broadcasted_iota(jnp.int32, (CHUNK, flat), 1)
     low, high = keep_of(wide, lane & 3)
     closing = jnp.where(low, lows, jnp.where(high, highs, 0.0))
@@ -513,14 +593,14 @@
     closing_ref[...] = jnp.sum(jnp.where(here, closing, 0.0), 0, keepdims=True)[:, : 18 * FIELDS]
 
 
-def opening_kernel(share_ref, wide_ref, out_ref):
+def opening_kernel(share_ref, bank_ref, out_ref):
     count = 9 * (FIELDS + COUPLED)
     wanted = lax.broadcasted_iota(jnp.int32, (count, 16 * SHARE), 0)
     block = (wanted * 4682) >> 16
     pick = one_hot((count, 16 * SHARE), 1, SHARE * block + wanted - 14 * block)
     pairs = dot(pick, share_ref[...]).astype(BF)
     repeat = repeat_four(HID // 4, HID)
-    low, high = keep_of(wide_ref[...].astype(F32), lax.broadcasted_iota(jnp.int32, (count, HID), 1) & 3)
+    low, high = keep_of(bank_ref[FIRST_WIDE : FIRST_WIDE + count].astype(F32), lax.broadcasted_iota(jnp.int32, (count, HID), 1) & 3)
     out_ref[...] = jnp.where(low, dot(pairs[:, :64], repeat), jnp.where(high, dot(pairs[:, 64:], repeat), 0.0))
 
 
@@ -530,6 +610,7 @@
 
 
 def call(body, out, args, scratch=(), scalars=(), far=(), flops=0, limit=10):
+    args = [pltpu.with_memory_space_constraint(arg, pltpu.HBM) if place in far else arg for place, arg in enumerate(args)]
     specs = [SMEM if place in scalars else HBM if place in far else VMEM for place in range(len(args))]
     size = sum(int(np.prod(item.shape)) * item.dtype.itemsize for item in list(args) + list(out))
     return pl.pallas_call(
@@ -556,7 +637,6 @@
     state, cotangent, land_sea, turn_table, first_kernel, mid_kernel, out_kernel, first_gates, mid_gates, out_gates
 ):
     sea = land_sea.reshape(1, CELLS)
-    depth = FIELDS + COUPLED
 
     packed = call(pack_kernel, [sds((8, 2 * FIELDS, CELLS), BF)], [state[0], cotangent[0], sea],
         scratch=[
@@ -567,39 +647,40 @@
     )[0]
     line = lax.all_to_all(packed, LINE_AXES, 0, 0).reshape(2, ROW, 2 * FIELDS, CELLS)
 
-    (
-        take, give, first_w, first_back, mid_w, mid_back, out_w, out_back, first_turned, mid_turned, out_turned,
-        first_wide,
-    ) = call(
-        prepare_kernel,
-        [
-            sds((256, LINE), BF), sds((LINE, 256), BF), sds((3, 3 * PADC, HID), BF), sds((3 * HID, 3 * PADC), BF),
-            sds((3, 3 * HID, HID), BF), sds((3 * HID, 3 * HID), BF), sds((3, 3 * HID, PADC), BF),
-            sds((3 * PADC, 3 * HID), BF), sds((64, 9 * PADC), BF), sds((64, 9 * HID), BF), sds((8, 9 * HID), BF),
-            sds((9 * depth, HID), BF),
+    turns, out_turned = turn_table.T, out_gates[0].T
+    first_turned, mid_turned = first_gates[0].T, mid_gates[0].T
+    early = call(
+        prepare_early_kernel, [sds((BANK_ONE, HID), BF)],
+        [turns, first_turned, out_turned, first_kernel[0], out_kernel[0].T],
+        scratch=[
+            pltpu.SMEM((4, TILES), jnp.int32), pltpu.VMEM((64, 9 * DEPTH), jnp.int32),
+            pltpu.VMEM((4, 9 * HID), jnp.int32), pltpu.VMEM((9 * DEPTH, HID), BF),
+            pltpu.VMEM((FIELDS, 9 * HID), BF), pltpu.SemaphoreType.DMA((5,)),
         ],
-        [turn_table.T, first_gates[0].T, mid_gates[0].T, out_gates[0].T, first_kernel[0], mid_kernel[0],
-         out_kernel[0].T],
-        scratch=[
-            pltpu.VMEM((64, 9 * depth), jnp.int32), pltpu.VMEM((64, 9 * HID), jnp.int32),
-            pltpu.VMEM((4, 9 * HID), jnp.int32), pltpu.VMEM((9 * depth, HID), BF), pltpu.VMEM((9 * HID, HID), BF),
-            pltpu.VMEM((FIELDS, 9 * HID), BF), pltpu.SemaphoreType.DMA((6,)),
-        ],
-        scalars=(0,), far=(1, 2, 3, 4, 5, 6), flops=5 * 10**9,
-    )
+        far=(0, 1, 2, 3, 4), flops=5 * 10**9,
+    )[0]
 
     field, grad_cells, strips_zero = call(
         start_kernel,
-        [sds((LINE, PADC), BF), sds((LINE, PADC), BF), sds((256, PADC), BF)], [line, take],
+        [sds((LINE, PADC), BF), sds((LINE, PADC), BF), sds((256, PADC), BF)], [line, early],
     )
     prev_zero = row_shift(strips_zero[UP], 1)
     next_zero = row_shift(strips_zero[DOWN], -1)
+    two, three = call(
+        prepare_late_kernel, [sds((BANK_TWO, HID), BF), sds((BANK_THREE, HID), BF)],
+        [early, first_turned, mid_turned, out_turned, mid_kernel[0]],
+        scratch=[
+            pltpu.VMEM((64, 9 * DEPTH), jnp.int32), pltpu.VMEM((64, 9 * HID), jnp.int32),
+            pltpu.VMEM((4, 9 * HID), jnp.int32), pltpu.VMEM((9 * HID, HID), BF), pltpu.SemaphoreType.DMA((4,)),
+        ],
+        far=(1, 2, 3, 4), flops=3 * 10**9,
+    )
 
     exchange = [sds((192, HID), BF), sds((160, HID), BF), sds((160, HID), BF), sds((LINE, HID), F32)]
     filled_zero, act_one, hid_one, local_one, up_one, down_one, inner_two = call(
         layer_one_kernel,
         [sds((ROW, TS + 2, TS, 3 * PADC), BF), sds((LINE, HID), F32), sds((LINE, HID), BF)] + exchange,
-        [field, strips_zero, prev_zero, next_zero, grad_cells, first_w, out_back, take],
+        [field, strips_zero, prev_zero, next_zero, grad_cells, early],
         scratch=[pltpu.VMEM((TS + 2, TS, 3 * PADC), BF)],
     )
     prev_one = row_shift(up_one, 1)
@@ -608,7 +689,7 @@
     filled_one, grad_two, hid_two, local_two, up_two, down_two, inner_one = call(
         layer_two_kernel,
         [sds((ROW, TS + 2, TS, 3 * HID), BF), sds((LINE, HID), BF), sds((LINE, HID), BF)] + exchange,
-        [hid_one, local_one, prev_one, next_one, inner_two, mid_w, mid_back, take, give],
+        [hid_one, local_one, prev_one, next_one, inner_two, early, two],
         scratch=[pltpu.VMEM((TS + 2, TS, 3 * HID), BF)],
     )
     prev_two = row_shift(up_two, 1)
@@ -617,16 +698,19 @@
     part, pick_out, pick_first = call(
         mid_term_kernel,
         [sds((32 * CHUNK, PADC), F32), sds((16 * CHUNK, 1152), BF), sds((4 * SHARE, 1152), BF)],
-        [filled_one, grad_two, mid_turned],
+        [filled_one, grad_two, two],
         scratch=[pltpu.VMEM((PADC, 9 * HID), BF)], flops=2 * 10**9,
     )
 
-    buffer, filled_two, grad_one = call(
+    buffer, mine_two, grad_one = call(
         terms_kernel,
-        [sds((ROWS, CHUNK + SHARE, PADC), BF), sds((ROW, TS + 2, TS, 3 * HID), BF), sds((LINE, HID), BF)],
-        [hid_two, local_two, prev_two, next_two, inner_one, act_one, filled_zero, grad_cells, give,
-         part, pick_out, pick_first, first_turned, out_turned],
-        scratch=[pltpu.VMEM((PADC, 9 * HID), BF), pltpu.VMEM((PADC, 9 * PADC), BF)],
+        [sds((ROWS, CHUNK + SHARE, PADC), BF), sds((TS + 2, TS, 3 * HID), BF), sds((LINE, HID), BF)],
+        [hid_two, local_two, prev_two, next_two, inner_one, act_one, filled_zero, grad_cells, early, two,
+         part, pick_out, pick_first],
+        scratch=[
+            pltpu.VMEM((ROW, TS + 2, TS, 3 * HID), BF), pltpu.VMEM((PADC, 9 * HID), BF),
+            pltpu.VMEM((PADC, 9 * PADC), BF),
+        ],
     )
     spread = lax.all_to_all(buffer, ROW_AXES, 0, 0)
 
@@ -634,7 +718,7 @@
         last_kernel,
         [sds((FIELDS, CELLS), BF), sds((CELLS, PADC), F32), sds((80, PADC), BF), sds((80, PADC), BF),
          sds((96, PADC), BF)],
-        [filled_two, grad_one, out_w, first_back, state[0], sea],
+        [mine_two, grad_one, three, state[0], sea],
         scratch=[pltpu.VMEM((TS + 2, TS, 3 * HID), BF), pltpu.VMEM((LINE, PADC), F32)], flops=2 * 10**9,
     )
     prev_three = row_shift(up_three, 1)
@@ -646,11 +730,11 @@
     own, send, central, closing = call(
         finish_kernel,
         [sds((FIELDS, CELLS), F32), sds((COUPLED, CELLS), F32), sds((1, 18 * HID), F32), sds((1, 18 * FIELDS), F32)],
-        [dx_own, next_three, prev_three, local_three, give, cotangent[0], summed, mid_turned, out_turned],
+        [dx_own, next_three, prev_three, local_three, three, cotangent[0], summed],
     )
     returned = lax.ppermute(send, "comp", [(0, 1), (1, 0)])
     adjoint = own + jnp.pad(returned, ((0, FIELDS - COUPLED), (0, 0)))
-    opening = call(opening_kernel, [sds((9 * depth, HID), F32)], [opened, first_wide])[0]
+    opening = call(opening_kernel, [sds((9 * DEPTH, HID), F32)], [opened, three])[0]
     return estimate[None], adjoint[None], opening[None], central, closing
 
 

time: 114 us -> 98.3 us (0.86)
  local copies, waits for them, and re-layouts: 20.5 us -> 1.38 us
  Pallas kernels: 25.4 us -> 29.8 us
  starting transfers between devices: 46 us -> 43.8 us
  waiting for transfers between devices: 19.8 us -> 21.5 us
    unnamed x64 -> x12, local copies, waits for them, and re-layouts: 20.5 us -> 1.38 us
    pallas_call x11 -> x12, Pallas kernels: 25.4 us -> 29.8 us  [call(): pl.pallas_call(body, out_shape=[jax.ShapeDtypeStruct(item.shape, item.dty...]
    all_to_all x1, waiting for transfers between devices: 0.01 us -> 3.52 us  [body(): lax.all_to_all(packed, LINE_AXES, 0, 0).reshape(2, ROW, 2 * FIELDS, CELLS)]
    ppermute x8, waiting for transfers between devices: 13.1 us -> 11.2 us  [row_shift(): return lax.ppermute(value, FACE, pairs)]
    ppermute x1, starting transfers between devices: 1.43 us -> 0.03 us  [body(): returned = lax.ppermute(send, 'comp', [(0, 1), (1, 0)])]
  transfers between devices with their start and end apart: 12 -> 12, of which waited for: 6 -> 6; matrix products, arithmetic and copies ran while one was open for 1% -> 1% of each run, Pallas kernels for 9% -> 14%
where the time goes in v3:
time: 98.3 us; the launch traced here: 97.8 us
  starting transfers between devices  43.8 us (45%)
  Pallas kernels  29.8 us (30%)
  waiting for transfers between devices  21.5 us (22%)
  local copies, waits for them, and re-layouts  1.38 us (1%)
    pallas_call x12, Pallas kernels, call(): pl.pallas_call(body, out_shape=[jax.ShapeDtypeStruct(item.shape, item.dty...  29.8 us
    ppermute x8, starting transfers between devices, row_shift(): return lax.ppermute(value, FACE, pairs)  21.6 us
    ppermute x8, waiting for transfers between devices, row_shift(): return lax.ppermute(value, FACE, pairs)  11.2 us
    all_to_all x1, starting transfers between devices, body(): lax.all_to_all(shared, ('y', 'xh', 'core'), 0, 0).reshape(16 * SHARE, PADC)  9.92 us
    all_to_all x1, waiting for transfers between devices, body(): lax.all_to_all(shared, ('y', 'xh', 'core'), 0, 0).reshape(16 * SHARE, PADC)  6.71 us
    all_to_all x1, starting transfers between devices, body(): lax.all_to_all(packed, LINE_AXES, 0, 0).reshape(2, ROW, 2 * FIELDS, CELLS)  6.49 us
    all_to_all x1, starting transfers between devices, body(): spread = lax.all_to_all(buffer, ROW_AXES, 0, 0)  5.72 us
    all_to_all x1, waiting for transfers between devices, body(): lax.all_to_all(packed, LINE_AXES, 0, 0).reshape(2, ROW, 2 * FIELDS, CELLS)  3.52 us
  transfers between devices with their start and end apart: 12, of which 6 were waited for; matrix products, arithmetic and copies ran while one was open for 1% of the time, Pallas kernels for 14%

profile of v3, /device:TPU:1, one launch (start us, length us, event | category | flops | bytes accessed | tf_op | source)
XLA Modules:
  0.0 97.8 jit_solution(5255580645641294821)
XLA Ops:
  0.6 1.4 %shard_map.137 = bf16[8,32,256]{2,1,0:T(8,128)(2,1)} custom-call(bf16[16,256]{1,0:T(8,128)(2,1)} %bitcast.28, bf16[16,256]{1,0:T(8,128)(2,1)} %bitcast.26, s32[1,256]{1,0:T(1,128)} %bitcast.30), custom_call_target="tpu_custom_call" | custom-call | bytes 148480 | tf_op jit(solution)/shard_map/pallas_call | solution.py:616
  2.0 6.5 %all-to-all-start = ((bf16[8,32,256]{2,1,0:T(8,128)(2,1)}), bf16[8,32,256]{2,1,0:T(8,128)(2,1)S(1)}, u32[]{:S(2)}, u32[]{:S(2)}) async-start(bf16[8,32,256]{2,1,0:T(8,128)(2,1)} %shard_map.137), calls=%async_computation | async-start | bytes 262144 | tf_op jit(solution)/shard_map/all_to_all | solution.py:648
  8.5 1.6 %shard_map.138.bank_ref.early_ref = bf16[4352,256]{1,0:T(8,128)(2,1)S(1)} custom-call(s32[4,128]{1,0:T(4,128)} %bitcast.41, s32[64,216]{1,0:T(8,128)} %bitcast.37, s32[4,2304]{1,0:T(4,128)} %bitcast.39, bf16[216,256]{1,0:T(8,128)(2,1)} %bitcast.35, bf16[16,2304]{1,0:T(8,128)(2,1)} %bitcast.36), custom_call_target="tpu_custom_call" | custom-call | flops 5000000000 | bytes 2506752 | tf_op jit(solution)/shard_map/pallas_call | solution.py:616
  10.2 3.5 %all-to-all-done = bf16[8,32,256]{2,1,0:T(8,128)(2,1)S(1)} async-done(((bf16[8,32,256]{2,1,0:T(8,128)(2,1)}), bf16[8,32,256]{2,1,0:T(8,128)(2,1)S(1)}, u32[]{:S(2)}, u32[]{:S(2)}) %all-to-all-start) | async-done | bytes 131104 | tf_op jit(solution)/shard_map/all_to_all | solution.py:648
  13.7 0.4 shard_map.139
  14.1 7.4 %collective-permute-start.1 = (bf16[80,128]{1,0:T(8,128)(2,1)S(1)}, bf16[80,128]{1,0:T(8,128)(2,1)S(1)}, u32[]{:S(2)}, u32[]{:S(2)}) collective-permute-start(bf16[80,128]{1,0:T(8,128)(2,1)S(1)} %get-tuple-element.77), channel_id=1, source_target_pairs={{0,124},{1,125},{2,126},{3,127},{4,0},{5,1},{6,2},{7,3},{8,4},{9,5... | collective-permute-start | bytes 61448 | tf_op jit(solution)/shard_map/ppermute | solution.py:633
  21.5 0.0 collective-permute-start
  21.5 0.9 collective-permute-done.1.next_ref
  22.4 5.0 %collective-permute-done.prev_ref = bf16[80,128]{1,0:T(8,128)(2,1)S(1)} collective-permute-done((bf16[80,128]{1,0:T(8,128)(2,1)S(1)}, bf16[80,128]{1,0:T(8,128)(2,1)S(1)}, u32[]{:S(2)}, u32[]{:S(2)}) %collective-permute-start) | collective-permute-done | bytes 20512 | tf_op jit(solution)/shard_map/ppermute | solution.py:633
  27.5 3.2 %shard_map.140 = (bf16[4,18,16,384]{3,2,1,0:T(8,128)(2,1)S(1)}, f32[1024,256]{1,0:T(8,128)S(1)}, bf16[1024,256]{1,0:T(8,128)(2,1)S(1)}, bf16[192,256]{1,0:T(8,12...) custom-call(bf16[1024,128]{1,0:T(8,128)(2,1)S(1)} %get-tuple-element.41.field_ref, ...), custom_call_target="tpu_custom_call" | custom-call | bytes 6627328 | tf_op jit(solution)/shard_map/pallas_call | solution.py:616
  30.7 0.0 collective-permute-start.2
  30.7 4.8 %collective-permute-start.3 = (bf16[160,256]{1,0:T(8,128)(2,1)S(1)}, bf16[160,256]{1,0:T(8,128)(2,1)S(1)}, u32[]{:S(2)}, u32[]{:S(2)}) collective-permute-start(bf16[160,256]{1,0:T(8,128)(2,1)S(1)} %get-tuple-element.47), channel_id=1, source_target_pairs={{0,124},{1,125},{2,126},{3,127},{4,0},{5,1},{6,2},{7,3},{8,4},{9,5... | collective-permute-start | bytes 245768 | tf_op jit(solution)/shard_map/ppermute | solution.py:633
  35.4 5.4 %shard_map.141 = (bf16[5648,256]{1,0:T(8,128)(2,1)S(1)}, bf16[2816,256]{1,0:T(8,128)(2,1)S(1)}) custom-call(bf16[4352,256]{1,0:T(8,128)(2,1)S(1)} %shard_map.138.bank_ref.early_ref, s32[64,216]{1,0:T(8,128)} %bitcast.38, s32[64,2304]{1,0:T(8,128)} %bitcast.34, s32[4,2304]{1,0:T(4,128)} %bitcast.40, bf16[2304,256]{1,0:T(8,128)(2,1)} %bitcast.33), custom_call_target="tpu_custom_call" | custom-call | flops 3000000000 | bytes 8423424 | tf_op jit(solution)/shard_map/pallas_call | solution.py:616
  40.8 0.0 copy-start
  40.8 0.0 collective-permute-done.2.prev_ref
  40.9 0.0 collective-permute-done.3.next_ref
  40.9 4.5 %shard_map.142 = (bf16[4,18,16,768]{3,2,1,0:T(8,128)(2,1)S(1)}, bf16[1024,256]{1,0:T(8,128)(2,1)S(1)}, bf16[1024,256]{1,0:T(8,128)(2,1)S(1)}, bf16[192,256]{1,0:...) custom-call(bf16[1024,256]{1,0:T(8,128)(2,1)S(1)} %get-tuple-element.44.hid_r, ...), custom_call_target="tpu_custom_call" | custom-call | bytes 11083776 | tf_op jit(solution)/shard_map/pallas_call | solution.py:616
  45.4 0.0 copy-done
  45.4 0.0 collective-permute-start.4
  45.4 4.8 %collective-permute-start.5 = (bf16[160,256]{1,0:T(8,128)(2,1)S(1)}, bf16[160,256]{1,0:T(8,128)(2,1)S(1)}, u32[]{:S(2)}, u32[]{:S(2)}) collective-permute-start(bf16[160,256]{1,0:T(8,128)(2,1)S(1)} %get-tuple-element.53), channel_id=1, source_target_pairs={{0,124},{1,125},{2,126},{3,127},{4,0},{5,1},{6,2},{7,3},{8,4},{9,5... | collective-permute-start | bytes 245768 | tf_op jit(solution)/shard_map/ppermute | solution.py:633
  50.2 2.5 %shard_map.143 = (f32[768,128]{1,0:T(8,128)S(1)}, bf16[384,1152]{1,0:T(8,128)(2,1)S(1)}, bf16[64,1152]{1,0:T(8,128)(2,1)S(1)}) custom-call(bf16[4,18,16,768]{3,2,1,0:T(8,128)(2,1)S(1)} %get-tuple-element.57.filled_ref, bf16[1024,256]{1,0:T(8,128)(2,1)S(1)} %get-tuple-element.58.grad_ref, bf16[5648,256]{1,0:T(8,128)(2,1)S(1)} %get-tuple-element.49.bank_ref), custom_call_target="tpu_custom_call" | custom-call | flops 2000000000 | bytes 6610944 | tf_op jit(solution)/shard_map/pallas_call | solution.py:616
  52.7 0.0 collective-permute-done.4.prev_ref
  52.7 0.0 collective-permute-done.5.next_ref
  52.7 0.0 copy-start.4
  52.7 0.0 copy-start.5
  52.7 4.1 %shard_map.144 = (bf16[32,40,128]{2,1,0:T(8,128)(2,1)}, bf16[18,16,768]{2,1,0:T(8,128)(2,1)S(1)}, bf16[1024,256]{1,0:T(8,128)(2,1)S(1)}) custom-call(bf16[1024,256]{1,0:T(8,128)(2,1)S(1)} %get-tuple-element.50.hid_two_ref, bf16[192,256]{1,0:T(8,128)(2,1)S(1)} %get-tuple-element.51.local_ref, bf16[160,256]{1,0:T(8,128)(2,1)S(1)} %collective-permute-done.4.prev_ref, ...), custom_call_target="tpu_custom_call" | custom-call | bytes 11870208 | tf_op jit(solution)/shard_map/pallas_call | solution.py:616
  56.8 5.7 %all-to-all-start.1 = ((bf16[32,40,128]{2,1,0:T(8,128)(2,1)}), bf16[32,40,128]{2,1,0:T(8,128)(2,1)S(1)}, u32[]{:S(2)}, u32[]{:S(2)}) async-start(bf16[32,40,128]{2,1,0:T(8,128)(2,1)} %get-tuple-element.70), calls=%async_computation.1 | async-start | bytes 655360 | tf_op jit(solution)/shard_map/all_to_all | solution.py:715
  62.5 0.0 copy-done.4
  62.6 0.0 copy-done.5
  62.6 0.0 copy-start.1
  62.6 1.4 %copy-done.1 = bf16[2816,256]{1,0:T(8,128)(2,1)S(1)} copy-done((bf16[2816,256]{1,0:T(8,128)(2,1)S(1)}, bf16[2816,256]{1,0:T(8,128)(2,1)}, u32[]{:S(2)}) %copy-start.1) | copy-done | bytes 1441816
  63.9 0.0 copy-start.2
  63.9 3.9 %shard_map.145 = (bf16[16,256]{1,0:T(8,128)(2,1)}, f32[256,128]{1,0:T(8,128)S(1)}, bf16[80,128]{1,0:T(8,128)(2,1)S(1)}, bf16[80,128]{1,0:T(8,128)(2,1)S(1)}, bf16[96,128]{1,0:T(8,128)(2,1)S(1)}) custom-call(bf16[18,16,768]{2,1,0:T(8,128)(2,1)S(1)} %get-tuple-element.62.mine_ref, bf16[1024,256]{1,0:T(8,128)(2,1)S(1)} %get-tuple-element.63.grad_ref, ...), custom_call_target="tpu_custom_call" | custom-call | flops 2000000000 | bytes 2622464 | tf_op jit(solution)/shard_map/pallas_call | solution.py:616
  67.8 4.6 %collective-permute-start.6 = (bf16[80,128]{1,0:T(8,128)(2,1)S(1)}, bf16[80,128]{1,0:T(8,128)(2,1)S(1)}, u32[]{:S(2)}, u32[]{:S(2)}) collective-permute-start(bf16[80,128]{1,0:T(8,128)(2,1)S(1)} %get-tuple-element.67), channel_id=1, source_target_pairs={{0,124},{1,125},{2,126},{3,127},{4,0},{5,1},{6,2},{7,3},{8,4},{9,5... | collective-permute-start | bytes 61448 | tf_op jit(solution)/shard_map/ppermute | solution.py:633
  72.4 0.0 collective-permute-start.7
  72.4 0.0 all-to-all-done.1.spread_ref
  72.5 0.7 shard_map.146
  73.1 0.2 collective-permute-done.6.next_ref
  73.3 5.0 %collective-permute-done.7.prev_ref = bf16[80,128]{1,0:T(8,128)(2,1)S(1)} collective-permute-done((bf16[80,128]{1,0:T(8,128)(2,1)S(1)}, bf16[80,128]{1,0:T(8,128)(2,1)S(1)}, u32[]{:S(2)}, u32[]{:S(2)}) %collective-permute-start.7) | collective-permute-done | bytes 20512 | tf_op jit(solution)/shard_map/ppermute | solution.py:633
  78.4 0.0 copy-done.2
  78.4 0.0 copy-done.3
  78.4 1.1 %shard_map.147 = (f32[16,256]{1,0:T(8,128)S(1)}, f32[8,256]{1,0:T(8,128)S(1)}, f32[1,4608]{1,0:T(1,128)}, f32[1,288]{1,0:T(1,128)}) custom-call(f32[256,128]{1,0:T(8,128)S(1)} %get-tuple-element.66.dx_ref, bf16[80,128]{1,0:T(8,128)(2,1)S(1)} %collective-permute-done.6.next_ref, bf16[80,128]{1,0:T(8,128)(2,1)S(1)} %collective-permute-done.7.prev_ref, ...), custom_call_target="tpu_custom_call" | custom-call | bytes 1703040 | tf_op jit(solution)/shard_map/pallas_call | solution.py:616
  79.5 0.0 collective-permute-start.8
  79.5 9.9 %all-to-all-start.2 = ((bf16[16,16,128]{2,1,0:T(8,128)(2,1)}), bf16[16,16,128]{2,1,0:T(8,128)(2,1)S(1)}, u32[]{:S(2)}, u32[]{:S(2)}) async-start(bf16[16,16,128]{2,1,0:T(8,128)(2,1)} %get-tuple-element.74), calls=%async_computation.2 | async-start | bytes 131072 | tf_op jit(solution)/shard_map/all_to_all | solution.py:728
  89.4 0.0 collective-permute-done.8
  89.4 0.6 add_bitcast_fusion
  90.0 6.7 %all-to-all-done.2 = bf16[16,16,128]{2,1,0:T(8,128)(2,1)S(1)} async-done(((bf16[16,16,128]{2,1,0:T(8,128)(2,1)}), bf16[16,16,128]{2,1,0:T(8,128)(2,1)S(1)}, u32[]{:S(2)}, u32[]{:S(2)}) %all-to-all-start.2) | async-done | bytes 65568 | tf_op jit(solution)/shard_map/all_to_all | solution.py:728
  96.7 1.1 %shard_map.148 = f32[216,256]{1,0:T(8,128)} custom-call(bf16[256,128]{1,0:T(8,128)(2,1)S(1)} %bitcast.25, bf16[2816,256]{1,0:T(8,128)(2,1)S(1)} %copy-done.2), custom_call_target="tpu_custom_call" | custom-call | bytes 1728512 | tf_op jit(solution)/shard_map/pallas_call | solution.py:616
  (2 shorter events, 0.0 us)
Async XLA Ops:
  2.0 11.6 %all-to-all-start = ((bf16[8,32,256]{2,1,0:T(8,128)(2,1)}), bf16[8,32,256]{2,1,0:T(8,128)(2,1)S(1)}, u32[]{:S(2)}, u32[]{:S(2)}) async-start(bf16[8,32,256]{2,1,0:T(8,128)(2,1)} %shard_map.137), calls=%async_computation | async-start | bytes 262144 | tf_op jit(solution)/shard_map/all_to_all | solution.py:648
  14.1 8.3 %collective-permute-start.1 = (bf16[80,128]{1,0:T(8,128)(2,1)S(1)}, bf16[80,128]{1,0:T(8,128)(2,1)S(1)}, u32[]{:S(2)}, u32[]{:S(2)}) collective-permute-start(bf16[80,128]{1,0:T(8,128)(2,1)S(1)} %get-tuple-element.77), channel_id=1, source_target_pairs={{0,124},{1,125},{2,126},{3,127},{4,0},{5,1},{6,2},{7,3},{8,4},{9,5... | collective-permute-start | bytes 61448 | tf_op jit(solution)/shard_map/ppermute | solution.py:633
  21.5 6.0 %collective-permute-start = (bf16[80,128]{1,0:T(8,128)(2,1)S(1)}, bf16[80,128]{1,0:T(8,128)(2,1)S(1)}, u32[]{:S(2)}, u32[]{:S(2)}) collective-permute-start(bf16[80,128]{1,0:T(8,128)(2,1)S(1)} %get-tuple-element.78), channel_id=1, source_target_pairs={{0,4},{1,5},{2,6},{3,7},{4,8},{5,9},{6,10},{7,11},{8,12},{9,13},{1... | collective-permute-start | bytes 61448 | tf_op jit(solution)/shard_map/ppermute | solution.py:633
  30.7 10.2 %collective-permute-start.2 = (bf16[160,256]{1,0:T(8,128)(2,1)S(1)}, bf16[160,256]{1,0:T(8,128)(2,1)S(1)}, u32[]{:S(2)}, u32[]{:S(2)}) collective-permute-start(bf16[160,256]{1,0:T(8,128)(2,1)S(1)} %get-tuple-element.46), channel_id=1, source_target_pairs={{0,4},{1,5},{2,6},{3,7},{4,8},{5,9},{6,10},{7,11},{8,12},{9,13},{1... | collective-permute-start | bytes 245768 | tf_op jit(solution)/shard_map/ppermute | solution.py:633
  30.7 10.2 %collective-permute-start.3 = (bf16[160,256]{1,0:T(8,128)(2,1)S(1)}, bf16[160,256]{1,0:T(8,128)(2,1)S(1)}, u32[]{:S(2)}, u32[]{:S(2)}) collective-permute-start(bf16[160,256]{1,0:T(8,128)(2,1)S(1)} %get-tuple-element.47), channel_id=1, source_target_pairs={{0,124},{1,125},{2,126},{3,127},{4,0},{5,1},{6,2},{7,3},{8,4},{9,5... | collective-permute-start | bytes 245768 | tf_op jit(solution)/shard_map/ppermute | solution.py:633
  40.8 4.5 %copy-start = (bf16[2816,256]{1,0:T(8,128)(2,1)}, bf16[2816,256]{1,0:T(8,128)(2,1)S(1)}, u32[]{:S(2)}) copy-start(bf16[2816,256]{1,0:T(8,128)(2,1)S(1)} %get-tuple-element.64.bank_ref) | copy-start | bytes 4325380
  45.4 7.3 %collective-permute-start.4 = (bf16[160,256]{1,0:T(8,128)(2,1)S(1)}, bf16[160,256]{1,0:T(8,128)(2,1)S(1)}, u32[]{:S(2)}, u32[]{:S(2)}) collective-permute-start(bf16[160,256]{1,0:T(8,128)(2,1)S(1)} %get-tuple-element.52), channel_id=1, source_target_pairs={{0,4},{1,5},{2,6},{3,7},{4,8},{5,9},{6,10},{7,11},{8,12},{9,13},{1... | collective-permute-start | bytes 245768 | tf_op jit(solution)/shard_map/ppermute | solution.py:633
  45.4 7.3 %collective-permute-start.5 = (bf16[160,256]{1,0:T(8,128)(2,1)S(1)}, bf16[160,256]{1,0:T(8,128)(2,1)S(1)}, u32[]{:S(2)}, u32[]{:S(2)}) collective-permute-start(bf16[160,256]{1,0:T(8,128)(2,1)S(1)} %get-tuple-element.53), channel_id=1, source_target_pairs={{0,124},{1,125},{2,126},{3,127},{4,0},{5,1},{6,2},{7,3},{8,4},{9,5... | collective-permute-start | bytes 245768 | tf_op jit(solution)/shard_map/ppermute | solution.py:633
  52.7 9.9 %copy-start.4 = (bf16[1,16,256]{2,1,0:T(8,128)(2,1)S(1)}, bf16[1,16,256]{2,1,0:T(8,128)(2,1)}, u32[]{:S(2)}) copy-start(bf16[1,16,256]{2,1,0:T(8,128)(2,1)} %param.10) | copy-start | bytes 24580
  52.7 9.9 %copy-start.5 = (s32[256]{0:T(256)S(1)}, s32[256]{0:T(256)}, u32[]{:S(2)}) copy-start(s32[256]{0:T(256)} %param.12) | copy-start | bytes 3076
  56.8 15.6 %all-to-all-start.1 = ((bf16[32,40,128]{2,1,0:T(8,128)(2,1)}), bf16[32,40,128]{2,1,0:T(8,128)(2,1)S(1)}, u32[]{:S(2)}, u32[]{:S(2)}) async-start(bf16[32,40,128]{2,1,0:T(8,128)(2,1)} %get-tuple-element.70), calls=%async_computation.1 | async-start | bytes 655360 | tf_op jit(solution)/shard_map/all_to_all | solution.py:715
  62.6 1.4 %copy-start.1 = (bf16[2816,256]{1,0:T(8,128)(2,1)S(1)}, bf16[2816,256]{1,0:T(8,128)(2,1)}, u32[]{:S(2)}) copy-start(bf16[2816,256]{1,0:T(8,128)(2,1)} %copy-done) | copy-start | bytes 4325380
  63.9 14.5 %copy-start.2 = (bf16[2816,256]{1,0:T(8,128)(2,1)S(1)}, bf16[2816,256]{1,0:T(8,128)(2,1)}, u32[]{:S(2)}) copy-start(bf16[2816,256]{1,0:T(8,128)(2,1)} %copy-done) | copy-start | bytes 4325380
  63.9 14.5 %copy-start.3 = (bf16[1,16,256]{2,1,0:T(8,128)(2,1)S(1)}, bf16[1,16,256]{2,1,0:T(8,128)(2,1)}, u32[]{:S(2)}) copy-start(bf16[1,16,256]{2,1,0:T(8,128)(2,1)} %param.11) | copy-start | bytes 24580
  67.8 5.5 %collective-permute-start.6 = (bf16[80,128]{1,0:T(8,128)(2,1)S(1)}, bf16[80,128]{1,0:T(8,128)(2,1)S(1)}, u32[]{:S(2)}, u32[]{:S(2)}) collective-permute-start(bf16[80,128]{1,0:T(8,128)(2,1)S(1)} %get-tuple-element.67), channel_id=1, source_target_pairs={{0,124},{1,125},{2,126},{3,127},{4,0},{5,1},{6,2},{7,3},{8,4},{9,5... | collective-permute-start | bytes 61448 | tf_op jit(solution)/shard_map/ppermute | solution.py:633
  72.4 6.0 %collective-permute-start.7 = (bf16[80,128]{1,0:T(8,128)(2,1)S(1)}, bf16[80,128]{1,0:T(8,128)(2,1)S(1)}, u32[]{:S(2)}, u32[]{:S(2)}) collective-permute-start(bf16[80,128]{1,0:T(8,128)(2,1)S(1)} %get-tuple-element.68), channel_id=1, source_target_pairs={{0,4},{1,5},{2,6},{3,7},{4,8},{5,9},{6,10},{7,11},{8,12},{9,13},{1... | collective-permute-start | bytes 61448 | tf_op jit(solution)/shard_map/ppermute | solution.py:633
  79.5 10.0 %collective-permute-start.8 = (f32[8,256]{1,0:T(8,128)S(1)}, f32[8,256]{1,0:T(8,128)S(1)}, u32[]{:S(2)}, u32[]{:S(2)}) collective-permute-start(f32[8,256]{1,0:T(8,128)S(1)} %get-tuple-element.73), channel_id=1, source_target_pairs={{0,128},{128,0},{1,129},{129,1},{2,130},{130,2},{3,131},{131,3},{4... | collective-permute-start | bytes 24584 | tf_op jit(solution)/shard_map/ppermute | solution.py:735
  79.5 17.3 %all-to-all-start.2 = ((bf16[16,16,128]{2,1,0:T(8,128)(2,1)}), bf16[16,16,128]{2,1,0:T(8,128)(2,1)S(1)}, u32[]{:S(2)}, u32[]{:S(2)}) async-start(bf16[16,16,128]{2,1,0:T(8,128)(2,1)} %get-tuple-element.74), calls=%async_computation.2 | async-start | bytes 131072 | tf_op jit(solution)/shard_map/all_to_all | solution.py:728

commit v4 on v3

--- a/solution.py
+++ b/solution.py
@@ -24,16 +24,16 @@
 GIVE = 0
 TAKE = GIVE + LINE
 FIRST_W = TAKE + LINE
-OUT_BACK = FIRST_W + 9 * PADC
-BANK_ONE = OUT_BACK + 9 * PADC
+OUT_BACK = FIRST_W + 3 * PADC
+MID_BACK = OUT_BACK + 3 * PADC
+MID_GATES = MID_BACK + 9 * HID
+BANK_ONE = MID_GATES + 9 * 64
 MID_W = 0
-MID_BACK = MID_W + 9 * HID
-MID_GATES = MID_BACK + 9 * HID
-FIRST_GATES = MID_GATES + 9 * 64
-OUT_GATES = FIRST_GATES + 5 * 64
+FIRST_GATES = MID_W + 9 * HID
+OUT_GATES = FIRST_GATES + 2 * 64
 BANK_TWO = OUT_GATES + 9 * 16
-NARROW = 0
-FIRST_WIDE = NARROW + 9 * HID
+LAST_W = 0
+FIRST_WIDE = LAST_W + 6 * PADC
 GIVE_OWN = FIRST_WIDE + 224
 OWN_GATES = GIVE_OWN + CELLS
 BANK_THREE = OWN_GATES + 32
@@ -110,18 +110,6 @@
     return (lax.broadcasted_iota(jnp.int32, shape, axis) == index).astype(F32).astype(BF)
 
 
-def edge_spread(column):
-    rows = lax.broadcasted_iota(jnp.int32, (CELLS, TS), 0)
-    cols = lax.broadcasted_iota(jnp.int32, (CELLS, TS), 1)
-    return (rows == cols * TS + column).astype(F32).astype(BF)
-
-
-def edge_take(column):
-    rows = lax.broadcasted_iota(jnp.int32, (TS, CELLS), 0)
-    cols = lax.broadcasted_iota(jnp.int32, (TS, CELLS), 1)
-    return (cols == rows * TS + column).astype(F32).astype(BF)
-
-
 def shift_cells(value, step, axis):
     along = lax.broadcasted_iota(jnp.int32, value.shape, axis)
     moved = pltpu.roll(value, step % TS, axis)
@@ -129,9 +117,15 @@
     return jnp.where(along == edge, 0.0, moved)
 
 
+def shift_lines(lines, step, strip):
+    along = lax.broadcasted_iota(jnp.int32, lines.shape, 1)
+    moved = pltpu.roll(lines, step % TS, 1)
+    edge = 0 if step == 1 else TS - 1
+    return jnp.where(along == edge, jnp.broadcast_to(strip.astype(F32)[:, None, :], lines.shape), moved)
+
+
 def fill(out_ref, tiles, local, from_prev, from_next):
     depth = tiles.shape[1]
-    spread_west, spread_east = edge_spread(0), edge_spread(TS - 1)
     for col in range(ROW):
         south = from_prev[TS * col : TS * (col + 1)]
         north = from_next[TS * col : TS * (col + 1)]
@@ -139,8 +133,8 @@
         east = from_next[4 * TS : 5 * TS] if col == 3 else local[TS * (3 + col) : TS * (4 + col)]
         own = tiles[CELLS * col : CELLS * (col + 1)]
         wide = own.astype(F32).reshape(TS, TS, depth)
-        left = shift_cells(wide, 1, 1) + dot(spread_west, west).reshape(TS, TS, depth)
-        right = shift_cells(wide, -1, 1) + dot(spread_east, east).reshape(TS, TS, depth)
+        left = shift_lines(wide, 1, west)
+        right = shift_lines(wide, -1, east)
         out_ref[col, 1 : TS + 1, :, 0:depth] = left.astype(BF)
         out_ref[col, 1 : TS + 1, :, depth : 2 * depth] = own.reshape(TS, TS, depth)
         out_ref[col, 1 : TS + 1, :, 2 * depth : 3 * depth] = right.astype(BF)
@@ -151,6 +145,25 @@
             out_ref[col, line, :, 2 * depth : 3 * depth] = shift_cells(wide, -1, 0).astype(BF)
 
 
+def fill_packed(out_ref, tiles, local, from_prev, from_next):
+    def choose(left, own, right):
+        lane = lax.broadcasted_iota(jnp.int32, own.shape, own.ndim - 1)
+        return jnp.where(lane < 32, left, jnp.where(lane < 64, own, right)).astype(BF)
+
+    for col in range(ROW):
+        south = from_prev[TS * col : TS * (col + 1)]
+        north = from_next[TS * col : TS * (col + 1)]
+        west = from_prev[4 * TS : 5 * TS] if col == 0 else local[TS * (col - 1) : TS * col]
+        east = from_next[4 * TS : 5 * TS] if col == 3 else local[TS * (3 + col) : TS * (4 + col)]
+        wide = tiles[CELLS * col : CELLS * (col + 1)].astype(F32).reshape(TS, TS, PADC)
+        left = shift_lines(wide, 1, west)
+        right = shift_lines(wide, -1, east)
+        out_ref[col, 1 : TS + 1] = choose(left, wide, right)
+        for line, strip in ((0, south), (TS + 1, north)):
+            wide = strip.astype(F32)
+            out_ref[col, line] = choose(shift_cells(wide, 1, 0), wide, shift_cells(wide, -1, 0))
+
+
 def take_strips(bank_ref, cells_ref):
     total = None
     for col in range(ROW):
@@ -170,14 +183,29 @@
     return total
 
 
-def fold_tile(grad, bank_ref, base, lanes, pad_ref):
+def pad_lines(grad, pad_ref):
     deep = grad.shape[1]
     lines = grad.reshape(TS, TS, deep)
     for a in range(3):
         pad_ref[a : a + TS, :, deep * a : deep * (a + 1)] = lines
-    padded = pad_ref[...].reshape((TS + 2) * TS, 3 * deep)
+    return pad_ref[...].reshape((TS + 2) * TS, 3 * deep)
+
+
+def pad_lines_packed(grad):
+    lines = grad.astype(F32).reshape(TS, TS, PADC)
+    blank = jnp.zeros((1, TS, PADC), F32)
+    lane = lax.broadcasted_iota(jnp.int32, (TS + 2, TS, PADC), 2)
+    one, two, three = (
+        jnp.concatenate([blank] * a + [lines] + [blank] * (2 - a), 0) for a in range(3)
+    )
+    padded = jnp.where(lane < 16, one, jnp.where(lane < 32, two, three))
+    return padded.reshape((TS + 2) * TS, PADC).astype(BF)
+
+
+def fold_tile(padded, bank_ref, base, lanes):
+    deep = padded.shape[1]
     left, mid, right = (
-        dot(padded, bank_ref[base + 3 * deep * b : base + 3 * deep * (b + 1), lanes]) for b in range(3)
+        dot(padded, bank_ref[base + deep * b : base + deep * (b + 1), lanes]) for b in range(3)
     )
     depth = mid.shape[1]
     left, mid, right = (part.reshape(TS + 2, TS, depth) for part in (left, mid, right))
@@ -185,15 +213,14 @@
     inner = merged[1 : TS + 1].reshape(CELLS, depth)
     south = merged[0].astype(BF)
     north = merged[TS + 1].astype(BF)
-    west = dot(edge_take(0), left[1 : TS + 1].reshape(CELLS, depth).astype(BF)).astype(BF)
-    east = dot(edge_take(TS - 1), right[1 : TS + 1].reshape(CELLS, depth).astype(BF)).astype(BF)
+    west = left[1 : TS + 1, 0, :].astype(BF)
+    east = right[1 : TS + 1, TS - 1, :].astype(BF)
     return inner, south, north, west, east
 
 
-def fold_row(grad_of, bank_ref, base, lanes, pad_ref, inner_ref, prev_ref, next_ref, local_ref):
-    pad_ref[...] = jnp.zeros_like(pad_ref)
+def fold_row(padded_of, bank_ref, base, lanes, inner_ref, prev_ref, next_ref, local_ref):
     for col in range(ROW):
-        inner, south, north, west, east = fold_tile(grad_of(col), bank_ref, base, lanes, pad_ref)
+        inner, south, north, west, east = fold_tile(padded_of(col), bank_ref, base, lanes)
         inner_ref[CELLS * col : CELLS * (col + 1)] = inner
         prev_ref[TS * col : TS * (col + 1)] = south
         next_ref[TS * col : TS * (col + 1)] = north
@@ -264,21 +291,22 @@
 def kept_rows(gates, kernel):
     outputs = kernel.shape[0]
     rows = lax.broadcasted_iota(jnp.int32, (outputs, outputs // 4), 0) >> 2
-    wide = dot(one_hot((outputs, outputs // 4), 1, rows), gates)
-    low, high = keep_of(wide, lax.broadcasted_iota(jnp.int32, wide.shape, 0) & 3)
-    return jnp.where(low | high, kernel, 0.0)
+    repeat = one_hot((outputs, outputs // 4), 1, rows)
+    low = jnp.where(gates >= 4.5, 2.0, jnp.where(gates >= 2.5, 1.0, 0.0)).astype(BF)
+    high = jnp.where(gates < 0.5, 1.0, jnp.where((gates < 1.5) | ((gates > 2.5) & (gates < 3.5)), 2.0, 3.0)).astype(BF)
+    lane = (lax.broadcasted_iota(jnp.int32, kernel.shape, 0) & 3).astype(F32)
+    return jnp.where((dot(repeat, low) == lane) | (dot(repeat, high) == lane), kernel, 0.0)
 
 
 def prepare_early_kernel(
-    turn_hbm, first_gates_hbm, out_gates_hbm, first_hbm, out_hbm, bank_ref,
-    turn_ref, first_gates_ref, out_gates_ref, first_ref, out_ref, sems,
+    turn_hbm, first_gates_hbm, out_gates_hbm, first_hbm, out_hbm, mid_gates_hbm, mid_hbm, bank_ref,
+    turn_ref, first_gates_ref, out_gates_ref, first_ref, out_ref, mid_gates_ref, mid_ref, sems,
 ):
     copies = fetch(
-        (turn_hbm, first_gates_hbm, out_gates_hbm, first_hbm, out_hbm),
-        (turn_ref, first_gates_ref, out_gates_ref, first_ref, out_ref), sems,
-    )
-    for copy in copies:
-        copy.wait()
+        (turn_hbm, first_gates_hbm, out_gates_hbm, first_hbm, out_hbm, mid_gates_hbm, mid_hbm),
+        (turn_ref, first_gates_ref, out_gates_ref, first_ref, out_ref, mid_gates_ref, mid_ref), sems,
+    )
+    copies[0].wait()
     row = lax.axis_index(ROW_AXES)
     strip_of = lax.broadcasted_iota(jnp.int32, (8, 256), 1) >> 4
     along = lax.broadcasted_iota(jnp.int32, (8, 256), 1) & 15
@@ -298,70 +326,70 @@
             at = TAKE + CELLS * col + TS * number
             bank_ref[at : at + TS] = hit[:, CELLS * col : CELLS * (col + 1)]
     bank_ref[GIVE : GIVE + LINE] = one_hot((LINE, 256), 0, cells[0:1])
+    for copy in copies[1:]:
+        copy.wait()
     count = 9 * DEPTH
     wide = dot_tn(first_gates_ref[...].astype(F32).astype(BF), repeat_four(HID // 4, HID))
     low, high = keep_of(wide, lax.broadcasted_iota(jnp.int32, (count, HID), 1) & 3)
     kernel = jnp.where(low | high, first_ref[...].astype(F32), 0.0)
-    blank = jnp.zeros((PADC - DEPTH, HID), F32)
+    blank = jnp.zeros((32 - DEPTH, HID), F32)
+    kernel_out = kept_rows(out_gates_ref[...].astype(F32), out_ref[...].astype(F32)).astype(BF)
+    for a in range(3):
+        pieces = []
+        for b in range(3):
+            tap = 3 * a + b
+            pieces += [kernel[DEPTH * tap : DEPTH * (tap + 1)], blank]
+            at = OUT_BACK + PADC * b + FIELDS * a
+            bank_ref[at : at + FIELDS] = kernel_out[:, HID * tap : HID * (tap + 1)]
+        pieces.append(jnp.zeros((32, HID), F32))
+        bank_ref[FIRST_W + PADC * a : FIRST_W + PADC * (a + 1)] = jnp.concatenate(pieces, 0).astype(BF)
+        bank_ref[OUT_BACK + PADC * a + 48 : OUT_BACK + PADC * (a + 1)] = jnp.zeros((PADC - 48, HID), BF)
     for tap in range(9):
-        block = jnp.concatenate([kernel[DEPTH * tap : DEPTH * (tap + 1)], blank], 0)
-        bank_ref[FIRST_W + PADC * tap : FIRST_W + PADC * (tap + 1)] = block.astype(BF)
         cols = slice(HID * tap, HID * (tap + 1))
-        kernel_out = kept_rows(out_gates_ref[:, cols].astype(F32).astype(BF), out_ref[:, cols].astype(F32))
-        kernel_out = jnp.concatenate([kernel_out, jnp.zeros((PADC - FIELDS, HID), F32)], 0)
-        at = OUT_BACK + PADC * (3 * (tap % 3) + tap // 3)
-        bank_ref[at : at + PADC] = kernel_out.astype(BF)
-
-
-def prepare_late_kernel(
-    early_ref, first_gates_hbm, mid_gates_hbm, out_gates_hbm, mid_hbm, two_ref, three_ref,
-    first_gates_ref, mid_gates_ref, out_gates_ref, mid_ref, sems,
-):
-    copies = fetch(
-        (first_gates_hbm, mid_gates_hbm, out_gates_hbm, mid_hbm),
-        (first_gates_ref, mid_gates_ref, out_gates_ref, mid_ref), sems,
-    )
+        gates = mid_gates_ref[:, cols].astype(F32)
+        bank_ref[MID_GATES + 64 * tap : MID_GATES + 64 * (tap + 1)] = gates.astype(BF)
+        at = MID_BACK + HID * (3 * (tap % 3) + tap // 3)
+        bank_ref[at : at + HID] = kept_rows(gates, dot_nt(eye(HID, HID), mid_ref[cols])).astype(BF)
+
+
+def prepare_late_kernel(early_ref, first_gates_hbm, out_gates_hbm, two_ref, first_gates_ref, out_gates_ref, sems):
+    copies = fetch((first_gates_hbm, out_gates_hbm), (first_gates_ref, out_gates_ref), sems)
+    for a in range(3):
+        for b in range(3):
+            at = MID_BACK + HID * (3 * b + a)
+            to = MID_W + HID * (3 * a + b)
+            two_ref[to : to + HID] = dot_tn(early_ref[at : at + HID], eye(HID, HID)).astype(BF)
+    for copy in copies:
+        copy.wait()
+    count = 9 * DEPTH
+    place = lax.broadcasted_iota(jnp.int32, (count, 3 * PADC), 0)
+    tap = (place * 2731) >> 16
+    third = (tap * 11) >> 5
+    target = PADC * third + 32 * (tap - 3 * third) + place - DEPTH * tap
+    gates = first_gates_ref[...].astype(F32).astype(BF)
+    spread = dot(gates, one_hot((count, 3 * PADC), 1, target)).astype(BF)
+    two_ref[FIRST_GATES : FIRST_GATES + 64] = spread[:, :HID]
+    two_ref[FIRST_GATES + 64 : FIRST_GATES + 128, :PADC] = spread[:, HID:]
+    gates = dot(eye(16, 4), out_gates_ref[...].astype(F32).astype(BF)).astype(BF)
+    for tap in range(9):
+        two_ref[OUT_GATES + 16 * tap : OUT_GATES + 16 * (tap + 1)] = gates[:, HID * tap : HID * (tap + 1)]
+
+
+def prepare_last_kernel(early_ref, first_gates_ref, out_gates_ref, act_ref, three_ref, slope_ref):
+    slope_ref[...] = slope(act_ref[...])
     col = lax.axis_index(("xh", "core"))
     tile = lax.axis_index(FACE)
     three_ref[GIVE_OWN : GIVE_OWN + CELLS] = early_ref[pl.ds(pl.multiple_of(GIVE + CELLS * col, CELLS), CELLS)]
-    for a in range(3):
-        for b in range(3):
-            tap = 3 * a + b
-            block = early_ref[FIRST_W + PADC * tap : FIRST_W + PADC * (tap + 1)]
-            at = NARROW + HID * (3 * b + a)
-            three_ref[at : at + HID, :PADC] = dot_nt(eye(HID, HID), block).astype(BF)
-            at = OUT_BACK + PADC * (3 * b + a)
-            block = early_ref[at : at + PADC]
-            at = NARROW + HID * tap
-            three_ref[at : at + HID, PADC:] = dot_tn(block, eye(PADC, PADC)).astype(BF)
-    for copy in copies:
-        copy.wait()
+    three_ref[LAST_W : LAST_W + 6 * PADC] = early_ref[FIRST_W : FIRST_W + 6 * PADC]
     count = 9 * DEPTH
     gates = first_gates_ref[...].astype(F32).astype(BF)
     three_ref[FIRST_WIDE : FIRST_WIDE + count] = dot_tn(gates, repeat_four(HID // 4, HID)).astype(BF)
-    place = lax.broadcasted_iota(jnp.int32, (count, 9 * PADC), 0)
-    tap = (place * 2731) >> 16
-    spread = dot(gates, one_hot((count, 9 * PADC), 1, tap * PADC + place - DEPTH * tap)).astype(BF)
-    for b in range(4):
-        two_ref[FIRST_GATES + 64 * b : FIRST_GATES + 64 * (b + 1)] = spread[:, HID * b : HID * (b + 1)]
-    two_ref[FIRST_GATES + 256 : FIRST_GATES + 320, :PADC] = spread[:, 4 * HID :]
     place = lax.broadcasted_iota(jnp.int32, (32, 9 * HID), 0)
     mine = one_hot((32, 9 * HID), 1, jnp.where(place < 18, 18 * tile + place, -1))
-    gates = mid_gates_ref[...].astype(F32).astype(BF)
+    gates = bank_gates(early_ref, MID_GATES, 64, range(9))
     three_ref[OWN_GATES : OWN_GATES + 32, :64] = dot_nt(mine, gates).astype(BF)
-    out_gates = dot(eye(PADC, 4), out_gates_ref[...].astype(F32).astype(BF)).astype(BF)
-    three_ref[OWN_GATES : OWN_GATES + 32, PADC:] = dot_nt(mine, out_gates).astype(BF)
-    for a in range(3):
-        for b in range(3):
-            tap = 3 * a + b
-            cols = slice(HID * tap, HID * (tap + 1))
-            two_ref[MID_GATES + 64 * tap : MID_GATES + 64 * (tap + 1)] = gates[:, cols]
-            turned = kept_rows(gates[:, cols], dot_nt(eye(HID, HID), mid_ref[cols])).astype(BF)
-            at = MID_BACK + HID * (3 * b + a)
-            two_ref[at : at + HID] = turned
-            at = MID_W + HID * tap
-            two_ref[at : at + HID] = dot_tn(turned, eye(HID, HID)).astype(BF)
-            two_ref[OUT_GATES + 16 * tap : OUT_GATES + 16 * (tap + 1)] = out_gates[:16, cols]
+    gates = dot(eye(PADC, 4), out_gates_ref[...].astype(F32).astype(BF)).astype(BF)
+    three_ref[OWN_GATES : OWN_GATES + 32, PADC:] = dot_nt(mine, gates).astype(BF)
 
 
 def bank_gates(bank_ref, base, rows, blocks):
@@ -376,11 +404,10 @@
     for col in range(ROW):
         own = line_ref[comp, col].astype(F32)
         other = line_ref[1 - comp, col][:FIELDS].astype(F32)[:COUPLED]
-        blank = jnp.zeros((PADC - FIELDS - COUPLED, CELLS), F32)
-        field = jnp.concatenate([own[:FIELDS], other, blank], 0)
+        blank = jnp.zeros((32 - DEPTH, CELLS), F32)
+        field = jnp.concatenate([own[:FIELDS], other, blank] * 3 + [jnp.zeros((32, CELLS), F32)], 0)
         field_ref[CELLS * col : CELLS * (col + 1)] = field.T.astype(BF)
-        blank = jnp.zeros((PADC - FIELDS, CELLS), F32)
-        grad = jnp.concatenate([own[FIELDS:], blank], 0)
+        grad = jnp.concatenate([own[FIELDS:]] * 3 + [jnp.zeros((PADC - 3 * FIELDS, CELLS), F32)], 0)
         grad_ref[CELLS * col : CELLS * (col + 1)] = grad.T.astype(BF)
     strips_ref[...] = take_strips(bank_ref, field_ref)
 
@@ -398,17 +425,16 @@
 def layer_one_kernel(
     field_ref, strips_ref, prev_ref, next_ref, grad_ref, bank_ref,
     filled_ref, act_ref, hid_ref, local_ref, up_ref, down_ref, inner_ref,
-    pad_ref,
 ):
-    fill(filled_ref, field_ref[...], strips_ref[LOCAL], prev_ref[...], next_ref[...])
+    fill_packed(filled_ref, field_ref[...], strips_ref[LOCAL], prev_ref[...], next_ref[...])
     for col in range(ROW):
         act = conv_tile(filled_ref, bank_ref, FIRST_W, col)
         act_ref[CELLS * col : CELLS * (col + 1)] = act
         hid_ref[CELLS * col : CELLS * (col + 1)] = (act * sigmoid(act)).astype(BF)
     send_strips(take_strips(bank_ref, hid_ref), up_ref, down_ref, local_ref)
     fold_row(
-        lambda col: grad_ref[CELLS * col : CELLS * (col + 1)],
-        bank_ref, OUT_BACK, slice(None), pad_ref, inner_ref, down_ref.at[80:160], up_ref.at[80:160], local_ref.at[96:192],
+        lambda col: pad_lines_packed(grad_ref[CELLS * col : CELLS * (col + 1)]),
+        bank_ref, OUT_BACK, slice(None), inner_ref, down_ref.at[80:160], up_ref.at[80:160], local_ref.at[96:192],
     )
 
 
@@ -427,9 +453,10 @@
         hid_two_ref[rows] = (act * sig).astype(BF)
         grad_ref[rows] = (grad_hid * (sig * (1.0 + act * (1.0 - sig)))).astype(BF)
     send_strips(take_strips(early_ref, hid_two_ref), up_ref, down_ref, local_ref)
+    pad_ref[...] = jnp.zeros_like(pad_ref)
     fold_row(
-        lambda col: grad_ref[CELLS * col : CELLS * (col + 1)],
-        bank_ref, MID_BACK, slice(None), pad_ref, inner_ref, down_ref.at[80:160], up_ref.at[80:160], local_ref.at[96:192],
+        lambda col: pad_lines(grad_ref[CELLS * col : CELLS * (col + 1)], pad_ref),
+        early_ref, MID_BACK, slice(None), inner_ref, down_ref.at[80:160], up_ref.at[80:160], local_ref.at[96:192],
     )
 
 
@@ -450,10 +477,10 @@
         flat_ref[64:128, cols] = high.astype(BF)
 
 
-def mid_term_kernel(filled_ref, grad_ref, bank_ref, part_ref, pick_out_ref, pick_first_ref, flat_ref):
+def mid_term_kernel(filled_ref, grad_ref, early_ref, part_ref, pick_out_ref, pick_first_ref, flat_ref):
     col = lax.axis_index(("xh", "core"))
     term_pairs(
-        filled_ref, grad_ref[...], lambda a: bank_gates(bank_ref, MID_GATES, 64, range(3 * a, 3 * a + 3)), flat_ref
+        filled_ref, grad_ref[...], lambda a: bank_gates(early_ref, MID_GATES, 64, range(3 * a, 3 * a + 3)), flat_ref
     )
     shape = (16 * CHUNK, 1152)
     place = lax.broadcasted_iota(jnp.int32, shape, 0)
@@ -463,13 +490,14 @@
     pick = ((ahead == inside) & (inside < 18)).astype(F32).astype(BF)
     late = ahead - 9 * (inside - 18)
     pick_out_ref[...] = ((late >= 0) & (late < 9) & (inside >= 18) & (inside < 20)).astype(F32).astype(BF)
-    shape = (4 * SHARE, 1152)
+    shape = (4 * SHARE, 3 * PADC)
     place = lax.broadcasted_iota(jnp.int32, shape, 0)
     inside = place & 15
     wanted = 14 * (4 * (place >> 4) + col) + inside
     tap = (wanted * 2731) >> 16
-    target = tap * PADC + wanted - (FIELDS + COUPLED) * tap
-    real = (inside < 14) & (wanted < 9 * (FIELDS + COUPLED))
+    third = (tap * 11) >> 5
+    target = PADC * third + 32 * (tap - 3 * third) + wanted - DEPTH * tap
+    real = (inside < 14) & (wanted < 9 * DEPTH)
     pick_first_ref[...] = ((lax.broadcasted_iota(jnp.int32, shape, 1) == target) & real).astype(F32).astype(BF)
     for half in range(2):
         part_ref[16 * CHUNK * half : 16 * CHUNK * (half + 1)] = dot_nt(
@@ -478,17 +506,19 @@
 
 
 def terms_kernel(
-    hid_two_ref, local_ref, prev_ref, next_ref, inner_ref, act_ref, filled_zero_ref, grad_three_ref, early_ref, bank_ref,
+    hid_two_ref, local_ref, prev_ref, next_ref, inner_ref, slope_ref, filled_zero_ref, grad_three_ref, early_ref, bank_ref,
     part_ref, pick_out_ref, pick_first_ref,
-    buffer_ref, mine_ref, grad_ref,
-    filled_ref, flat_ref, flat_zero_ref,
+    buffer_ref, mine_hbm, grad_ref,
+    filled_ref, flat_ref, flat_zero_ref, sem,
 ):
     fill(filled_ref, hid_two_ref[...], local_ref[0:96], prev_ref[0:80], next_ref[0:80])
+    keep = pltpu.make_async_copy(filled_ref.at[lax.axis_index(("xh", "core"))], mine_hbm, sem)
+    keep.start()
     strips = back_strips(prev_ref, next_ref, local_ref)
     for col in range(ROW):
         rows = slice(CELLS * col, CELLS * (col + 1))
         grad_hid = inner_ref[rows] + dot(early_ref[rows], strips)
-        grad_ref[rows] = (grad_hid * slope(act_ref[rows])).astype(BF)
+        grad_ref[rows] = (grad_hid * slope_ref[rows]).astype(BF)
     place = lax.broadcasted_iota(jnp.int32, (32, PADC), 0)
     group = place & 7
     wanted = jnp.where(group < 4, 4 * group + (place >> 3), -1)
@@ -505,40 +535,49 @@
         slot = kernel_row - 9 * ((kernel_row * 7282) >> 16)
         mine = (lax.broadcasted_iota(jnp.int32, (128, width), 0) >> 3) == slot
         flat_ref[:, cols] = jnp.where(mine, wide, 0.0).astype(BF)
-    gates = jnp.concatenate(
-        [bank_ref[FIRST_GATES + 64 * b : FIRST_GATES + 64 * (b + 1)] for b in range(4)]
-        + [bank_ref[FIRST_GATES + 256 : FIRST_GATES + 320, :PADC]], 1,
-    )
-    term_pairs(
-        filled_zero_ref, grad_ref[...], lambda a: gates[:, 3 * PADC * a : 3 * PADC * (a + 1)], flat_zero_ref
-    )
+    gates = [
+        bank_ref[FIRST_GATES : FIRST_GATES + 64, :PADC], bank_ref[FIRST_GATES : FIRST_GATES + 64, PADC:],
+        bank_ref[FIRST_GATES + 64 : FIRST_GATES + 128, :PADC],
+    ]
+    term_pairs(filled_zero_ref, grad_ref[...], lambda a: gates[a], flat_zero_ref)
     for half in range(2):
         rows = slice(16 * CHUNK * half, 16 * CHUNK * (half + 1))
         part = part_ref[rows] + dot_nt(pick_out_ref[...], flat_ref[:, 1152 * half : 1152 * (half + 1)])
         buffer_ref[16 * half : 16 * (half + 1), 0:CHUNK] = part.astype(BF).reshape(16, CHUNK, PADC)
-    mine_ref[...] = filled_ref[lax.axis_index(("xh", "core"))]
     share = dot_nt(pick_first_ref[...], flat_zero_ref[...]).astype(BF)
     for place in range(ROWS):
         kind = place // 8
         buffer_ref[place, CHUNK : CHUNK + SHARE] = share[SHARE * kind : SHARE * (kind + 1)]
+    keep.wait()
 
 
 def last_kernel(
     mine_ref, grad_ref, bank_ref, state_ref, sea_ref,
     estimate_ref, dx_ref, up_ref, down_ref, local_ref,
-    pad_ref, dx_all_ref,
+    pad_ref, dx_all_ref, narrow_ref,
 ):
+    for a in range(3):
+        for b in range(3):
+            at = LAST_W + PADC * a + 32 * b
+            block = jnp.concatenate([bank_ref[at : at + 32], jnp.zeros((PADC - 32, HID), BF)], 0)
+            to = HID * (3 * b + a)
+            narrow_ref[to : to + HID, :PADC] = dot_nt(eye(HID, HID), block).astype(BF)
+            at = LAST_W + PADC * (3 + b) + FIELDS * a
+            block = jnp.concatenate([bank_ref[at : at + FIELDS], jnp.zeros((PADC - FIELDS, HID), BF)], 0)
+            to = HID * (3 * a + b)
+            narrow_ref[to : to + HID, PADC:] = dot_tn(block, eye(PADC, PADC)).astype(BF)
     comp = lax.axis_index("comp")
     col = lax.axis_index(("xh", "core"))
     width = mine_ref.shape[2]
+    pad_ref[...] = jnp.zeros_like(pad_ref)
     fold_row(
-        lambda col: grad_ref[CELLS * col : CELLS * (col + 1)],
-        bank_ref, NARROW, slice(0, PADC), pad_ref, dx_all_ref, down_ref, up_ref, local_ref,
+        lambda col: pad_lines(grad_ref[CELLS * col : CELLS * (col + 1)], pad_ref),
+        narrow_ref, 0, slice(0, PADC), dx_all_ref, down_ref, up_ref, local_ref,
     )
     dx_ref[...] = dx_all_ref[pl.ds(pl.multiple_of(col * CELLS, CELLS), CELLS)]
     total = None
     for a in range(3):
-        weights = bank_ref[NARROW + width * a : NARROW + width * (a + 1), PADC:]
+        weights = narrow_ref[width * a : width * (a + 1), PADC:]
         piece = dot(mine_ref[a : a + TS].reshape(CELLS, width), weights)
         total = piece if total is None else total + piece
     weight = jnp.where(comp == 1, sea_ref[...].astype(F32), 1.0)
@@ -609,7 +648,7 @@
 HBM = pl.BlockSpec(memory_space=pltpu.HBM)
 
 
-def call(body, out, args, scratch=(), scalars=(), far=(), flops=0, limit=10):
+def call(body, out, args, scratch=(), scalars=(), far=(), far_out=(), flops=0, limit=10):
     args = [pltpu.with_memory_space_constraint(arg, pltpu.HBM) if place in far else arg for place, arg in enumerate(args)]
     specs = [SMEM if place in scalars else HBM if place in far else VMEM for place in range(len(args))]
     size = sum(int(np.prod(item.shape)) * item.dtype.itemsize for item in list(args) + list(out))
@@ -617,7 +656,7 @@
         body,
         out_shape=[jax.ShapeDtypeStruct(item.shape, item.dtype) for item in out],
         in_specs=specs,
-        out_specs=[VMEM] * len(out),
+        out_specs=[HBM if place in far_out else VMEM for place in range(len(out))],
         scratch_shapes=list(scratch),
         compiler_params=pltpu.CompilerParams(vmem_limit_bytes=limit * 1024 * 1024),
         cost_estimate=pl.CostEstimate(flops=flops, bytes_accessed=size, transcendentals=0),
@@ -651,13 +690,14 @@
     first_turned, mid_turned = first_gates[0].T, mid_gates[0].T
     early = call(
         prepare_early_kernel, [sds((BANK_ONE, HID), BF)],
-        [turns, first_turned, out_turned, first_kernel[0], out_kernel[0].T],
+        [turns, first_turned, out_turned, first_kernel[0], out_kernel[0].T, mid_turned, mid_kernel[0]],
         scratch=[
             pltpu.SMEM((4, TILES), jnp.int32), pltpu.VMEM((64, 9 * DEPTH), jnp.int32),
             pltpu.VMEM((4, 9 * HID), jnp.int32), pltpu.VMEM((9 * DEPTH, HID), BF),
-            pltpu.VMEM((FIELDS, 9 * HID), BF), pltpu.SemaphoreType.DMA((5,)),
+            pltpu.VMEM((FIELDS, 9 * HID), BF), pltpu.VMEM((64, 9 * HID), jnp.int32),
+            pltpu.VMEM((9 * HID, HID), BF), pltpu.SemaphoreType.DMA((7,)),
         ],
-        far=(0, 1, 2, 3, 4), flops=5 * 10**9,
+        far=(0, 1, 2, 3, 4, 5, 6), flops=5 * 10**9,
     )[0]
 
     field, grad_cells, strips_zero = call(
@@ -666,25 +706,27 @@
     )
     prev_zero = row_shift(strips_zero[UP], 1)
     next_zero = row_shift(strips_zero[DOWN], -1)
-    two, three = call(
-        prepare_late_kernel, [sds((BANK_TWO, HID), BF), sds((BANK_THREE, HID), BF)],
-        [early, first_turned, mid_turned, out_turned, mid_kernel[0]],
+    two = call(
+        prepare_late_kernel, [sds((BANK_TWO, HID), BF)], [early, first_turned, out_turned],
         scratch=[
-            pltpu.VMEM((64, 9 * DEPTH), jnp.int32), pltpu.VMEM((64, 9 * HID), jnp.int32),
-            pltpu.VMEM((4, 9 * HID), jnp.int32), pltpu.VMEM((9 * HID, HID), BF), pltpu.SemaphoreType.DMA((4,)),
+            pltpu.VMEM((64, 9 * DEPTH), jnp.int32), pltpu.VMEM((4, 9 * HID), jnp.int32),
+            pltpu.SemaphoreType.DMA((2,)),
         ],
-        far=(1, 2, 3, 4), flops=3 * 10**9,
-    )
-
+        far=(1, 2), flops=10**9,
+    )[0]
     exchange = [sds((192, HID), BF), sds((160, HID), BF), sds((160, HID), BF), sds((LINE, HID), F32)]
     filled_zero, act_one, hid_one, local_one, up_one, down_one, inner_two = call(
         layer_one_kernel,
-        [sds((ROW, TS + 2, TS, 3 * PADC), BF), sds((LINE, HID), F32), sds((LINE, HID), BF)] + exchange,
+        [sds((ROW, TS + 2, TS, PADC), BF), sds((LINE, HID), F32), sds((LINE, HID), BF)] + exchange,
         [field, strips_zero, prev_zero, next_zero, grad_cells, early],
-        scratch=[pltpu.VMEM((TS + 2, TS, 3 * PADC), BF)],
     )
     prev_one = row_shift(up_one, 1)
     next_one = row_shift(down_one, -1)
+
+    three, slope_one = call(
+        prepare_last_kernel, [sds((BANK_THREE, HID), BF), sds((LINE, HID), F32)],
+        [early, first_turned, out_turned, act_one], flops=10**9,
+    )
 
     filled_one, grad_two, hid_two, local_two, up_two, down_two, inner_one = call(
         layer_two_kernel,
@@ -697,20 +739,21 @@
 
     part, pick_out, pick_first = call(
         mid_term_kernel,
-        [sds((32 * CHUNK, PADC), F32), sds((16 * CHUNK, 1152), BF), sds((4 * SHARE, 1152), BF)],
-        [filled_one, grad_two, two],
+        [sds((32 * CHUNK, PADC), F32), sds((16 * CHUNK, 1152), BF), sds((4 * SHARE, 3 * PADC), BF)],
+        [filled_one, grad_two, early],
         scratch=[pltpu.VMEM((PADC, 9 * HID), BF)], flops=2 * 10**9,
     )
 
     buffer, mine_two, grad_one = call(
         terms_kernel,
         [sds((ROWS, CHUNK + SHARE, PADC), BF), sds((TS + 2, TS, 3 * HID), BF), sds((LINE, HID), BF)],
-        [hid_two, local_two, prev_two, next_two, inner_one, act_one, filled_zero, grad_cells, early, two,
+        [hid_two, local_two, prev_two, next_two, inner_one, slope_one, filled_zero, grad_cells, early, two,
          part, pick_out, pick_first],
         scratch=[
             pltpu.VMEM((ROW, TS + 2, TS, 3 * HID), BF), pltpu.VMEM((PADC, 9 * HID), BF),
-            pltpu.VMEM((PADC, 9 * PADC), BF),
+            pltpu.VMEM((PADC, 3 * PADC), BF), pltpu.SemaphoreType.DMA,
         ],
+        far_out=(1,),
     )
     spread = lax.all_to_all(buffer, ROW_AXES, 0, 0)
 
@@ -719,7 +762,11 @@
         [sds((FIELDS, CELLS), BF), sds((CELLS, PADC), F32), sds((80, PADC), BF), sds((80, PADC), BF),
          sds((96, PADC), BF)],
         [mine_two, grad_one, three, state[0], sea],
-        scratch=[pltpu.VMEM((TS + 2, TS, 3 * HID), BF), pltpu.VMEM((LINE, PADC), F32)], flops=2 * 10**9,
+        scratch=[
+            pltpu.VMEM((TS + 2, TS, 3 * HID), BF), pltpu.VMEM((LINE, PADC), F32),
+            pltpu.VMEM((9 * HID, HID), BF),
+        ],
+        flops=2 * 10**9,
     )
     prev_three = row_shift(up_three, 1)
     next_three = row_shift(down_three, -1)

time: 98.3 us -> 88.1 us (0.90)
  waiting for transfers between devices: 21.5 us -> 14.2 us
  Pallas kernels: 29.8 us -> 23.9 us
  local copies, waits for them, and re-layouts: 1.38 us -> 3.76 us
    ppermute x8, waiting for transfers between devices: 11.2 us -> 5.13 us  [row_shift(): return lax.ppermute(value, FACE, pairs)]
    pallas_call x12 -> x13, Pallas kernels: 29.8 us -> 23.9 us  [call(): pl.pallas_call(body, out_shape=[jax.ShapeDtypeStruct(item.shape, item.dty...]
    unnamed x12 -> x20, local copies, waits for them, and re-layouts: 1.38 us -> 3.76 us
    all_to_all x1, waiting for transfers between devices: 3.52 us -> 2.16 us  [body(): lax.all_to_all(packed, LINE_AXES, 0, 0).reshape(2, ROW, 2 * FIELDS, CELLS)]
  transfers between devices with their start and end apart: 12 -> 12, of which waited for: 6 -> 5; matrix products, arithmetic and copies ran while one was open for 1% -> 1% of each run, Pallas kernels for 14% -> 13%
where the time goes in v4:
time: 88.1 us; the launch traced here: 87.6 us
  starting transfers between devices  44.3 us (50%)
  Pallas kernels  23.9 us (27%)
  waiting for transfers between devices  14.2 us (16%)
  local copies, waits for them, and re-layouts  3.76 us (4%)
    pallas_call x13, Pallas kernels, call(): pl.pallas_call(body, out_shape=[jax.ShapeDtypeStruct(item.shape, item.dty...  23.9 us
    ppermute x8, starting transfers between devices, row_shift(): return lax.ppermute(value, FACE, pairs)  22.1 us
    all_to_all x1, starting transfers between devices, body(): lax.all_to_all(shared, ('y', 'xh', 'core'), 0, 0).reshape(16 * SHARE, PADC)  9.94 us
    all_to_all x1, waiting for transfers between devices, body(): lax.all_to_all(shared, ('y', 'xh', 'core'), 0, 0).reshape(16 * SHARE, PADC)  6.71 us
    all_to_all x1, starting transfers between devices, body(): lax.all_to_all(packed, LINE_AXES, 0, 0).reshape(2, ROW, 2 * FIELDS, CELLS)  6.49 us
    all_to_all x1, starting transfers between devices, body(): spread = lax.all_to_all(buffer, ROW_AXES, 0, 0)  5.76 us
    ppermute x8, waiting for transfers between devices, row_shift(): return lax.ppermute(value, FACE, pairs)  5.13 us
    unnamed x20, local copies, waits for them, and re-layouts  3.76 us
  transfers between devices with their start and end apart: 12, of which 5 were waited for; matrix products, arithmetic and copies ran while one was open for 1% of the time, Pallas kernels for 13%

profile of v4, /device:TPU:1, one launch (start us, length us, event | category | flops | bytes accessed | tf_op | source)
XLA Modules:
  0.0 87.6 jit_solution(2316307709669684900)
XLA Ops:
  0.6 1.4 %shard_map.137 = bf16[8,32,256]{2,1,0:T(8,128)(2,1)} custom-call(bf16[16,256]{1,0:T(8,128)(2,1)} %bitcast.34, bf16[16,256]{1,0:T(8,128)(2,1)} %bitcast.32, s32[1,256]{1,0:T(1,128)} %bitcast.36), custom_call_target="tpu_custom_call" | custom-call | bytes 148480 | tf_op jit(solution)/shard_map/pallas_call | solution.py:655
  2.0 6.5 %all-to-all-start = ((bf16[8,32,256]{2,1,0:T(8,128)(2,1)}), bf16[8,32,256]{2,1,0:T(8,128)(2,1)S(1)}, u32[]{:S(2)}, u32[]{:S(2)}) async-start(bf16[8,32,256]{2,1,0:T(8,128)(2,1)} %shard_map.137), calls=%async_computation | async-start | bytes 262144 | tf_op jit(solution)/shard_map/all_to_all | solution.py:687
  8.5 3.0 %shard_map.138.bank_ref.early_ref = bf16[5696,256]{1,0:T(8,128)(2,1)S(1)} custom-call(s32[4,128]{1,0:T(4,128)} %bitcast.43, s32[64,216]{1,0:T(8,128)} %bitcast.25, s32[4,2304]{1,0:T(4,128)} %bitcast.29, bf16[216,256]{1,0:T(8,128)(2,1)} %bitcast.41, bf16[16,2304]{1,0:T(8,128)(2,1)} %bitcast.42, s32[64,2304]{1,0:T(8,128)} %bitcast.40, bf16[2304,256]{1,0:T(8,128)(2,1)} %bitcast.39), custom_call_target="tpu_custom_call" | custom-call | flops 5000000000 | bytes 4964352 | tf_op jit(solution)/shard_map/pallas_call | solution.py:655
  11.5 2.2 %all-to-all-done = bf16[8,32,256]{2,1,0:T(8,128)(2,1)S(1)} async-done(((bf16[8,32,256]{2,1,0:T(8,128)(2,1)}), bf16[8,32,256]{2,1,0:T(8,128)(2,1)S(1)}, u32[]{:S(2)}, u32[]{:S(2)}) %all-to-all-start) | async-done | bytes 131104 | tf_op jit(solution)/shard_map/all_to_all | solution.py:687
  13.7 0.4 shard_map.139
  14.1 1.0 %collective-permute-start = (bf16[80,128]{1,0:T(8,128)(2,1)S(1)}, bf16[80,128]{1,0:T(8,128)(2,1)S(1)}, u32[]{:S(2)}, u32[]{:S(2)}) collective-permute-start(bf16[80,128]{1,0:T(8,128)(2,1)S(1)} %get-tuple-element.78), channel_id=1, source_target_pairs={{0,4},{1,5},{2,6},{3,7},{4,8},{5,9},{6,10},{7,11},{8,12},{9,13},{1... | collective-permute-start | bytes 61448 | tf_op jit(solution)/shard_map/ppermute | solution.py:672
  15.1 6.5 %collective-permute-start.1 = (bf16[80,128]{1,0:T(8,128)(2,1)S(1)}, bf16[80,128]{1,0:T(8,128)(2,1)S(1)}, u32[]{:S(2)}, u32[]{:S(2)}) collective-permute-start(bf16[80,128]{1,0:T(8,128)(2,1)S(1)} %get-tuple-element.77), channel_id=1, source_target_pairs={{0,124},{1,125},{2,126},{3,127},{4,0},{5,1},{6,2},{7,3},{8,4},{9,5... | collective-permute-start | bytes 61448 | tf_op jit(solution)/shard_map/ppermute | solution.py:672
  21.6 1.1 %shard_map.141.bank_ref = bf16[2576,256]{1,0:T(8,128)(2,1)S(1)} custom-call(bf16[5696,256]{1,0:T(8,128)(2,1)S(1)} %shard_map.138.bank_ref.early_ref, s32[64,216]{1,0:T(8,128)} %bitcast.26, s32[4,2304]{1,0:T(4,128)} %bitcast.30), custom_call_target="tpu_custom_call" | custom-call | flops 1000000000 | bytes 4327424 | tf_op jit(solution)/shard_map/pallas_call | solution.py:655
  22.8 0.0 collective-permute-done.prev_ref
  22.8 0.0 collective-permute-done.1.next_ref
  22.8 0.0 copy-start.3
  22.8 0.0 copy-start.4
  22.8 1.3 %shard_map.140 = (bf16[4,18,16,128]{3,2,1,0:T(8,128)(2,1)S(1)}, f32[1024,256]{1,0:T(8,128)S(1)}, bf16[1024,256]{1,0:T(8,128)(2,1)S(1)}, bf16[192,256]{1,0:T(8,12...) custom-call(bf16[1024,128]{1,0:T(8,128)(2,1)S(1)} %get-tuple-element.41.field_ref, ...), custom_call_target="tpu_custom_call" | custom-call | bytes 6725632 | tf_op jit(solution)/shard_map/pallas_call | solution.py:655
  24.1 0.1 collective-permute-start.2
  24.2 4.8 %collective-permute-start.3 = (bf16[160,256]{1,0:T(8,128)(2,1)S(1)}, bf16[160,256]{1,0:T(8,128)(2,1)S(1)}, u32[]{:S(2)}, u32[]{:S(2)}) collective-permute-start(bf16[160,256]{1,0:T(8,128)(2,1)S(1)} %get-tuple-element.47), channel_id=1, source_target_pairs={{0,124},{1,125},{2,126},{3,127},{4,0},{5,1},{6,2},{7,3},{8,4},{9,5... | collective-permute-start | bytes 245768 | tf_op jit(solution)/shard_map/ppermute | solution.py:672
  29.0 0.0 copy-done.3
  29.0 0.0 copy-done.4
  29.0 1.1 %shard_map.143 = (bf16[1280,256]{1,0:T(8,128)(2,1)S(1)}, f32[1024,256]{1,0:T(8,128)S(1)}) custom-call(bf16[5696,256]{1,0:T(8,128)(2,1)S(1)} %shard_map.138.bank_ref.early_ref, s32[64,216]{1,0:T(8,128)S(1)} %bitcast.27, s32[4,2304]{1,0:T(4,128)S(1)} %bitcast.31, f32[1024,256]{1,0:T(8,128)S(1)} %get-tuple-element.54.act_ref), custom_call_target="tpu_custom_call" | custom-call | flops 1000000000 | bytes 5761024 | tf_op jit(solution)/shard_map/pallas_call | solution.py:655
  30.1 0.9 copy-done
  31.0 0.0 collective-permute-done.2.prev_ref
  31.0 0.0 collective-permute-done.3.next_ref
  31.0 3.7 %shard_map.142 = (bf16[4,18,16,768]{3,2,1,0:T(8,128)(2,1)S(1)}, bf16[1024,256]{1,0:T(8,128)(2,1)S(1)}, bf16[1024,256]{1,0:T(8,128)(2,1)S(1)}, bf16[192,256]{1,0:...) custom-call(bf16[1024,256]{1,0:T(8,128)(2,1)S(1)} %get-tuple-element.44.hid_r, ...), custom_call_target="tpu_custom_call" | custom-call | bytes 10199040 | tf_op jit(solution)/shard_map/pallas_call | solution.py:655
  34.6 0.1 collective-permute-start.4
  34.7 4.9 %collective-permute-start.5 = (bf16[160,256]{1,0:T(8,128)(2,1)S(1)}, bf16[160,256]{1,0:T(8,128)(2,1)S(1)}, u32[]{:S(2)}, u32[]{:S(2)}) collective-permute-start(bf16[160,256]{1,0:T(8,128)(2,1)S(1)} %get-tuple-element.52), channel_id=1, source_target_pairs={{0,124},{1,125},{2,126},{3,127},{4,0},{5,1},{6,2},{7,3},{8,4},{9,5... | collective-permute-start | bytes 245768 | tf_op jit(solution)/shard_map/ppermute | solution.py:672
  39.6 2.5 %shard_map.144 = (f32[768,128]{1,0:T(8,128)S(1)}, bf16[384,1152]{1,0:T(8,128)(2,1)S(1)}, bf16[64,384]{1,0:T(8,128)(2,1)S(1)}) custom-call(bf16[4,18,16,768]{3,2,1,0:T(8,128)(2,1)S(1)} %get-tuple-element.57.filled_ref, bf16[1024,256]{1,0:T(8,128)(2,1)S(1)} %get-tuple-element.58.grad_ref, bf16[5696,256]{1,0:T(8,128)(2,1)S(1)} %shard_map.138.bank_ref.early_ref), custom_call_target="tpu_custom_call" | custom-call | flops 2000000000 | bytes 6537216 | tf_op jit(solution)/shard_map/pallas_call | solution.py:655
  42.1 0.0 collective-permute-done.4.prev_ref
  42.1 0.0 collective-permute-done.5.next_ref
  42.1 0.0 copy-start.6
  42.1 0.0 copy-start.7
  42.2 3.7 %shard_map.145 = (bf16[32,40,128]{2,1,0:T(8,128)(2,1)}, bf16[18,16,768]{2,1,0:T(8,128)(2,1)S(1)}, bf16[1024,256]{1,0:T(8,128)(2,1)S(1)}) custom-call(bf16[1024,256]{1,0:T(8,128)(2,1)S(1)} %get-tuple-element.49.hid_two_ref, bf16[192,256]{1,0:T(8,128)(2,1)S(1)} %get-tuple-element.50.local_ref, bf16[160,256]{1,0:T(8,128)(2,1)S(1)} %collective-permute-done.4.prev_ref, ...), custom_call_target="tpu_custom_call" | custom-call | bytes 10297344 | tf_op jit(solution)/shard_map/pallas_call | solution.py:655
  45.9 0.8 copy-done.8
  46.7 5.8 %all-to-all-start.1 = ((bf16[32,40,128]{2,1,0:T(8,128)(2,1)}), bf16[32,40,128]{2,1,0:T(8,128)(2,1)S(1)}, u32[]{:S(2)}, u32[]{:S(2)}) async-start(bf16[32,40,128]{2,1,0:T(8,128)(2,1)} %get-tuple-element.70), calls=%async_computation.1 | async-start | bytes 655360 | tf_op jit(solution)/shard_map/all_to_all | solution.py:758
  52.5 1.1 %copy-done.1 = bf16[1280,256]{1,0:T(8,128)(2,1)S(1)} copy-done((bf16[1280,256]{1,0:T(8,128)(2,1)S(1)}, bf16[1280,256]{1,0:T(8,128)(2,1)}, u32[]{:S(2)}) %copy-start.1) | copy-done | bytes 655384
  53.5 1.0 %copy-done.9 = bf16[18,16,768]{2,1,0:T(8,128)(2,1)S(1)} copy-done((bf16[18,16,768]{2,1,0:T(8,128)(2,1)S(1)}, bf16[18,16,768]{2,1,0:T(8,128)(2,1)}, u32[]{:S(2)}) %copy-start.9) | copy-done | bytes 442392
  54.5 3.0 %shard_map.146 = (bf16[16,256]{1,0:T(8,128)(2,1)}, f32[256,128]{1,0:T(8,128)S(1)}, bf16[80,128]{1,0:T(8,128)(2,1)S(1)}, bf16[80,128]{1,0:T(8,128)(2,1)S(1)}, bf16[96,128]{1,0:T(8,128)(2,1)S(1)}) custom-call(bf16[18,16,768]{2,1,0:T(8,128)(2,1)S(1)} %copy-done.9, bf16[1024,256]{1,0:T(8,128)(2,1)S(1)} %get-tuple-element.63.grad_ref, ...), custom_call_target="tpu_custom_call" | custom-call | flops 2000000000 | bytes 1836032 | tf_op jit(solution)/shard_map/pallas_call | solution.py:655
  57.5 4.6 %collective-permute-start.6 = (bf16[80,128]{1,0:T(8,128)(2,1)S(1)}, bf16[80,128]{1,0:T(8,128)(2,1)S(1)}, u32[]{:S(2)}, u32[]{:S(2)}) collective-permute-start(bf16[80,128]{1,0:T(8,128)(2,1)S(1)} %get-tuple-element.67), channel_id=1, source_target_pairs={{0,124},{1,125},{2,126},{3,127},{4,0},{5,1},{6,2},{7,3},{8,4},{9,5... | collective-permute-start | bytes 61448 | tf_op jit(solution)/shard_map/ppermute | solution.py:672
  62.2 0.0 collective-permute-start.7
  62.2 0.2 all-to-all-done.1.spread_ref
  62.3 0.7 shard_map.147
  63.0 0.1 collective-permute-done.6.next_ref
  63.1 5.0 %collective-permute-done.7.prev_ref = bf16[80,128]{1,0:T(8,128)(2,1)S(1)} collective-permute-done((bf16[80,128]{1,0:T(8,128)(2,1)S(1)}, bf16[80,128]{1,0:T(8,128)(2,1)S(1)}, u32[]{:S(2)}, u32[]{:S(2)}) %collective-permute-start.7) | collective-permute-done | bytes 20512 | tf_op jit(solution)/shard_map/ppermute | solution.py:672
  68.1 1.1 %shard_map.148 = (f32[16,256]{1,0:T(8,128)S(1)}, f32[8,256]{1,0:T(8,128)S(1)}, f32[1,4608]{1,0:T(1,128)}, f32[1,288]{1,0:T(1,128)}) custom-call(f32[256,128]{1,0:T(8,128)S(1)} %get-tuple-element.66.dx_ref, bf16[80,128]{1,0:T(8,128)(2,1)S(1)} %collective-permute-done.6.next_ref, bf16[80,128]{1,0:T(8,128)(2,1)S(1)} %collective-permute-done.7.prev_ref, ...), custom_call_target="tpu_custom_call" | custom-call | bytes 916608 | tf_op jit(solution)/shard_map/pallas_call | solution.py:655
  69.2 0.0 collective-permute-start.8
  69.2 9.9 %all-to-all-start.2 = ((bf16[16,16,128]{2,1,0:T(8,128)(2,1)}), bf16[16,16,128]{2,1,0:T(8,128)(2,1)S(1)}, u32[]{:S(2)}, u32[]{:S(2)}) async-start(bf16[16,16,128]{2,1,0:T(8,128)(2,1)} %get-tuple-element.74), calls=%async_computation.2 | async-start | bytes 131072 | tf_op jit(solution)/shard_map/all_to_all | solution.py:775
  79.2 0.0 collective-permute-done.8
  79.2 0.6 add_bitcast_fusion
  79.8 6.7 %all-to-all-done.2 = bf16[16,16,128]{2,1,0:T(8,128)(2,1)S(1)} async-done(((bf16[16,16,128]{2,1,0:T(8,128)(2,1)}), bf16[16,16,128]{2,1,0:T(8,128)(2,1)S(1)}, u32[]{:S(2)}, u32[]{:S(2)}) %all-to-all-start.2) | async-done | bytes 65568 | tf_op jit(solution)/shard_map/all_to_all | solution.py:775
  86.5 1.1 %shard_map.149 = f32[216,256]{1,0:T(8,128)} custom-call(bf16[256,128]{1,0:T(8,128)(2,1)S(1)} %bitcast.28, bf16[1280,256]{1,0:T(8,128)(2,1)S(1)} %copy-done.2), custom_call_target="tpu_custom_call" | custom-call | bytes 942080 | tf_op jit(solution)/shard_map/pallas_call | solution.py:655
  (11 shorter events, 0.0 us)
Async XLA Ops:
  2.0 11.6 %all-to-all-start = ((bf16[8,32,256]{2,1,0:T(8,128)(2,1)}), bf16[8,32,256]{2,1,0:T(8,128)(2,1)S(1)}, u32[]{:S(2)}, u32[]{:S(2)}) async-start(bf16[8,32,256]{2,1,0:T(8,128)(2,1)} %shard_map.137), calls=%async_computation | async-start | bytes 262144 | tf_op jit(solution)/shard_map/all_to_all | solution.py:687
  14.1 8.6 %collective-permute-start = (bf16[80,128]{1,0:T(8,128)(2,1)S(1)}, bf16[80,128]{1,0:T(8,128)(2,1)S(1)}, u32[]{:S(2)}, u32[]{:S(2)}) collective-permute-start(bf16[80,128]{1,0:T(8,128)(2,1)S(1)} %get-tuple-element.78), channel_id=1, source_target_pairs={{0,4},{1,5},{2,6},{3,7},{4,8},{5,9},{6,10},{7,11},{8,12},{9,13},{1... | collective-permute-start | bytes 61448 | tf_op jit(solution)/shard_map/ppermute | solution.py:672
  15.1 7.6 %collective-permute-start.1 = (bf16[80,128]{1,0:T(8,128)(2,1)S(1)}, bf16[80,128]{1,0:T(8,128)(2,1)S(1)}, u32[]{:S(2)}, u32[]{:S(2)}) collective-permute-start(bf16[80,128]{1,0:T(8,128)(2,1)S(1)} %get-tuple-element.77), channel_id=1, source_target_pairs={{0,124},{1,125},{2,126},{3,127},{4,0},{5,1},{6,2},{7,3},{8,4},{9,5... | collective-permute-start | bytes 61448 | tf_op jit(solution)/shard_map/ppermute | solution.py:672
  22.8 6.2 %copy-start.3 = (s32[1,216,64]{1,2,0:T(8,128)S(1)}, s32[1,216,64]{1,2,0:T(8,128)}, u32[]{:S(2)}) copy-start(s32[1,216,64]{1,2,0:T(8,128)} %param.17) | copy-start | bytes 165892
  22.8 6.2 %copy-start.4 = (s32[1,2304,4]{1,2,0:T(4,128)S(1)}, s32[1,2304,4]{1,2,0:T(4,128)}, u32[]{:S(2)}) copy-start(s32[1,2304,4]{1,2,0:T(4,128)} %param.19) | copy-start | bytes 110596
  24.1 6.9 %collective-permute-start.2 = (bf16[160,256]{1,0:T(8,128)(2,1)S(1)}, bf16[160,256]{1,0:T(8,128)(2,1)S(1)}, u32[]{:S(2)}, u32[]{:S(2)}) collective-permute-start(bf16[160,256]{1,0:T(8,128)(2,1)S(1)} %get-tuple-element.46), channel_id=1, source_target_pairs={{0,4},{1,5},{2,6},{3,7},{4,8},{5,9},{6,10},{7,11},{8,12},{9,13},{1... | collective-permute-start | bytes 245768 | tf_op jit(solution)/shard_map/ppermute | solution.py:672
  24.2 6.8 %collective-permute-start.3 = (bf16[160,256]{1,0:T(8,128)(2,1)S(1)}, bf16[160,256]{1,0:T(8,128)(2,1)S(1)}, u32[]{:S(2)}, u32[]{:S(2)}) collective-permute-start(bf16[160,256]{1,0:T(8,128)(2,1)S(1)} %get-tuple-element.47), channel_id=1, source_target_pairs={{0,124},{1,125},{2,126},{3,127},{4,0},{5,1},{6,2},{7,3},{8,4},{9,5... | collective-permute-start | bytes 245768 | tf_op jit(solution)/shard_map/ppermute | solution.py:672
  30.1 0.9 copy-start
  34.6 7.5 %collective-permute-start.4 = (bf16[160,256]{1,0:T(8,128)(2,1)S(1)}, bf16[160,256]{1,0:T(8,128)(2,1)S(1)}, u32[]{:S(2)}, u32[]{:S(2)}) collective-permute-start(bf16[160,256]{1,0:T(8,128)(2,1)S(1)} %get-tuple-element.51), channel_id=1, source_target_pairs={{0,4},{1,5},{2,6},{3,7},{4,8},{5,9},{6,10},{7,11},{8,12},{9,13},{1... | collective-permute-start | bytes 245768 | tf_op jit(solution)/shard_map/ppermute | solution.py:672
  34.7 7.4 %collective-permute-start.5 = (bf16[160,256]{1,0:T(8,128)(2,1)S(1)}, bf16[160,256]{1,0:T(8,128)(2,1)S(1)}, u32[]{:S(2)}, u32[]{:S(2)}) collective-permute-start(bf16[160,256]{1,0:T(8,128)(2,1)S(1)} %get-tuple-element.52), channel_id=1, source_target_pairs={{0,124},{1,125},{2,126},{3,127},{4,0},{5,1},{6,2},{7,3},{8,4},{9,5... | collective-permute-start | bytes 245768 | tf_op jit(solution)/shard_map/ppermute | solution.py:672
  42.1 10.3 %copy-start.6 = (bf16[1,16,256]{2,1,0:T(8,128)(2,1)S(1)}, bf16[1,16,256]{2,1,0:T(8,128)(2,1)}, u32[]{:S(2)}) copy-start(bf16[1,16,256]{2,1,0:T(8,128)(2,1)} %param.10) | copy-start | bytes 24580
  42.1 10.3 %copy-start.7 = (s32[256]{0:T(256)S(1)}, s32[256]{0:T(256)}, u32[]{:S(2)}) copy-start(s32[256]{0:T(256)} %param.12) | copy-start | bytes 3076
  45.9 0.8 copy-start.8
  46.7 15.7 %all-to-all-start.1 = ((bf16[32,40,128]{2,1,0:T(8,128)(2,1)}), bf16[32,40,128]{2,1,0:T(8,128)(2,1)S(1)}, u32[]{:S(2)}, u32[]{:S(2)}) async-start(bf16[32,40,128]{2,1,0:T(8,128)(2,1)} %get-tuple-element.70), calls=%async_computation.1 | async-start | bytes 655360 | tf_op jit(solution)/shard_map/all_to_all | solution.py:758
  52.4 1.1 %copy-start.1 = (bf16[1280,256]{1,0:T(8,128)(2,1)S(1)}, bf16[1280,256]{1,0:T(8,128)(2,1)}, u32[]{:S(2)}) copy-start(bf16[1280,256]{1,0:T(8,128)(2,1)} %copy-done) | copy-start | bytes 1966084
  53.5 1.0 %copy-start.9 = (bf16[18,16,768]{2,1,0:T(8,128)(2,1)S(1)}, bf16[18,16,768]{2,1,0:T(8,128)(2,1)}, u32[]{:S(2)}) copy-start(bf16[18,16,768]{2,1,0:T(8,128)(2,1)} %copy-done.8) | copy-start | bytes 1327108
  54.5 13.6 %copy-start.2 = (bf16[1280,256]{1,0:T(8,128)(2,1)S(1)}, bf16[1280,256]{1,0:T(8,128)(2,1)}, u32[]{:S(2)}) copy-start(bf16[1280,256]{1,0:T(8,128)(2,1)} %copy-done) | copy-start | bytes 1966084
  54.5 13.6 %copy-start.5 = (bf16[1,16,256]{2,1,0:T(8,128)(2,1)S(1)}, bf16[1,16,256]{2,1,0:T(8,128)(2,1)}, u32[]{:S(2)}) copy-start(bf16[1,16,256]{2,1,0:T(8,128)(2,1)} %param.11) | copy-start | bytes 24580
  57.5 5.6 %collective-permute-start.6 = (bf16[80,128]{1,0:T(8,128)(2,1)S(1)}, bf16[80,128]{1,0:T(8,128)(2,1)S(1)}, u32[]{:S(2)}, u32[]{:S(2)}) collective-permute-start(bf16[80,128]{1,0:T(8,128)(2,1)S(1)} %get-tuple-element.67), channel_id=1, source_target_pairs={{0,124},{1,125},{2,126},{3,127},{4,0},{5,1},{6,2},{7,3},{8,4},{9,5... | collective-permute-start | bytes 61448 | tf_op jit(solution)/shard_map/ppermute | solution.py:672
  62.2 6.0 %collective-permute-start.7 = (bf16[80,128]{1,0:T(8,128)(2,1)S(1)}, bf16[80,128]{1,0:T(8,128)(2,1)S(1)}, u32[]{:S(2)}, u32[]{:S(2)}) collective-permute-start(bf16[80,128]{1,0:T(8,128)(2,1)S(1)} %get-tuple-element.68), channel_id=1, source_target_pairs={{0,4},{1,5},{2,6},{3,7},{4,8},{5,9},{6,10},{7,11},{8,12},{9,13},{1... | collective-permute-start | bytes 61448 | tf_op jit(solution)/shard_map/ppermute | solution.py:672
  69.2 10.0 %collective-permute-start.8 = (f32[8,256]{1,0:T(8,128)S(1)}, f32[8,256]{1,0:T(8,128)S(1)}, u32[]{:S(2)}, u32[]{:S(2)}) collective-permute-start(f32[8,256]{1,0:T(8,128)S(1)} %get-tuple-element.73), channel_id=1, source_target_pairs={{0,128},{128,0},{1,129},{129,1},{2,130},{130,2},{3,131},{131,3},{4... | collective-permute-start | bytes 24584 | tf_op jit(solution)/shard_map/ppermute | solution.py:782
  69.2 17.3 %all-to-all-start.2 = ((bf16[16,16,128]{2,1,0:T(8,128)(2,1)}), bf16[16,16,128]{2,1,0:T(8,128)(2,1)S(1)}, u32[]{:S(2)}, u32[]{:S(2)}) async-start(bf16[16,16,128]{2,1,0:T(8,128)(2,1)} %get-tuple-element.74), calls=%async_computation.2 | async-start | bytes 131072 | tf_op jit(solution)/shard_map/all_to_all | solution.py:775

commit v5 on v4

--- a/solution.py
+++ b/solution.py
@@ -25,15 +25,15 @@
 TAKE = GIVE + LINE
 FIRST_W = TAKE + LINE
 OUT_BACK = FIRST_W + 3 * PADC
-MID_BACK = OUT_BACK + 3 * PADC
+BANK_ONE = OUT_BACK + 3 * PADC
+MID_BACK = 0
 MID_GATES = MID_BACK + 9 * HID
-BANK_ONE = MID_GATES + 9 * 64
+BANK_MID = MID_GATES + 9 * 64
 MID_W = 0
 FIRST_GATES = MID_W + 9 * HID
 OUT_GATES = FIRST_GATES + 2 * 64
 BANK_TWO = OUT_GATES + 9 * 16
-LAST_W = 0
-FIRST_WIDE = LAST_W + 6 * PADC
+FIRST_WIDE = 0
 GIVE_OWN = FIRST_WIDE + 224
 OWN_GATES = GIVE_OWN + CELLS
 BANK_THREE = OWN_GATES + 32
@@ -299,7 +299,7 @@
 
 
 def prepare_early_kernel(
-    turn_hbm, first_gates_hbm, out_gates_hbm, first_hbm, out_hbm, mid_gates_hbm, mid_hbm, bank_ref,
+    turn_hbm, first_gates_hbm, out_gates_hbm, first_hbm, out_hbm, mid_gates_hbm, mid_hbm, bank_ref, middle_ref,
     turn_ref, first_gates_ref, out_gates_ref, first_ref, out_ref, mid_gates_ref, mid_ref, sems,
 ):
     copies = fetch(
@@ -347,18 +347,18 @@
     for tap in range(9):
         cols = slice(HID * tap, HID * (tap + 1))
         gates = mid_gates_ref[:, cols].astype(F32)
-        bank_ref[MID_GATES + 64 * tap : MID_GATES + 64 * (tap + 1)] = gates.astype(BF)
+        middle_ref[MID_GATES + 64 * tap : MID_GATES + 64 * (tap + 1)] = gates.astype(BF)
         at = MID_BACK + HID * (3 * (tap % 3) + tap // 3)
-        bank_ref[at : at + HID] = kept_rows(gates, dot_nt(eye(HID, HID), mid_ref[cols])).astype(BF)
-
-
-def prepare_late_kernel(early_ref, first_gates_hbm, out_gates_hbm, two_ref, first_gates_ref, out_gates_ref, sems):
+        middle_ref[at : at + HID] = kept_rows(gates, dot_nt(eye(HID, HID), mid_ref[cols])).astype(BF)
+
+
+def prepare_late_kernel(middle_ref, first_gates_hbm, out_gates_hbm, two_ref, first_gates_ref, out_gates_ref, sems):
     copies = fetch((first_gates_hbm, out_gates_hbm), (first_gates_ref, out_gates_ref), sems)
     for a in range(3):
         for b in range(3):
             at = MID_BACK + HID * (3 * b + a)
             to = MID_W + HID * (3 * a + b)
-            two_ref[to : to + HID] = dot_tn(early_ref[at : at + HID], eye(HID, HID)).astype(BF)
+            two_ref[to : to + HID] = dot_tn(middle_ref[at : at + HID], eye(HID, HID)).astype(BF)
     for copy in copies:
         copy.wait()
     count = 9 * DEPTH
@@ -375,18 +375,17 @@
         two_ref[OUT_GATES + 16 * tap : OUT_GATES + 16 * (tap + 1)] = gates[:, HID * tap : HID * (tap + 1)]
 
 
-def prepare_last_kernel(early_ref, first_gates_ref, out_gates_ref, act_ref, three_ref, slope_ref):
+def prepare_last_kernel(early_ref, middle_ref, first_gates_ref, out_gates_ref, act_ref, three_ref, slope_ref):
     slope_ref[...] = slope(act_ref[...])
     col = lax.axis_index(("xh", "core"))
     tile = lax.axis_index(FACE)
     three_ref[GIVE_OWN : GIVE_OWN + CELLS] = early_ref[pl.ds(pl.multiple_of(GIVE + CELLS * col, CELLS), CELLS)]
-    three_ref[LAST_W : LAST_W + 6 * PADC] = early_ref[FIRST_W : FIRST_W + 6 * PADC]
     count = 9 * DEPTH
     gates = first_gates_ref[...].astype(F32).astype(BF)
     three_ref[FIRST_WIDE : FIRST_WIDE + count] = dot_tn(gates, repeat_four(HID // 4, HID)).astype(BF)
     place = lax.broadcasted_iota(jnp.int32, (32, 9 * HID), 0)
     mine = one_hot((32, 9 * HID), 1, jnp.where(place < 18, 18 * tile + place, -1))
-    gates = bank_gates(early_ref, MID_GATES, 64, range(9))
+    gates = bank_gates(middle_ref, MID_GATES, 64, range(9))
     three_ref[OWN_GATES : OWN_GATES + 32, :64] = dot_nt(mine, gates).astype(BF)
     gates = dot(eye(PADC, 4), out_gates_ref[...].astype(F32).astype(BF)).astype(BF)
     three_ref[OWN_GATES : OWN_GATES + 32, PADC:] = dot_nt(mine, gates).astype(BF)
@@ -439,7 +438,7 @@
 
 
 def layer_two_kernel(
-    hid_ref, local_in_ref, prev_ref, next_ref, inner_two_ref, early_ref, bank_ref,
+    hid_ref, local_in_ref, prev_ref, next_ref, inner_two_ref, early_ref, middle_ref, bank_ref,
     filled_ref, grad_ref, hid_two_ref, local_ref, up_ref, down_ref, inner_ref,
     pad_ref,
 ):
@@ -456,7 +455,7 @@
     pad_ref[...] = jnp.zeros_like(pad_ref)
     fold_row(
         lambda col: pad_lines(grad_ref[CELLS * col : CELLS * (col + 1)], pad_ref),
-        early_ref, MID_BACK, slice(None), inner_ref, down_ref.at[80:160], up_ref.at[80:160], local_ref.at[96:192],
+        middle_ref, MID_BACK, slice(None), inner_ref, down_ref.at[80:160], up_ref.at[80:160], local_ref.at[96:192],
     )
 
 
@@ -477,10 +476,10 @@
         flat_ref[64:128, cols] = high.astype(BF)
 
 
-def mid_term_kernel(filled_ref, grad_ref, early_ref, part_ref, pick_out_ref, pick_first_ref, flat_ref):
+def mid_term_kernel(filled_ref, grad_ref, middle_ref, part_ref, pick_out_ref, pick_first_ref, flat_ref):
     col = lax.axis_index(("xh", "core"))
     term_pairs(
-        filled_ref, grad_ref[...], lambda a: bank_gates(early_ref, MID_GATES, 64, range(3 * a, 3 * a + 3)), flat_ref
+        filled_ref, grad_ref[...], lambda a: bank_gates(middle_ref, MID_GATES, 64, range(3 * a, 3 * a + 3)), flat_ref
     )
     shape = (16 * CHUNK, 1152)
     place = lax.broadcasted_iota(jnp.int32, shape, 0)
@@ -558,11 +557,11 @@
 ):
     for a in range(3):
         for b in range(3):
-            at = LAST_W + PADC * a + 32 * b
+            at = FIRST_W + PADC * a + 32 * b
             block = jnp.concatenate([bank_ref[at : at + 32], jnp.zeros((PADC - 32, HID), BF)], 0)
             to = HID * (3 * b + a)
             narrow_ref[to : to + HID, :PADC] = dot_nt(eye(HID, HID), block).astype(BF)
-            at = LAST_W + PADC * (3 + b) + FIELDS * a
+            at = OUT_BACK + PADC * b + FIELDS * a
             block = jnp.concatenate([bank_ref[at : at + FIELDS], jnp.zeros((PADC - FIELDS, HID), BF)], 0)
             to = HID * (3 * a + b)
             narrow_ref[to : to + HID, PADC:] = dot_tn(block, eye(PADC, PADC)).astype(BF)
@@ -688,8 +687,8 @@
 
     turns, out_turned = turn_table.T, out_gates[0].T
     first_turned, mid_turned = first_gates[0].T, mid_gates[0].T
-    early = call(
-        prepare_early_kernel, [sds((BANK_ONE, HID), BF)],
+    early, middle = call(
+        prepare_early_kernel, [sds((BANK_ONE, HID), BF), sds((BANK_MID, HID), BF)],
         [turns, first_turned, out_turned, first_kernel[0], out_kernel[0].T, mid_turned, mid_kernel[0]],
         scratch=[
             pltpu.SMEM((4, TILES), jnp.int32), pltpu.VMEM((64, 9 * DEPTH), jnp.int32),
@@ -698,7 +697,7 @@
             pltpu.VMEM((9 * HID, HID), BF), pltpu.SemaphoreType.DMA((7,)),
         ],
         far=(0, 1, 2, 3, 4, 5, 6), flops=5 * 10**9,
-    )[0]
+    )
 
     field, grad_cells, strips_zero = call(
         start_kernel,
@@ -707,7 +706,7 @@
     prev_zero = row_shift(strips_zero[UP], 1)
     next_zero = row_shift(strips_zero[DOWN], -1)
     two = call(
-        prepare_late_kernel, [sds((BANK_TWO, HID), BF)], [early, first_turned, out_turned],
+        prepare_late_kernel, [sds((BANK_TWO, HID), BF)], [middle, first_turned, out_turned],
         scratch=[
             pltpu.VMEM((64, 9 * DEPTH), jnp.int32), pltpu.VMEM((4, 9 * HID), jnp.int32),
             pltpu.SemaphoreType.DMA((2,)),
@@ -725,13 +724,13 @@
 
     three, slope_one = call(
         prepare_last_kernel, [sds((BANK_THREE, HID), BF), sds((LINE, HID), F32)],
-        [early, first_turned, out_turned, act_one], flops=10**9,
+        [early, middle, first_turned, out_turned, act_one], flops=10**9,
     )
 
     filled_one, grad_two, hid_two, local_two, up_two, down_two, inner_one = call(
         layer_two_kernel,
         [sds((ROW, TS + 2, TS, 3 * HID), BF), sds((LINE, HID), BF), sds((LINE, HID), BF)] + exchange,
-        [hid_one, local_one, prev_one, next_one, inner_two, early, two],
+        [hid_one, local_one, prev_one, next_one, inner_two, early, middle, two],
         scratch=[pltpu.VMEM((TS + 2, TS, 3 * HID), BF)],
     )
     prev_two = row_shift(up_two, 1)
@@ -740,7 +739,7 @@
     part, pick_out, pick_first = call(
         mid_term_kernel,
         [sds((32 * CHUNK, PADC), F32), sds((16 * CHUNK, 1152), BF), sds((4 * SHARE, 3 * PADC), BF)],
-        [filled_one, grad_two, early],
+        [filled_one, grad_two, middle],
         scratch=[pltpu.VMEM((PADC, 9 * HID), BF)], flops=2 * 10**9,
     )
 
@@ -761,7 +760,7 @@
         last_kernel,
         [sds((FIELDS, CELLS), BF), sds((CELLS, PADC), F32), sds((80, PADC), BF), sds((80, PADC), BF),
          sds((96, PADC), BF)],
-        [mine_two, grad_one, three, state[0], sea],
+        [mine_two, grad_one, early, state[0], sea],
         scratch=[
             pltpu.VMEM((TS + 2, TS, 3 * HID), BF), pltpu.VMEM((LINE, PADC), F32),
             pltpu.VMEM((9 * HID, HID), BF),

time: 88.1 us -> 85.2 us (0.967)
  local copies, waits for them, and re-layouts: 3.76 us -> 0.04 us
  waiting for transfers between devices: 14.2 us -> 15.3 us
    unnamed x20 -> x10, local copies, waits for them, and re-layouts: 3.76 us -> 0.03 us
    all_to_all x1, waiting for transfers between devices: 0.16 us -> 2.26 us  [body(): spread = lax.all_to_all(buffer, ROW_AXES, 0, 0)]
    ppermute x8, waiting for transfers between devices: 5.13 us -> 4.22 us  [row_shift(): return lax.ppermute(value, FACE, pairs)]
where the time goes in v5:
time: 85.2 us; the launch traced here: 84.7 us
  starting transfers between devices  43.9 us (52%)
  Pallas kernels  23.9 us (28%)
  waiting for transfers between devices  15.3 us (18%)
    pallas_call x13, Pallas kernels, call(): pl.pallas_call(body, out_shape=[jax.ShapeDtypeStruct(item.shape, item.dty...  23.9 us
    ppermute x8, starting transfers between devices, row_shift(): return lax.ppermute(value, FACE, pairs)  22.2 us
    all_to_all x1, starting transfers between devices, body(): lax.all_to_all(shared, ('y', 'xh', 'core'), 0, 0).reshape(16 * SHARE, PADC)  9.42 us
    all_to_all x1, waiting for transfers between devices, body(): lax.all_to_all(shared, ('y', 'xh', 'core'), 0, 0).reshape(16 * SHARE, PADC)  6.71 us
    all_to_all x1, starting transfers between devices, body(): lax.all_to_all(packed, LINE_AXES, 0, 0).reshape(2, ROW, 2 * FIELDS, CELLS)  6.49 us
    all_to_all x1, starting transfers between devices, body(): spread = lax.all_to_all(buffer, ROW_AXES, 0, 0)  5.75 us
    ppermute x8, waiting for transfers between devices, row_shift(): return lax.ppermute(value, FACE, pairs)  4.22 us
    all_to_all x1, waiting for transfers between devices, body(): spread = lax.all_to_all(buffer, ROW_AXES, 0, 0)  2.26 us
  transfers between devices with their start and end apart: 12, of which 5 were waited for; matrix products, arithmetic and copies ran while one was open for 1% of the time, Pallas kernels for 13%

profile of v5, /device:TPU:1, one launch (start us, length us, event | category | flops | bytes accessed | tf_op | source)
XLA Modules:
  0.0 84.7 jit_solution(15450651743844742667)
XLA Ops:
  0.6 1.4 %shard_map.137 = bf16[8,32,256]{2,1,0:T(8,128)(2,1)} custom-call(bf16[16,256]{1,0:T(8,128)(2,1)} %bitcast.34, bf16[16,256]{1,0:T(8,128)(2,1)} %bitcast.32, s32[1,256]{1,0:T(1,128)} %bitcast.36), custom_call_target="tpu_custom_call" | custom-call | bytes 148480 | tf_op jit(solution)/shard_map/pallas_call | solution.py:654
  2.0 6.5 %all-to-all-start = ((bf16[8,32,256]{2,1,0:T(8,128)(2,1)}), bf16[8,32,256]{2,1,0:T(8,128)(2,1)S(1)}, u32[]{:S(2)}, u32[]{:S(2)}) async-start(bf16[8,32,256]{2,1,0:T(8,128)(2,1)} %shard_map.137), calls=%async_computation | async-start | bytes 262144 | tf_op jit(solution)/shard_map/all_to_all | solution.py:686
  8.5 3.0 %shard_map.138 = (bf16[2816,256]{1,0:T(8,128)(2,1)S(1)}, bf16[2880,256]{1,0:T(8,128)(2,1)S(1)}) custom-call(s32[4,128]{1,0:T(4,128)} %bitcast.43, s32[64,216]{1,0:T(8,128)} %bitcast.26, s32[4,2304]{1,0:T(4,128)} %bitcast.29, bf16[216,256]{1,0:T(8,128)(2,1)} %bitcast.41, bf16[16,2304]{1,0:T(8,128)(2,1)} %bitcast.42, s32[64,2304]{1,0:T(8,128)} %bitcast.40, ...), custom_call_target="tpu_custom_call" | custom-call | flops 5000000000 | bytes 4964352 | tf_op jit(solution)/shard_map/pallas_call | solution.py:654
  11.5 2.2 %all-to-all-done = bf16[8,32,256]{2,1,0:T(8,128)(2,1)S(1)} async-done(((bf16[8,32,256]{2,1,0:T(8,128)(2,1)}), bf16[8,32,256]{2,1,0:T(8,128)(2,1)S(1)}, u32[]{:S(2)}, u32[]{:S(2)}) %all-to-all-start) | async-done | bytes 131104 | tf_op jit(solution)/shard_map/all_to_all | solution.py:686
  13.7 0.4 shard_map.139
  14.1 1.0 %collective-permute-start = (bf16[80,128]{1,0:T(8,128)(2,1)S(1)}, bf16[80,128]{1,0:T(8,128)(2,1)S(1)}, u32[]{:S(2)}, u32[]{:S(2)}) collective-permute-start(bf16[80,128]{1,0:T(8,128)(2,1)S(1)} %get-tuple-element.82), channel_id=1, source_target_pairs={{0,4},{1,5},{2,6},{3,7},{4,8},{5,9},{6,10},{7,11},{8,12},{9,13},{1... | collective-permute-start | bytes 61448 | tf_op jit(solution)/shard_map/ppermute | solution.py:671
  15.1 6.5 %collective-permute-start.1 = (bf16[80,128]{1,0:T(8,128)(2,1)S(1)}, bf16[80,128]{1,0:T(8,128)(2,1)S(1)}, u32[]{:S(2)}, u32[]{:S(2)}) collective-permute-start(bf16[80,128]{1,0:T(8,128)(2,1)S(1)} %get-tuple-element.81), channel_id=1, source_target_pairs={{0,124},{1,125},{2,126},{3,127},{4,0},{5,1},{6,2},{7,3},{8,4},{9,5... | collective-permute-start | bytes 61448 | tf_op jit(solution)/shard_map/ppermute | solution.py:671
  21.6 1.1 %shard_map.141.bank_ref = bf16[2576,256]{1,0:T(8,128)(2,1)S(1)} custom-call(bf16[2880,256]{1,0:T(8,128)(2,1)S(1)} %get-tuple-element.52.middle_ref, s32[64,216]{1,0:T(8,128)} %bitcast.27, s32[4,2304]{1,0:T(4,128)} %bitcast.30), custom_call_target="tpu_custom_call" | custom-call | flops 1000000000 | bytes 2885632 | tf_op jit(solution)/shard_map/pallas_call | solution.py:654
  22.8 0.0 copy-start
  22.8 0.0 copy-start.1
  22.8 0.0 collective-permute-done.prev_ref
  22.8 0.0 collective-permute-done.1.next_ref
  22.8 1.3 %shard_map.140 = (bf16[4,18,16,128]{3,2,1,0:T(8,128)(2,1)S(1)}, f32[1024,256]{1,0:T(8,128)S(1)}, bf16[1024,256]{1,0:T(8,128)(2,1)S(1)}, bf16[192,256]{1,0:T(8,12...) custom-call(bf16[1024,128]{1,0:T(8,128)(2,1)S(1)} %get-tuple-element.44.field_ref, ...), custom_call_target="tpu_custom_call" | custom-call | bytes 5251072 | tf_op jit(solution)/shard_map/pallas_call | solution.py:654
  24.1 0.1 collective-permute-start.2
  24.2 4.8 %collective-permute-start.3 = (bf16[160,256]{1,0:T(8,128)(2,1)S(1)}, bf16[160,256]{1,0:T(8,128)(2,1)S(1)}, u32[]{:S(2)}, u32[]{:S(2)}) collective-permute-start(bf16[160,256]{1,0:T(8,128)(2,1)S(1)} %get-tuple-element.50), channel_id=1, source_target_pairs={{0,124},{1,125},{2,126},{3,127},{4,0},{5,1},{6,2},{7,3},{8,4},{9,5... | collective-permute-start | bytes 245768 | tf_op jit(solution)/shard_map/ppermute | solution.py:671
  29.0 0.0 copy-done
  29.0 0.0 copy-done.1
  29.0 1.1 %shard_map.143 = (bf16[512,256]{1,0:T(8,128)(2,1)S(1)}, f32[1024,256]{1,0:T(8,128)S(1)}) custom-call(bf16[2816,256]{1,0:T(8,128)(2,1)S(1)} %get-tuple-element.43.bank_ref.early_ref, bf16[2880,256]{1,0:T(8,128)(2,1)S(1)} %get-tuple-element.52.middle_ref, s32[64,216]{1,0:T(8,128)S(1)} %bitcast.28, s32[4,2304]{1,0:T(4,128)S(1)} %bitcast.31, ...), custom_call_target="tpu_custom_call" | custom-call | flops 1000000000 | bytes 5367808 | tf_op jit(solution)/shard_map/pallas_call | solution.py:654
  30.1 0.7 collective-permute-done.2.prev_ref
  30.8 0.0 collective-permute-done.3.next_ref
  30.8 3.7 %shard_map.142 = (bf16[4,18,16,768]{3,2,1,0:T(8,128)(2,1)S(1)}, bf16[1024,256]{1,0:T(8,128)(2,1)S(1)}, bf16[1024,256]{1,0:T(8,128)(2,1)S(1)}, bf16[192,256]{1,0:...) custom-call(bf16[1024,256]{1,0:T(8,128)(2,1)S(1)} %get-tuple-element.47.hid_r, ...), custom_call_target="tpu_custom_call" | custom-call | bytes 10199040 | tf_op jit(solution)/shard_map/pallas_call | solution.py:654
  34.4 0.1 collective-permute-start.4
  34.5 5.1 %collective-permute-start.5 = (bf16[160,256]{1,0:T(8,128)(2,1)S(1)}, bf16[160,256]{1,0:T(8,128)(2,1)S(1)}, u32[]{:S(2)}, u32[]{:S(2)}) collective-permute-start(bf16[160,256]{1,0:T(8,128)(2,1)S(1)} %get-tuple-element.56), channel_id=1, source_target_pairs={{0,124},{1,125},{2,126},{3,127},{4,0},{5,1},{6,2},{7,3},{8,4},{9,5... | collective-permute-start | bytes 245768 | tf_op jit(solution)/shard_map/ppermute | solution.py:671
  39.6 2.5 %shard_map.144 = (f32[768,128]{1,0:T(8,128)S(1)}, bf16[384,1152]{1,0:T(8,128)(2,1)S(1)}, bf16[64,384]{1,0:T(8,128)(2,1)S(1)}) custom-call(bf16[4,18,16,768]{3,2,1,0:T(8,128)(2,1)S(1)} %get-tuple-element.61.filled_ref, bf16[1024,256]{1,0:T(8,128)(2,1)S(1)} %get-tuple-element.62.grad_ref, bf16[2880,256]{1,0:T(8,128)(2,1)S(1)} %get-tuple-element.52.middle_ref), custom_call_target="tpu_custom_call" | custom-call | flops 2000000000 | bytes 5095424 | tf_op jit(solution)/shard_map/pallas_call | solution.py:654
  42.1 0.0 collective-permute-done.4.prev_ref
  42.1 0.0 collective-permute-done.5.next_ref
  42.2 0.0 copy-start.3
  42.2 0.0 copy-start.4
  42.2 3.7 %shard_map.145 = (bf16[32,40,128]{2,1,0:T(8,128)(2,1)}, bf16[18,16,768]{2,1,0:T(8,128)(2,1)S(1)}, bf16[1024,256]{1,0:T(8,128)(2,1)S(1)}) custom-call(bf16[1024,256]{1,0:T(8,128)(2,1)S(1)} %get-tuple-element.53.hid_two_ref, bf16[192,256]{1,0:T(8,128)(2,1)S(1)} %get-tuple-element.54.local_ref, bf16[160,256]{1,0:T(8,128)(2,1)S(1)} %collective-permute-done.4.prev_ref, ...), custom_call_target="tpu_custom_call" | custom-call | bytes 8822784 | tf_op jit(solution)/shard_map/pallas_call | solution.py:654
  45.9 5.7 %all-to-all-start.1 = ((bf16[32,40,128]{2,1,0:T(8,128)(2,1)}), bf16[32,40,128]{2,1,0:T(8,128)(2,1)S(1)}, u32[]{:S(2)}, u32[]{:S(2)}) async-start(bf16[32,40,128]{2,1,0:T(8,128)(2,1)} %get-tuple-element.74), calls=%async_computation.1 | async-start | bytes 655360 | tf_op jit(solution)/shard_map/all_to_all | solution.py:757
  51.6 0.0 copy-done.3
  51.6 0.0 copy-done.4
  51.6 0.0 copy-start.2
  51.6 3.0 %shard_map.146 = (bf16[16,256]{1,0:T(8,128)(2,1)}, f32[256,128]{1,0:T(8,128)S(1)}, bf16[80,128]{1,0:T(8,128)(2,1)S(1)}, bf16[80,128]{1,0:T(8,128)(2,1)S(1)}, bf16[96,128]{1,0:T(8,128)(2,1)S(1)}) custom-call(bf16[18,16,768]{2,1,0:T(8,128)(2,1)S(1)} %get-tuple-element.66.mine_ref, bf16[1024,256]{1,0:T(8,128)(2,1)S(1)} %get-tuple-element.67.grad_ref, ...), custom_call_target="tpu_custom_call" | custom-call | flops 2000000000 | bytes 2622464 | tf_op jit(solution)/shard_map/pallas_call | solution.py:654
  54.6 4.6 %collective-permute-start.6 = (bf16[80,128]{1,0:T(8,128)(2,1)S(1)}, bf16[80,128]{1,0:T(8,128)(2,1)S(1)}, u32[]{:S(2)}, u32[]{:S(2)}) collective-permute-start(bf16[80,128]{1,0:T(8,128)(2,1)S(1)} %get-tuple-element.70), channel_id=1, source_target_pairs={{0,124},{1,125},{2,126},{3,127},{4,0},{5,1},{6,2},{7,3},{8,4},{9,5... | collective-permute-start | bytes 61448 | tf_op jit(solution)/shard_map/ppermute | solution.py:671
  59.3 0.0 collective-permute-start.7
  59.3 2.3 %all-to-all-done.1.spread_ref = bf16[32,40,128]{2,1,0:T(8,128)(2,1)S(1)} async-done(((bf16[32,40,128]{2,1,0:T(8,128)(2,1)}), bf16[32,40,128]{2,1,0:T(8,128)(2,1)S(1)}, u32[]{:S(2)}, u32[]{:S(2)}) %all-to-all-start.1) | async-done | bytes 327712 | tf_op jit(solution)/shard_map/all_to_all | solution.py:757
  61.5 0.7 shard_map.147
  62.2 0.0 collective-permute-done.6.next_ref
  62.2 3.5 %collective-permute-done.7.prev_ref = bf16[80,128]{1,0:T(8,128)(2,1)S(1)} collective-permute-done((bf16[80,128]{1,0:T(8,128)(2,1)S(1)}, bf16[80,128]{1,0:T(8,128)(2,1)S(1)}, u32[]{:S(2)}, u32[]{:S(2)}) %collective-permute-start.7) | collective-permute-done | bytes 20512 | tf_op jit(solution)/shard_map/ppermute | solution.py:671
  65.7 0.0 copy-done.2
  65.7 1.1 %shard_map.148 = (f32[16,256]{1,0:T(8,128)S(1)}, f32[8,256]{1,0:T(8,128)S(1)}, f32[1,4608]{1,0:T(1,128)}, f32[1,288]{1,0:T(1,128)}) custom-call(f32[256,128]{1,0:T(8,128)S(1)} %get-tuple-element.69.dx_ref, bf16[80,128]{1,0:T(8,128)(2,1)S(1)} %collective-permute-done.6.next_ref, bf16[80,128]{1,0:T(8,128)(2,1)S(1)} %collective-permute-done.7.prev_ref, ...), custom_call_target="tpu_custom_call" | custom-call | bytes 523392 | tf_op jit(solution)/shard_map/pallas_call | solution.py:654
  66.8 0.1 collective-permute-start.8
  66.8 9.4 %all-to-all-start.2 = ((bf16[16,16,128]{2,1,0:T(8,128)(2,1)}), bf16[16,16,128]{2,1,0:T(8,128)(2,1)S(1)}, u32[]{:S(2)}, u32[]{:S(2)}) async-start(bf16[16,16,128]{2,1,0:T(8,128)(2,1)} %get-tuple-element.78), calls=%async_computation.2 | async-start | bytes 131072 | tf_op jit(solution)/shard_map/all_to_all | solution.py:774
  76.3 0.0 collective-permute-done.8
  76.3 0.6 add_bitcast_fusion
  76.9 6.7 %all-to-all-done.2 = bf16[16,16,128]{2,1,0:T(8,128)(2,1)S(1)} async-done(((bf16[16,16,128]{2,1,0:T(8,128)(2,1)}), bf16[16,16,128]{2,1,0:T(8,128)(2,1)S(1)}, u32[]{:S(2)}, u32[]{:S(2)}) %all-to-all-start.2) | async-done | bytes 65568 | tf_op jit(solution)/shard_map/all_to_all | solution.py:774
  83.6 1.1 %shard_map.149 = f32[216,256]{1,0:T(8,128)} custom-call(bf16[256,128]{1,0:T(8,128)(2,1)S(1)} %bitcast.25, bf16[512,256]{1,0:T(8,128)(2,1)S(1)} %get-tuple-element.73.bank_ref), custom_call_target="tpu_custom_call" | custom-call | bytes 548864 | tf_op jit(solution)/shard_map/pallas_call | solution.py:654
  (1 shorter events, 0.0 us)
Async XLA Ops:
  2.0 11.6 %all-to-all-start = ((bf16[8,32,256]{2,1,0:T(8,128)(2,1)}), bf16[8,32,256]{2,1,0:T(8,128)(2,1)S(1)}, u32[]{:S(2)}, u32[]{:S(2)}) async-start(bf16[8,32,256]{2,1,0:T(8,128)(2,1)} %shard_map.137), calls=%async_computation | async-start | bytes 262144 | tf_op jit(solution)/shard_map/all_to_all | solution.py:686
  14.1 8.7 %collective-permute-start = (bf16[80,128]{1,0:T(8,128)(2,1)S(1)}, bf16[80,128]{1,0:T(8,128)(2,1)S(1)}, u32[]{:S(2)}, u32[]{:S(2)}) collective-permute-start(bf16[80,128]{1,0:T(8,128)(2,1)S(1)} %get-tuple-element.82), channel_id=1, source_target_pairs={{0,4},{1,5},{2,6},{3,7},{4,8},{5,9},{6,10},{7,11},{8,12},{9,13},{1... | collective-permute-start | bytes 61448 | tf_op jit(solution)/shard_map/ppermute | solution.py:671
  15.1 7.7 %collective-permute-start.1 = (bf16[80,128]{1,0:T(8,128)(2,1)S(1)}, bf16[80,128]{1,0:T(8,128)(2,1)S(1)}, u32[]{:S(2)}, u32[]{:S(2)}) collective-permute-start(bf16[80,128]{1,0:T(8,128)(2,1)S(1)} %get-tuple-element.81), channel_id=1, source_target_pairs={{0,124},{1,125},{2,126},{3,127},{4,0},{5,1},{6,2},{7,3},{8,4},{9,5... | collective-permute-start | bytes 61448 | tf_op jit(solution)/shard_map/ppermute | solution.py:671
  22.8 6.3 %copy-start = (s32[1,216,64]{1,2,0:T(8,128)S(1)}, s32[1,216,64]{1,2,0:T(8,128)}, u32[]{:S(2)}) copy-start(s32[1,216,64]{1,2,0:T(8,128)} %param.17) | copy-start | bytes 165892
  22.8 6.3 %copy-start.1 = (s32[1,2304,4]{1,2,0:T(4,128)S(1)}, s32[1,2304,4]{1,2,0:T(4,128)}, u32[]{:S(2)}) copy-start(s32[1,2304,4]{1,2,0:T(4,128)} %param.19) | copy-start | bytes 110596
  24.1 6.7 %collective-permute-start.2 = (bf16[160,256]{1,0:T(8,128)(2,1)S(1)}, bf16[160,256]{1,0:T(8,128)(2,1)S(1)}, u32[]{:S(2)}, u32[]{:S(2)}) collective-permute-start(bf16[160,256]{1,0:T(8,128)(2,1)S(1)} %get-tuple-element.49), channel_id=1, source_target_pairs={{0,4},{1,5},{2,6},{3,7},{4,8},{5,9},{6,10},{7,11},{8,12},{9,13},{1... | collective-permute-start | bytes 245768 | tf_op jit(solution)/shard_map/ppermute | solution.py:671
  24.2 6.6 %collective-permute-start.3 = (bf16[160,256]{1,0:T(8,128)(2,1)S(1)}, bf16[160,256]{1,0:T(8,128)(2,1)S(1)}, u32[]{:S(2)}, u32[]{:S(2)}) collective-permute-start(bf16[160,256]{1,0:T(8,128)(2,1)S(1)} %get-tuple-element.50), channel_id=1, source_target_pairs={{0,124},{1,125},{2,126},{3,127},{4,0},{5,1},{6,2},{7,3},{8,4},{9,5... | collective-permute-start | bytes 245768 | tf_op jit(solution)/shard_map/ppermute | solution.py:671
  34.4 7.7 %collective-permute-start.4 = (bf16[160,256]{1,0:T(8,128)(2,1)S(1)}, bf16[160,256]{1,0:T(8,128)(2,1)S(1)}, u32[]{:S(2)}, u32[]{:S(2)}) collective-permute-start(bf16[160,256]{1,0:T(8,128)(2,1)S(1)} %get-tuple-element.55), channel_id=1, source_target_pairs={{0,4},{1,5},{2,6},{3,7},{4,8},{5,9},{6,10},{7,11},{8,12},{9,13},{1... | collective-permute-start | bytes 245768 | tf_op jit(solution)/shard_map/ppermute | solution.py:671
  34.5 7.6 %collective-permute-start.5 = (bf16[160,256]{1,0:T(8,128)(2,1)S(1)}, bf16[160,256]{1,0:T(8,128)(2,1)S(1)}, u32[]{:S(2)}, u32[]{:S(2)}) collective-permute-start(bf16[160,256]{1,0:T(8,128)(2,1)S(1)} %get-tuple-element.56), channel_id=1, source_target_pairs={{0,124},{1,125},{2,126},{3,127},{4,0},{5,1},{6,2},{7,3},{8,4},{9,5... | collective-permute-start | bytes 245768 | tf_op jit(solution)/shard_map/ppermute | solution.py:671
  42.2 9.5 %copy-start.3 = (bf16[1,16,256]{2,1,0:T(8,128)(2,1)S(1)}, bf16[1,16,256]{2,1,0:T(8,128)(2,1)}, u32[]{:S(2)}) copy-start(bf16[1,16,256]{2,1,0:T(8,128)(2,1)} %param.10) | copy-start | bytes 24580
  42.2 9.5 %copy-start.4 = (s32[256]{0:T(256)S(1)}, s32[256]{0:T(256)}, u32[]{:S(2)}) copy-start(s32[256]{0:T(256)} %param.12) | copy-start | bytes 3076
  45.9 15.7 %all-to-all-start.1 = ((bf16[32,40,128]{2,1,0:T(8,128)(2,1)}), bf16[32,40,128]{2,1,0:T(8,128)(2,1)S(1)}, u32[]{:S(2)}, u32[]{:S(2)}) async-start(bf16[32,40,128]{2,1,0:T(8,128)(2,1)} %get-tuple-element.74), calls=%async_computation.1 | async-start | bytes 655360 | tf_op jit(solution)/shard_map/all_to_all | solution.py:757
  51.6 14.1 %copy-start.2 = (bf16[1,16,256]{2,1,0:T(8,128)(2,1)S(1)}, bf16[1,16,256]{2,1,0:T(8,128)(2,1)}, u32[]{:S(2)}) copy-start(bf16[1,16,256]{2,1,0:T(8,128)(2,1)} %param.11) | copy-start | bytes 24580
  54.6 7.6 %collective-permute-start.6 = (bf16[80,128]{1,0:T(8,128)(2,1)S(1)}, bf16[80,128]{1,0:T(8,128)(2,1)S(1)}, u32[]{:S(2)}, u32[]{:S(2)}) collective-permute-start(bf16[80,128]{1,0:T(8,128)(2,1)S(1)} %get-tuple-element.70), channel_id=1, source_target_pairs={{0,124},{1,125},{2,126},{3,127},{4,0},{5,1},{6,2},{7,3},{8,4},{9,5... | collective-permute-start | bytes 61448 | tf_op jit(solution)/shard_map/ppermute | solution.py:671
  59.3 6.5 %collective-permute-start.7 = (bf16[80,128]{1,0:T(8,128)(2,1)S(1)}, bf16[80,128]{1,0:T(8,128)(2,1)S(1)}, u32[]{:S(2)}, u32[]{:S(2)}) collective-permute-start(bf16[80,128]{1,0:T(8,128)(2,1)S(1)} %get-tuple-element.71), channel_id=1, source_target_pairs={{0,4},{1,5},{2,6},{3,7},{4,8},{5,9},{6,10},{7,11},{8,12},{9,13},{1... | collective-permute-start | bytes 61448 | tf_op jit(solution)/shard_map/ppermute | solution.py:671
  66.8 9.5 %collective-permute-start.8 = (f32[8,256]{1,0:T(8,128)S(1)}, f32[8,256]{1,0:T(8,128)S(1)}, u32[]{:S(2)}, u32[]{:S(2)}) collective-permute-start(f32[8,256]{1,0:T(8,128)S(1)} %get-tuple-element.77), channel_id=1, source_target_pairs={{0,128},{128,0},{1,129},{129,1},{2,130},{130,2},{3,131},{131,3},{4... | collective-permute-start | bytes 24584 | tf_op jit(solution)/shard_map/ppermute | solution.py:781
  66.8 16.7 %all-to-all-start.2 = ((bf16[16,16,128]{2,1,0:T(8,128)(2,1)}), bf16[16,16,128]{2,1,0:T(8,128)(2,1)S(1)}, u32[]{:S(2)}, u32[]{:S(2)}) async-start(bf16[16,16,128]{2,1,0:T(8,128)(2,1)} %get-tuple-element.78), calls=%async_computation.2 | async-start | bytes 131072 | tf_op jit(solution)/shard_map/all_to_all | solution.py:774

commit v6 on v5

--- a/solution.py
+++ b/solution.py
@@ -375,10 +375,28 @@
         two_ref[OUT_GATES + 16 * tap : OUT_GATES + 16 * (tap + 1)] = gates[:, HID * tap : HID * (tap + 1)]
 
 
-def prepare_last_kernel(early_ref, middle_ref, first_gates_ref, out_gates_ref, act_ref, three_ref, slope_ref):
+def prepare_last_kernel(early_ref, middle_ref, first_gates_ref, out_gates_ref, act_ref,
+    three_ref, slope_ref, pick_ref, pick_out_ref, pick_first_ref):
     slope_ref[...] = slope(act_ref[...])
     col = lax.axis_index(("xh", "core"))
     tile = lax.axis_index(FACE)
+    shape = (16 * CHUNK, 1152)
+    place = lax.broadcasted_iota(jnp.int32, shape, 0)
+    block = (place * 2731) >> 16
+    inside = place - CHUNK * block
+    ahead = lax.broadcasted_iota(jnp.int32, shape, 1) - (72 * block + 18 * col)
+    pick_ref[...] = ((ahead == inside) & (inside < 18)).astype(F32).astype(BF)
+    late = ahead - 9 * (inside - 18)
+    pick_out_ref[...] = ((late >= 0) & (late < 9) & (inside >= 18) & (inside < 20)).astype(F32).astype(BF)
+    shape = (4 * SHARE, 3 * PADC)
+    place = lax.broadcasted_iota(jnp.int32, shape, 0)
+    inside = place & 15
+    wanted = 14 * (4 * (place >> 4) + col) + inside
+    tap = (wanted * 2731) >> 16
+    third = (tap * 11) >> 5
+    target = PADC * third + 32 * (tap - 3 * third) + wanted - DEPTH * tap
+    real = (inside < 14) & (wanted < 9 * DEPTH)
+    pick_first_ref[...] = ((lax.broadcasted_iota(jnp.int32, shape, 1) == target) & real).astype(F32).astype(BF)
     three_ref[GIVE_OWN : GIVE_OWN + CELLS] = early_ref[pl.ds(pl.multiple_of(GIVE + CELLS * col, CELLS), CELLS)]
     count = 9 * DEPTH
     gates = first_gates_ref[...].astype(F32).astype(BF)
@@ -476,31 +494,13 @@
         flat_ref[64:128, cols] = high.astype(BF)
 
 
-def mid_term_kernel(filled_ref, grad_ref, middle_ref, part_ref, pick_out_ref, pick_first_ref, flat_ref):
-    col = lax.axis_index(("xh", "core"))
+def mid_term_kernel(filled_ref, grad_ref, middle_ref, pick_ref, part_ref, flat_ref):
     term_pairs(
         filled_ref, grad_ref[...], lambda a: bank_gates(middle_ref, MID_GATES, 64, range(3 * a, 3 * a + 3)), flat_ref
     )
-    shape = (16 * CHUNK, 1152)
-    place = lax.broadcasted_iota(jnp.int32, shape, 0)
-    block = (place * 2731) >> 16
-    inside = place - CHUNK * block
-    ahead = lax.broadcasted_iota(jnp.int32, shape, 1) - (72 * block + 18 * col)
-    pick = ((ahead == inside) & (inside < 18)).astype(F32).astype(BF)
-    late = ahead - 9 * (inside - 18)
-    pick_out_ref[...] = ((late >= 0) & (late < 9) & (inside >= 18) & (inside < 20)).astype(F32).astype(BF)
-    shape = (4 * SHARE, 3 * PADC)
-    place = lax.broadcasted_iota(jnp.int32, shape, 0)
-    inside = place & 15
-    wanted = 14 * (4 * (place >> 4) + col) + inside
-    tap = (wanted * 2731) >> 16
-    third = (tap * 11) >> 5
-    target = PADC * third + 32 * (tap - 3 * third) + wanted - DEPTH * tap
-    real = (inside < 14) & (wanted < 9 * DEPTH)
-    pick_first_ref[...] = ((lax.broadcasted_iota(jnp.int32, shape, 1) == target) & real).astype(F32).astype(BF)
     for half in range(2):
         part_ref[16 * CHUNK * half : 16 * CHUNK * (half + 1)] = dot_nt(
-            pick, flat_ref[:, 1152 * half : 1152 * (half + 1)]
+            pick_ref[...], flat_ref[:, 1152 * half : 1152 * (half + 1)]
         )
 
 
@@ -530,8 +530,9 @@
         low, high = kept_pair([term[8 * m : 8 * (m + 1)] for m in range(4)], gates)
         pair = low + pltpu.roll(high, 4, 0)
         wide = jnp.broadcast_to(pair[None], (16, 8, width)).reshape(128, width)
-        kernel_row = lax.broadcasted_iota(jnp.int32, (128, width), 1) + width * a
+        kernel_row = lax.broadcasted_iota(jnp.int32, (8, width), 1) + width * a
         slot = kernel_row - 9 * ((kernel_row * 7282) >> 16)
+        slot = jnp.broadcast_to(slot[None], (16, 8, width)).reshape(128, width)
         mine = (lax.broadcasted_iota(jnp.int32, (128, width), 0) >> 3) == slot
         flat_ref[:, cols] = jnp.where(mine, wide, 0.0).astype(BF)
     gates = [
@@ -722,8 +723,9 @@
     prev_one = row_shift(up_one, 1)
     next_one = row_shift(down_one, -1)
 
-    three, slope_one = call(
-        prepare_last_kernel, [sds((BANK_THREE, HID), BF), sds((LINE, HID), F32)],
+    three, slope_one, pick_mid, pick_out, pick_first = call(
+        prepare_last_kernel, [sds((BANK_THREE, HID), BF), sds((LINE, HID), F32), sds((16 * CHUNK, 1152), BF), sds((16 * CHUNK, 1152), BF),
+         sds((4 * SHARE, 3 * PADC), BF)],
         [early, middle, first_turned, out_turned, act_one], flops=10**9,
     )
 
@@ -736,12 +738,12 @@
     prev_two = row_shift(up_two, 1)
     next_two = row_shift(down_two, -1)
 
-    part, pick_out, pick_first = call(
+    part = call(
         mid_term_kernel,
-        [sds((32 * CHUNK, PADC), F32), sds((16 * CHUNK, 1152), BF), sds((4 * SHARE, 3 * PADC), BF)],
-        [filled_one, grad_two, middle],
+        [sds((32 * CHUNK, PADC), F32)],
+        [filled_one, grad_two, middle, pick_mid],
         scratch=[pltpu.VMEM((PADC, 9 * HID), BF)], flops=2 * 10**9,
-    )
+    )[0]
 
     buffer, mine_two, grad_one = call(
         terms_kernel,

time: 85.2 us -> 90.3 us (1.060)
  waiting for transfers between devices: 15.3 us -> 19.6 us
    ppermute x8, waiting for transfers between devices: 4.22 us -> 8.47 us  [row_shift(): return lax.ppermute(value, FACE, pairs)]
where the time goes in v6:
time: 90.3 us; the launch traced here: 89.8 us
  starting transfers between devices  44.4 us (49%)
  Pallas kernels  24.4 us (27%)
  waiting for transfers between devices  19.6 us (22%)
    pallas_call x13, Pallas kernels, call(): pl.pallas_call(body, out_shape=[jax.ShapeDtypeStruct(item.shape, item.dty...  24.4 us
    ppermute x8, starting transfers between devices, row_shift(): return lax.ppermute(value, FACE, pairs)  21.9 us
    all_to_all x1, starting transfers between devices, body(): lax.all_to_all(shared, ('y', 'xh', 'core'), 0, 0).reshape(16 * SHARE, PADC)  9.73 us
    ppermute x8, waiting for transfers between devices, row_shift(): return lax.ppermute(value, FACE, pairs)  8.47 us
    all_to_all x1, waiting for transfers between devices, body(): lax.all_to_all(shared, ('y', 'xh', 'core'), 0, 0).reshape(16 * SHARE, PADC)  6.71 us
    all_to_all x1, starting transfers between devices, body(): lax.all_to_all(packed, LINE_AXES, 0, 0).reshape(2, ROW, 2 * FIELDS, CELLS)  6.49 us
    all_to_all x1, starting transfers between devices, body(): spread = lax.all_to_all(buffer, ROW_AXES, 0, 0)  6.13 us
    all_to_all x1, waiting for transfers between devices, body(): spread = lax.all_to_all(buffer, ROW_AXES, 0, 0)  2.26 us
  transfers between devices with their start and end apart: 12, of which 5 were waited for; matrix products, arithmetic and copies ran while one was open for 1% of the time, Pallas kernels for 13%

profile of v6, /device:TPU:1, one launch (start us, length us, event | category | flops | bytes accessed | tf_op | source)
XLA Modules:
  0.0 89.8 jit_solution(10200237026783141528)
XLA Ops:
  0.6 1.4 %shard_map.137 = bf16[8,32,256]{2,1,0:T(8,128)(2,1)} custom-call(bf16[16,256]{1,0:T(8,128)(2,1)} %bitcast.34, bf16[16,256]{1,0:T(8,128)(2,1)} %bitcast.32, s32[1,256]{1,0:T(1,128)} %bitcast.36), custom_call_target="tpu_custom_call" | custom-call | bytes 148480 | tf_op jit(solution)/shard_map/pallas_call | solution.py:655
  2.0 6.5 %all-to-all-start = ((bf16[8,32,256]{2,1,0:T(8,128)(2,1)}), bf16[8,32,256]{2,1,0:T(8,128)(2,1)S(1)}, u32[]{:S(2)}, u32[]{:S(2)}) async-start(bf16[8,32,256]{2,1,0:T(8,128)(2,1)} %shard_map.137), calls=%async_computation | async-start | bytes 262144 | tf_op jit(solution)/shard_map/all_to_all | solution.py:687
  8.5 3.0 %shard_map.138 = (bf16[2816,256]{1,0:T(8,128)(2,1)S(1)}, bf16[2880,256]{1,0:T(8,128)(2,1)S(1)}) custom-call(s32[4,128]{1,0:T(4,128)} %bitcast.43, s32[64,216]{1,0:T(8,128)} %bitcast.26, s32[4,2304]{1,0:T(4,128)} %bitcast.29, bf16[216,256]{1,0:T(8,128)(2,1)} %bitcast.41, bf16[16,2304]{1,0:T(8,128)(2,1)} %bitcast.42, s32[64,2304]{1,0:T(8,128)} %bitcast.40, ...), custom_call_target="tpu_custom_call" | custom-call | flops 5000000000 | bytes 4964352 | tf_op jit(solution)/shard_map/pallas_call | solution.py:655
  11.5 2.2 %all-to-all-done = bf16[8,32,256]{2,1,0:T(8,128)(2,1)S(1)} async-done(((bf16[8,32,256]{2,1,0:T(8,128)(2,1)}), bf16[8,32,256]{2,1,0:T(8,128)(2,1)S(1)}, u32[]{:S(2)}, u32[]{:S(2)}) %all-to-all-start) | async-done | bytes 131104 | tf_op jit(solution)/shard_map/all_to_all | solution.py:687
  13.7 0.4 shard_map.139
  14.1 7.4 %collective-permute-start.1 = (bf16[80,128]{1,0:T(8,128)(2,1)S(1)}, bf16[80,128]{1,0:T(8,128)(2,1)S(1)}, u32[]{:S(2)}, u32[]{:S(2)}) collective-permute-start(bf16[80,128]{1,0:T(8,128)(2,1)S(1)} %get-tuple-element.81), channel_id=1, source_target_pairs={{0,124},{1,125},{2,126},{3,127},{4,0},{5,1},{6,2},{7,3},{8,4},{9,5... | collective-permute-start | bytes 61448 | tf_op jit(solution)/shard_map/ppermute | solution.py:672
  21.5 0.0 collective-permute-start
  21.5 1.1 %shard_map.141.bank_ref = bf16[2576,256]{1,0:T(8,128)(2,1)S(1)} custom-call(bf16[2880,256]{1,0:T(8,128)(2,1)S(1)} %get-tuple-element.52.middle_ref, s32[64,216]{1,0:T(8,128)} %bitcast.27, s32[4,2304]{1,0:T(4,128)} %bitcast.30), custom_call_target="tpu_custom_call" | custom-call | flops 1000000000 | bytes 2885632 | tf_op jit(solution)/shard_map/pallas_call | solution.py:655
  22.7 0.0 copy-start
  22.7 0.0 copy-start.1
  22.7 0.0 collective-permute-done.1.next_ref
  22.7 4.8 %collective-permute-done.prev_ref = bf16[80,128]{1,0:T(8,128)(2,1)S(1)} collective-permute-done((bf16[80,128]{1,0:T(8,128)(2,1)S(1)}, bf16[80,128]{1,0:T(8,128)(2,1)S(1)}, u32[]{:S(2)}, u32[]{:S(2)}) %collective-permute-start) | collective-permute-done | bytes 20512 | tf_op jit(solution)/shard_map/ppermute | solution.py:672
  27.5 1.3 %shard_map.140 = (bf16[4,18,16,128]{3,2,1,0:T(8,128)(2,1)S(1)}, f32[1024,256]{1,0:T(8,128)S(1)}, bf16[1024,256]{1,0:T(8,128)(2,1)S(1)}, bf16[192,256]{1,0:T(8,12...) custom-call(bf16[1024,128]{1,0:T(8,128)(2,1)S(1)} %get-tuple-element.44.field_ref, ...), custom_call_target="tpu_custom_call" | custom-call | bytes 5251072 | tf_op jit(solution)/shard_map/pallas_call | solution.py:655
  28.8 0.1 collective-permute-start.2
  28.9 4.8 %collective-permute-start.3 = (bf16[160,256]{1,0:T(8,128)(2,1)S(1)}, bf16[160,256]{1,0:T(8,128)(2,1)S(1)}, u32[]{:S(2)}, u32[]{:S(2)}) collective-permute-start(bf16[160,256]{1,0:T(8,128)(2,1)S(1)} %get-tuple-element.50), channel_id=1, source_target_pairs={{0,124},{1,125},{2,126},{3,127},{4,0},{5,1},{6,2},{7,3},{8,4},{9,5... | collective-permute-start | bytes 245768 | tf_op jit(solution)/shard_map/ppermute | solution.py:672
  33.6 0.0 copy-done
  33.6 0.0 copy-done.1
  33.6 1.9 %shard_map.143 = (bf16[512,256]{1,0:T(8,128)(2,1)S(1)}, f32[1024,256]{1,0:T(8,128)S(1)}, bf16[384,1152]{1,0:T(8,128)(2,1)S(1)}, bf16[384,1152]{1,0:T(8,128)(2,1)S(1)}, bf16[64,384]{1,0:T(8,128)(2,1)S(1)}) custom-call(bf16[2816,256]{1,0:T(8,128)(2,1)S(1)} %get-tuple-element.43.bank_ref.early_ref, bf16[2880,256]{1,0:T(8,128)(2,1)S(1)} %get-tuple-element.52.middle_ref, ...), custom_call_target="tpu_custom_call" | custom-call | flops 1000000000 | bytes 7186432 | tf_op jit(solution)/shard_map/pallas_call | solution.py:655
  35.5 0.0 collective-permute-done.2.prev_ref
  35.6 0.0 collective-permute-done.3.next_ref
  35.6 3.7 %shard_map.142 = (bf16[4,18,16,768]{3,2,1,0:T(8,128)(2,1)S(1)}, bf16[1024,256]{1,0:T(8,128)(2,1)S(1)}, bf16[1024,256]{1,0:T(8,128)(2,1)S(1)}, bf16[192,256]{1,0:...) custom-call(bf16[1024,256]{1,0:T(8,128)(2,1)S(1)} %get-tuple-element.47.hid_r, ...), custom_call_target="tpu_custom_call" | custom-call | bytes 10199040 | tf_op jit(solution)/shard_map/pallas_call | solution.py:655
  39.2 0.3 collective-permute-start.4
  39.5 4.8 %collective-permute-start.5 = (bf16[160,256]{1,0:T(8,128)(2,1)S(1)}, bf16[160,256]{1,0:T(8,128)(2,1)S(1)}, u32[]{:S(2)}, u32[]{:S(2)}) collective-permute-start(bf16[160,256]{1,0:T(8,128)(2,1)S(1)} %get-tuple-element.56), channel_id=1, source_target_pairs={{0,124},{1,125},{2,126},{3,127},{4,0},{5,1},{6,2},{7,3},{8,4},{9,5... | collective-permute-start | bytes 245768 | tf_op jit(solution)/shard_map/ppermute | solution.py:672
  44.3 2.1 %shard_map.144.part_ref = f32[768,128]{1,0:T(8,128)S(1)} custom-call(bf16[4,18,16,768]{3,2,1,0:T(8,128)(2,1)S(1)} %get-tuple-element.61.filled_ref, bf16[1024,256]{1,0:T(8,128)(2,1)S(1)} %get-tuple-element.62.grad_ref, bf16[2880,256]{1,0:T(8,128)(2,1)S(1)} %get-tuple-element.52.middle_ref, bf16[384,1152]{1,0:T(8,128)(2,1)S(1)} %get-tuple-element.63.pick_ref), custom_call_target="tpu_custom_call" | custom-call | flops 2000000000 | bytes 5046272 | tf_op jit(solution)/shard_map/pallas_call | solution.py:655
  46.4 0.0 collective-permute-done.4.prev_ref
  46.4 0.0 collective-permute-done.5.next_ref
  46.4 0.0 copy-start.3
  46.4 0.0 copy-start.4
  46.4 3.7 %shard_map.145 = (bf16[32,40,128]{2,1,0:T(8,128)(2,1)}, bf16[18,16,768]{2,1,0:T(8,128)(2,1)S(1)}, bf16[1024,256]{1,0:T(8,128)(2,1)S(1)}) custom-call(bf16[1024,256]{1,0:T(8,128)(2,1)S(1)} %get-tuple-element.53.hid_two_ref, bf16[192,256]{1,0:T(8,128)(2,1)S(1)} %get-tuple-element.54.local_ref, bf16[160,256]{1,0:T(8,128)(2,1)S(1)} %collective-permute-done.4.prev_ref, ...), custom_call_target="tpu_custom_call" | custom-call | bytes 8822784 | tf_op jit(solution)/shard_map/pallas_call | solution.py:655
  50.1 6.1 %all-to-all-start.1 = ((bf16[32,40,128]{2,1,0:T(8,128)(2,1)}), bf16[32,40,128]{2,1,0:T(8,128)(2,1)S(1)}, u32[]{:S(2)}, u32[]{:S(2)}) async-start(bf16[32,40,128]{2,1,0:T(8,128)(2,1)} %get-tuple-element.74), calls=%async_computation.1 | async-start | bytes 655360 | tf_op jit(solution)/shard_map/all_to_all | solution.py:759
  56.3 0.0 copy-done.3
  56.3 0.0 copy-done.4
  56.3 0.0 copy-start.2
  56.3 3.0 %shard_map.146 = (bf16[16,256]{1,0:T(8,128)(2,1)}, f32[256,128]{1,0:T(8,128)S(1)}, bf16[80,128]{1,0:T(8,128)(2,1)S(1)}, bf16[80,128]{1,0:T(8,128)(2,1)S(1)}, bf16[96,128]{1,0:T(8,128)(2,1)S(1)}) custom-call(bf16[18,16,768]{2,1,0:T(8,128)(2,1)S(1)} %get-tuple-element.66.mine_ref, bf16[1024,256]{1,0:T(8,128)(2,1)S(1)} %get-tuple-element.67.grad_ref, ...), custom_call_target="tpu_custom_call" | custom-call | flops 2000000000 | bytes 2622464 | tf_op jit(solution)/shard_map/pallas_call | solution.py:655
  59.3 4.6 %collective-permute-start.6 = (bf16[80,128]{1,0:T(8,128)(2,1)S(1)}, bf16[80,128]{1,0:T(8,128)(2,1)S(1)}, u32[]{:S(2)}, u32[]{:S(2)}) collective-permute-start(bf16[80,128]{1,0:T(8,128)(2,1)S(1)} %get-tuple-element.70), channel_id=1, source_target_pairs={{0,124},{1,125},{2,126},{3,127},{4,0},{5,1},{6,2},{7,3},{8,4},{9,5... | collective-permute-start | bytes 61448 | tf_op jit(solution)/shard_map/ppermute | solution.py:672
  63.9 0.0 collective-permute-start.7
  63.9 2.3 %all-to-all-done.1.spread_ref = bf16[32,40,128]{2,1,0:T(8,128)(2,1)S(1)} async-done(((bf16[32,40,128]{2,1,0:T(8,128)(2,1)}), bf16[32,40,128]{2,1,0:T(8,128)(2,1)S(1)}, u32[]{:S(2)}, u32[]{:S(2)}) %all-to-all-start.1) | async-done | bytes 327712 | tf_op jit(solution)/shard_map/all_to_all | solution.py:759
  66.2 0.7 shard_map.147
  66.9 0.0 collective-permute-done.6.next_ref
  66.9 3.7 %collective-permute-done.7.prev_ref = bf16[80,128]{1,0:T(8,128)(2,1)S(1)} collective-permute-done((bf16[80,128]{1,0:T(8,128)(2,1)S(1)}, bf16[80,128]{1,0:T(8,128)(2,1)S(1)}, u32[]{:S(2)}, u32[]{:S(2)}) %collective-permute-start.7) | collective-permute-done | bytes 20512 | tf_op jit(solution)/shard_map/ppermute | solution.py:672
  70.5 0.0 copy-done.2
  70.5 1.1 %shard_map.148 = (f32[16,256]{1,0:T(8,128)S(1)}, f32[8,256]{1,0:T(8,128)S(1)}, f32[1,4608]{1,0:T(1,128)}, f32[1,288]{1,0:T(1,128)}) custom-call(f32[256,128]{1,0:T(8,128)S(1)} %get-tuple-element.69.dx_ref, bf16[80,128]{1,0:T(8,128)(2,1)S(1)} %collective-permute-done.6.next_ref, bf16[80,128]{1,0:T(8,128)(2,1)S(1)} %collective-permute-done.7.prev_ref, ...), custom_call_target="tpu_custom_call" | custom-call | bytes 523392 | tf_op jit(solution)/shard_map/pallas_call | solution.py:655
  71.6 0.1 collective-permute-start.8
  71.7 9.7 %all-to-all-start.2 = ((bf16[16,16,128]{2,1,0:T(8,128)(2,1)}), bf16[16,16,128]{2,1,0:T(8,128)(2,1)S(1)}, u32[]{:S(2)}, u32[]{:S(2)}) async-start(bf16[16,16,128]{2,1,0:T(8,128)(2,1)} %get-tuple-element.78), calls=%async_computation.2 | async-start | bytes 131072 | tf_op jit(solution)/shard_map/all_to_all | solution.py:776
  81.4 0.0 collective-permute-done.8
  81.4 0.6 add_bitcast_fusion
  82.1 6.7 %all-to-all-done.2 = bf16[16,16,128]{2,1,0:T(8,128)(2,1)S(1)} async-done(((bf16[16,16,128]{2,1,0:T(8,128)(2,1)}), bf16[16,16,128]{2,1,0:T(8,128)(2,1)S(1)}, u32[]{:S(2)}, u32[]{:S(2)}) %all-to-all-start.2) | async-done | bytes 65568 | tf_op jit(solution)/shard_map/all_to_all | solution.py:776
  88.8 1.1 %shard_map.149 = f32[216,256]{1,0:T(8,128)} custom-call(bf16[256,128]{1,0:T(8,128)(2,1)S(1)} %bitcast.25, bf16[512,256]{1,0:T(8,128)(2,1)S(1)} %get-tuple-element.73.bank_ref), custom_call_target="tpu_custom_call" | custom-call | bytes 548864 | tf_op jit(solution)/shard_map/pallas_call | solution.py:655
  (1 shorter events, 0.0 us)
Async XLA Ops:
  2.0 11.6 %all-to-all-start = ((bf16[8,32,256]{2,1,0:T(8,128)(2,1)}), bf16[8,32,256]{2,1,0:T(8,128)(2,1)S(1)}, u32[]{:S(2)}, u32[]{:S(2)}) async-start(bf16[8,32,256]{2,1,0:T(8,128)(2,1)} %shard_map.137), calls=%async_computation | async-start | bytes 262144 | tf_op jit(solution)/shard_map/all_to_all | solution.py:687
  14.1 8.6 %collective-permute-start.1 = (bf16[80,128]{1,0:T(8,128)(2,1)S(1)}, bf16[80,128]{1,0:T(8,128)(2,1)S(1)}, u32[]{:S(2)}, u32[]{:S(2)}) collective-permute-start(bf16[80,128]{1,0:T(8,128)(2,1)S(1)} %get-tuple-element.81), channel_id=1, source_target_pairs={{0,124},{1,125},{2,126},{3,127},{4,0},{5,1},{6,2},{7,3},{8,4},{9,5... | collective-permute-start | bytes 61448 | tf_op jit(solution)/shard_map/ppermute | solution.py:672
  21.5 6.0 %collective-permute-start = (bf16[80,128]{1,0:T(8,128)(2,1)S(1)}, bf16[80,128]{1,0:T(8,128)(2,1)S(1)}, u32[]{:S(2)}, u32[]{:S(2)}) collective-permute-start(bf16[80,128]{1,0:T(8,128)(2,1)S(1)} %get-tuple-element.82), channel_id=1, source_target_pairs={{0,4},{1,5},{2,6},{3,7},{4,8},{5,9},{6,10},{7,11},{8,12},{9,13},{1... | collective-permute-start | bytes 61448 | tf_op jit(solution)/shard_map/ppermute | solution.py:672
  22.7 11.0 %copy-start = (s32[1,216,64]{1,2,0:T(8,128)S(1)}, s32[1,216,64]{1,2,0:T(8,128)}, u32[]{:S(2)}) copy-start(s32[1,216,64]{1,2,0:T(8,128)} %param.17) | copy-start | bytes 165892
  22.7 10.9 %copy-start.1 = (s32[1,2304,4]{1,2,0:T(4,128)S(1)}, s32[1,2304,4]{1,2,0:T(4,128)}, u32[]{:S(2)}) copy-start(s32[1,2304,4]{1,2,0:T(4,128)} %param.19) | copy-start | bytes 110596
  28.8 6.8 %collective-permute-start.2 = (bf16[160,256]{1,0:T(8,128)(2,1)S(1)}, bf16[160,256]{1,0:T(8,128)(2,1)S(1)}, u32[]{:S(2)}, u32[]{:S(2)}) collective-permute-start(bf16[160,256]{1,0:T(8,128)(2,1)S(1)} %get-tuple-element.49), channel_id=1, source_target_pairs={{0,4},{1,5},{2,6},{3,7},{4,8},{5,9},{6,10},{7,11},{8,12},{9,13},{1... | collective-permute-start | bytes 245768 | tf_op jit(solution)/shard_map/ppermute | solution.py:672
  28.9 6.7 %collective-permute-start.3 = (bf16[160,256]{1,0:T(8,128)(2,1)S(1)}, bf16[160,256]{1,0:T(8,128)(2,1)S(1)}, u32[]{:S(2)}, u32[]{:S(2)}) collective-permute-start(bf16[160,256]{1,0:T(8,128)(2,1)S(1)} %get-tuple-element.50), channel_id=1, source_target_pairs={{0,124},{1,125},{2,126},{3,127},{4,0},{5,1},{6,2},{7,3},{8,4},{9,5... | collective-permute-start | bytes 245768 | tf_op jit(solution)/shard_map/ppermute | solution.py:672
  39.2 7.2 %collective-permute-start.4 = (bf16[160,256]{1,0:T(8,128)(2,1)S(1)}, bf16[160,256]{1,0:T(8,128)(2,1)S(1)}, u32[]{:S(2)}, u32[]{:S(2)}) collective-permute-start(bf16[160,256]{1,0:T(8,128)(2,1)S(1)} %get-tuple-element.55), channel_id=1, source_target_pairs={{0,4},{1,5},{2,6},{3,7},{4,8},{5,9},{6,10},{7,11},{8,12},{9,13},{1... | collective-permute-start | bytes 245768 | tf_op jit(solution)/shard_map/ppermute | solution.py:672
  39.5 6.9 %collective-permute-start.5 = (bf16[160,256]{1,0:T(8,128)(2,1)S(1)}, bf16[160,256]{1,0:T(8,128)(2,1)S(1)}, u32[]{:S(2)}, u32[]{:S(2)}) collective-permute-start(bf16[160,256]{1,0:T(8,128)(2,1)S(1)} %get-tuple-element.56), channel_id=1, source_target_pairs={{0,124},{1,125},{2,126},{3,127},{4,0},{5,1},{6,2},{7,3},{8,4},{9,5... | collective-permute-start | bytes 245768 | tf_op jit(solution)/shard_map/ppermute | solution.py:672
  46.4 9.9 %copy-start.3 = (bf16[1,16,256]{2,1,0:T(8,128)(2,1)S(1)}, bf16[1,16,256]{2,1,0:T(8,128)(2,1)}, u32[]{:S(2)}) copy-start(bf16[1,16,256]{2,1,0:T(8,128)(2,1)} %param.10) | copy-start | bytes 24580
  46.4 9.9 %copy-start.4 = (s32[256]{0:T(256)S(1)}, s32[256]{0:T(256)}, u32[]{:S(2)}) copy-start(s32[256]{0:T(256)} %param.12) | copy-start | bytes 3076
  50.1 16.1 %all-to-all-start.1 = ((bf16[32,40,128]{2,1,0:T(8,128)(2,1)}), bf16[32,40,128]{2,1,0:T(8,128)(2,1)S(1)}, u32[]{:S(2)}, u32[]{:S(2)}) async-start(bf16[32,40,128]{2,1,0:T(8,128)(2,1)} %get-tuple-element.74), calls=%async_computation.1 | async-start | bytes 655360 | tf_op jit(solution)/shard_map/all_to_all | solution.py:759
  56.3 14.3 %copy-start.2 = (bf16[1,16,256]{2,1,0:T(8,128)(2,1)S(1)}, bf16[1,16,256]{2,1,0:T(8,128)(2,1)}, u32[]{:S(2)}) copy-start(bf16[1,16,256]{2,1,0:T(8,128)(2,1)} %param.11) | copy-start | bytes 24580
  59.3 7.6 %collective-permute-start.6 = (bf16[80,128]{1,0:T(8,128)(2,1)S(1)}, bf16[80,128]{1,0:T(8,128)(2,1)S(1)}, u32[]{:S(2)}, u32[]{:S(2)}) collective-permute-start(bf16[80,128]{1,0:T(8,128)(2,1)S(1)} %get-tuple-element.70), channel_id=1, source_target_pairs={{0,124},{1,125},{2,126},{3,127},{4,0},{5,1},{6,2},{7,3},{8,4},{9,5... | collective-permute-start | bytes 61448 | tf_op jit(solution)/shard_map/ppermute | solution.py:672
  63.9 6.6 %collective-permute-start.7 = (bf16[80,128]{1,0:T(8,128)(2,1)S(1)}, bf16[80,128]{1,0:T(8,128)(2,1)S(1)}, u32[]{:S(2)}, u32[]{:S(2)}) collective-permute-start(bf16[80,128]{1,0:T(8,128)(2,1)S(1)} %get-tuple-element.71), channel_id=1, source_target_pairs={{0,4},{1,5},{2,6},{3,7},{4,8},{5,9},{6,10},{7,11},{8,12},{9,13},{1... | collective-permute-start | bytes 61448 | tf_op jit(solution)/shard_map/ppermute | solution.py:672
  71.6 9.8 %collective-permute-start.8 = (f32[8,256]{1,0:T(8,128)S(1)}, f32[8,256]{1,0:T(8,128)S(1)}, u32[]{:S(2)}, u32[]{:S(2)}) collective-permute-start(f32[8,256]{1,0:T(8,128)S(1)} %get-tuple-element.77), channel_id=1, source_target_pairs={{0,128},{128,0},{1,129},{129,1},{2,130},{130,2},{3,131},{131,3},{4... | collective-permute-start | bytes 24584 | tf_op jit(solution)/shard_map/ppermute | solution.py:783
  71.7 17.1 %all-to-all-start.2 = ((bf16[16,16,128]{2,1,0:T(8,128)(2,1)}), bf16[16,16,128]{2,1,0:T(8,128)(2,1)S(1)}, u32[]{:S(2)}, u32[]{:S(2)}) async-start(bf16[16,16,128]{2,1,0:T(8,128)(2,1)} %get-tuple-element.78), calls=%async_computation.2 | async-start | bytes 131072 | tf_op jit(solution)/shard_map/all_to_all | solution.py:776

commit v7 on v6

--- a/solution.py
+++ b/solution.py
@@ -483,6 +483,15 @@
     )
 
 
+def term_by_tile(turned, filled_ref, a):
+    total = None
+    for col in range(ROW):
+        tile = filled_ref[col, a : a + TS].reshape(CELLS, filled_ref.shape[3])
+        piece = dot(turned[:, CELLS * col : CELLS * (col + 1)], tile)
+        total = piece if total is None else total + piece
+    return total
+
+
 def term_pairs(filled_ref, grad, gates_of, flat_ref):
     turned = dot_nt(plane_order(), grad).astype(BF)
     width = filled_ref.shape[3]
@@ -525,7 +534,7 @@
     width = filled_ref.shape[3]
     for a in range(3):
         cols = slice(width * a, width * (a + 1))
-        term = dot(turned, gather_rows(filled_ref, a))
+        term = term_by_tile(turned, filled_ref, a)
         gates = bank_gates(bank_ref, OUT_GATES, 16, range(3 * a, 3 * a + 3)).astype(F32)[:8]
         low, high = kept_pair([term[8 * m : 8 * (m + 1)] for m in range(4)], gates)
         pair = low + pltpu.roll(high, 4, 0)

time: 90.3 us -> 90.3 us (level)
  no operation moved by 1% of the time
where the time goes in v7:
time: 90.3 us; the launch traced here: 89.8 us
  starting transfers between devices  44.4 us (49%)
  Pallas kernels  24.3 us (27%)
  waiting for transfers between devices  19.6 us (22%)
    pallas_call x13, Pallas kernels, call(): pl.pallas_call(body, out_shape=[jax.ShapeDtypeStruct(item.shape, item.dty...  24.3 us
    ppermute x8, starting transfers between devices, row_shift(): return lax.ppermute(value, FACE, pairs)  21.9 us
    all_to_all x1, starting transfers between devices, body(): lax.all_to_all(shared, ('y', 'xh', 'core'), 0, 0).reshape(16 * SHARE, PADC)  9.73 us
    ppermute x8, waiting for transfers between devices, row_shift(): return lax.ppermute(value, FACE, pairs)  8.48 us
    all_to_all x1, waiting for transfers between devices, body(): lax.all_to_all(shared, ('y', 'xh', 'core'), 0, 0).reshape(16 * SHARE, PADC)  6.71 us
    all_to_all x1, starting transfers between devices, body(): lax.all_to_all(packed, LINE_AXES, 0, 0).reshape(2, ROW, 2 * FIELDS, CELLS)  6.49 us
    all_to_all x1, starting transfers between devices, body(): spread = lax.all_to_all(buffer, ROW_AXES, 0, 0)  6.13 us
    all_to_all x1, waiting for transfers between devices, body(): spread = lax.all_to_all(buffer, ROW_AXES, 0, 0)  2.26 us
  transfers between devices with their start and end apart: 12, of which 5 were waited for; matrix products, arithmetic and copies ran while one was open for 1% of the time, Pallas kernels for 13%

profile of v7, /device:TPU:1, one launch (start us, length us, event | category | flops | bytes accessed | tf_op | source)
XLA Modules:
  0.0 89.8 jit_solution(3039863882437941891)
XLA Ops:
  0.6 1.4 %shard_map.137 = bf16[8,32,256]{2,1,0:T(8,128)(2,1)} custom-call(bf16[16,256]{1,0:T(8,128)(2,1)} %bitcast.34, bf16[16,256]{1,0:T(8,128)(2,1)} %bitcast.32, s32[1,256]{1,0:T(1,128)} %bitcast.36), custom_call_target="tpu_custom_call" | custom-call | bytes 148480 | tf_op jit(solution)/shard_map/pallas_call | solution.py:664
  2.0 6.5 %all-to-all-start = ((bf16[8,32,256]{2,1,0:T(8,128)(2,1)}), bf16[8,32,256]{2,1,0:T(8,128)(2,1)S(1)}, u32[]{:S(2)}, u32[]{:S(2)}) async-start(bf16[8,32,256]{2,1,0:T(8,128)(2,1)} %shard_map.137), calls=%async_computation | async-start | bytes 262144 | tf_op jit(solution)/shard_map/all_to_all | solution.py:696
  8.5 3.0 %shard_map.138 = (bf16[2816,256]{1,0:T(8,128)(2,1)S(1)}, bf16[2880,256]{1,0:T(8,128)(2,1)S(1)}) custom-call(s32[4,128]{1,0:T(4,128)} %bitcast.43, s32[64,216]{1,0:T(8,128)} %bitcast.26, s32[4,2304]{1,0:T(4,128)} %bitcast.29, bf16[216,256]{1,0:T(8,128)(2,1)} %bitcast.41, bf16[16,2304]{1,0:T(8,128)(2,1)} %bitcast.42, s32[64,2304]{1,0:T(8,128)} %bitcast.40, ...), custom_call_target="tpu_custom_call" | custom-call | flops 5000000000 | bytes 4964352 | tf_op jit(solution)/shard_map/pallas_call | solution.py:664
  11.5 2.2 %all-to-all-done = bf16[8,32,256]{2,1,0:T(8,128)(2,1)S(1)} async-done(((bf16[8,32,256]{2,1,0:T(8,128)(2,1)}), bf16[8,32,256]{2,1,0:T(8,128)(2,1)S(1)}, u32[]{:S(2)}, u32[]{:S(2)}) %all-to-all-start) | async-done | bytes 131104 | tf_op jit(solution)/shard_map/all_to_all | solution.py:696
  13.7 0.4 shard_map.139
  14.1 7.4 %collective-permute-start.1 = (bf16[80,128]{1,0:T(8,128)(2,1)S(1)}, bf16[80,128]{1,0:T(8,128)(2,1)S(1)}, u32[]{:S(2)}, u32[]{:S(2)}) collective-permute-start(bf16[80,128]{1,0:T(8,128)(2,1)S(1)} %get-tuple-element.81), channel_id=1, source_target_pairs={{0,124},{1,125},{2,126},{3,127},{4,0},{5,1},{6,2},{7,3},{8,4},{9,5... | collective-permute-start | bytes 61448 | tf_op jit(solution)/shard_map/ppermute | solution.py:681
  21.5 0.0 collective-permute-start
  21.5 1.1 %shard_map.141.bank_ref = bf16[2576,256]{1,0:T(8,128)(2,1)S(1)} custom-call(bf16[2880,256]{1,0:T(8,128)(2,1)S(1)} %get-tuple-element.52.middle_ref, s32[64,216]{1,0:T(8,128)} %bitcast.27, s32[4,2304]{1,0:T(4,128)} %bitcast.30), custom_call_target="tpu_custom_call" | custom-call | flops 1000000000 | bytes 2885632 | tf_op jit(solution)/shard_map/pallas_call | solution.py:664
  22.7 0.0 copy-start
  22.7 0.0 copy-start.1
  22.7 0.0 collective-permute-done.1.next_ref
  22.7 4.8 %collective-permute-done.prev_ref = bf16[80,128]{1,0:T(8,128)(2,1)S(1)} collective-permute-done((bf16[80,128]{1,0:T(8,128)(2,1)S(1)}, bf16[80,128]{1,0:T(8,128)(2,1)S(1)}, u32[]{:S(2)}, u32[]{:S(2)}) %collective-permute-start) | collective-permute-done | bytes 20512 | tf_op jit(solution)/shard_map/ppermute | solution.py:681
  27.5 1.3 %shard_map.140 = (bf16[4,18,16,128]{3,2,1,0:T(8,128)(2,1)S(1)}, f32[1024,256]{1,0:T(8,128)S(1)}, bf16[1024,256]{1,0:T(8,128)(2,1)S(1)}, bf16[192,256]{1,0:T(8,12...) custom-call(bf16[1024,128]{1,0:T(8,128)(2,1)S(1)} %get-tuple-element.44.field_ref, ...), custom_call_target="tpu_custom_call" | custom-call | bytes 5251072 | tf_op jit(solution)/shard_map/pallas_call | solution.py:664
  28.8 0.1 collective-permute-start.2
  28.9 4.8 %collective-permute-start.3 = (bf16[160,256]{1,0:T(8,128)(2,1)S(1)}, bf16[160,256]{1,0:T(8,128)(2,1)S(1)}, u32[]{:S(2)}, u32[]{:S(2)}) collective-permute-start(bf16[160,256]{1,0:T(8,128)(2,1)S(1)} %get-tuple-element.50), channel_id=1, source_target_pairs={{0,124},{1,125},{2,126},{3,127},{4,0},{5,1},{6,2},{7,3},{8,4},{9,5... | collective-permute-start | bytes 245768 | tf_op jit(solution)/shard_map/ppermute | solution.py:681
  33.6 0.0 copy-done
  33.6 0.0 copy-done.1
  33.6 1.9 %shard_map.143 = (bf16[512,256]{1,0:T(8,128)(2,1)S(1)}, f32[1024,256]{1,0:T(8,128)S(1)}, bf16[384,1152]{1,0:T(8,128)(2,1)S(1)}, bf16[384,1152]{1,0:T(8,128)(2,1)S(1)}, bf16[64,384]{1,0:T(8,128)(2,1)S(1)}) custom-call(bf16[2816,256]{1,0:T(8,128)(2,1)S(1)} %get-tuple-element.43.bank_ref.early_ref, bf16[2880,256]{1,0:T(8,128)(2,1)S(1)} %get-tuple-element.52.middle_ref, ...), custom_call_target="tpu_custom_call" | custom-call | flops 1000000000 | bytes 7186432 | tf_op jit(solution)/shard_map/pallas_call | solution.py:664
  35.5 0.0 collective-permute-done.2.prev_ref
  35.6 0.0 collective-permute-done.3.next_ref
  35.6 3.7 %shard_map.142 = (bf16[4,18,16,768]{3,2,1,0:T(8,128)(2,1)S(1)}, bf16[1024,256]{1,0:T(8,128)(2,1)S(1)}, bf16[1024,256]{1,0:T(8,128)(2,1)S(1)}, bf16[192,256]{1,0:...) custom-call(bf16[1024,256]{1,0:T(8,128)(2,1)S(1)} %get-tuple-element.47.hid_r, ...), custom_call_target="tpu_custom_call" | custom-call | bytes 10199040 | tf_op jit(solution)/shard_map/pallas_call | solution.py:664
  39.2 0.3 collective-permute-start.4
  39.5 4.8 %collective-permute-start.5 = (bf16[160,256]{1,0:T(8,128)(2,1)S(1)}, bf16[160,256]{1,0:T(8,128)(2,1)S(1)}, u32[]{:S(2)}, u32[]{:S(2)}) collective-permute-start(bf16[160,256]{1,0:T(8,128)(2,1)S(1)} %get-tuple-element.56), channel_id=1, source_target_pairs={{0,124},{1,125},{2,126},{3,127},{4,0},{5,1},{6,2},{7,3},{8,4},{9,5... | collective-permute-start | bytes 245768 | tf_op jit(solution)/shard_map/ppermute | solution.py:681
  44.3 2.1 %shard_map.144.part_ref = f32[768,128]{1,0:T(8,128)S(1)} custom-call(bf16[4,18,16,768]{3,2,1,0:T(8,128)(2,1)S(1)} %get-tuple-element.61.filled_ref, bf16[1024,256]{1,0:T(8,128)(2,1)S(1)} %get-tuple-element.62.grad_ref, bf16[2880,256]{1,0:T(8,128)(2,1)S(1)} %get-tuple-element.52.middle_ref, bf16[384,1152]{1,0:T(8,128)(2,1)S(1)} %get-tuple-element.63.pick_ref), custom_call_target="tpu_custom_call" | custom-call | flops 2000000000 | bytes 5046272 | tf_op jit(solution)/shard_map/pallas_call | solution.py:664
  46.4 0.0 collective-permute-done.4.prev_ref
  46.4 0.0 collective-permute-done.5.next_ref
  46.4 0.0 copy-start.3
  46.4 0.0 copy-start.4
  46.4 3.7 %shard_map.145 = (bf16[32,40,128]{2,1,0:T(8,128)(2,1)}, bf16[18,16,768]{2,1,0:T(8,128)(2,1)S(1)}, bf16[1024,256]{1,0:T(8,128)(2,1)S(1)}) custom-call(bf16[1024,256]{1,0:T(8,128)(2,1)S(1)} %get-tuple-element.53.hid_two_ref, bf16[192,256]{1,0:T(8,128)(2,1)S(1)} %get-tuple-element.54.local_ref, bf16[160,256]{1,0:T(8,128)(2,1)S(1)} %collective-permute-done.4.prev_ref, ...), custom_call_target="tpu_custom_call" | custom-call | bytes 8822784 | tf_op jit(solution)/shard_map/pallas_call | solution.py:664
  50.1 6.1 %all-to-all-start.1 = ((bf16[32,40,128]{2,1,0:T(8,128)(2,1)}), bf16[32,40,128]{2,1,0:T(8,128)(2,1)S(1)}, u32[]{:S(2)}, u32[]{:S(2)}) async-start(bf16[32,40,128]{2,1,0:T(8,128)(2,1)} %get-tuple-element.74), calls=%async_computation.1 | async-start | bytes 655360 | tf_op jit(solution)/shard_map/all_to_all | solution.py:768
  56.3 0.0 copy-done.3
  56.3 0.0 copy-done.4
  56.3 0.0 copy-start.2
  56.3 3.0 %shard_map.146 = (bf16[16,256]{1,0:T(8,128)(2,1)}, f32[256,128]{1,0:T(8,128)S(1)}, bf16[80,128]{1,0:T(8,128)(2,1)S(1)}, bf16[80,128]{1,0:T(8,128)(2,1)S(1)}, bf16[96,128]{1,0:T(8,128)(2,1)S(1)}) custom-call(bf16[18,16,768]{2,1,0:T(8,128)(2,1)S(1)} %get-tuple-element.66.mine_ref, bf16[1024,256]{1,0:T(8,128)(2,1)S(1)} %get-tuple-element.67.grad_ref, ...), custom_call_target="tpu_custom_call" | custom-call | flops 2000000000 | bytes 2622464 | tf_op jit(solution)/shard_map/pallas_call | solution.py:664
  59.3 4.6 %collective-permute-start.6 = (bf16[80,128]{1,0:T(8,128)(2,1)S(1)}, bf16[80,128]{1,0:T(8,128)(2,1)S(1)}, u32[]{:S(2)}, u32[]{:S(2)}) collective-permute-start(bf16[80,128]{1,0:T(8,128)(2,1)S(1)} %get-tuple-element.70), channel_id=1, source_target_pairs={{0,124},{1,125},{2,126},{3,127},{4,0},{5,1},{6,2},{7,3},{8,4},{9,5... | collective-permute-start | bytes 61448 | tf_op jit(solution)/shard_map/ppermute | solution.py:681
  63.9 0.0 collective-permute-start.7
  63.9 2.3 %all-to-all-done.1.spread_ref = bf16[32,40,128]{2,1,0:T(8,128)(2,1)S(1)} async-done(((bf16[32,40,128]{2,1,0:T(8,128)(2,1)}), bf16[32,40,128]{2,1,0:T(8,128)(2,1)S(1)}, u32[]{:S(2)}, u32[]{:S(2)}) %all-to-all-start.1) | async-done | bytes 327712 | tf_op jit(solution)/shard_map/all_to_all | solution.py:768
  66.2 0.7 shard_map.147
  66.8 0.0 collective-permute-done.6.next_ref
  66.8 3.7 %collective-permute-done.7.prev_ref = bf16[80,128]{1,0:T(8,128)(2,1)S(1)} collective-permute-done((bf16[80,128]{1,0:T(8,128)(2,1)S(1)}, bf16[80,128]{1,0:T(8,128)(2,1)S(1)}, u32[]{:S(2)}, u32[]{:S(2)}) %collective-permute-start.7) | collective-permute-done | bytes 20512 | tf_op jit(solution)/shard_map/ppermute | solution.py:681
  70.5 0.0 copy-done.2
  70.5 1.1 %shard_map.148 = (f32[16,256]{1,0:T(8,128)S(1)}, f32[8,256]{1,0:T(8,128)S(1)}, f32[1,4608]{1,0:T(1,128)}, f32[1,288]{1,0:T(1,128)}) custom-call(f32[256,128]{1,0:T(8,128)S(1)} %get-tuple-element.69.dx_ref, bf16[80,128]{1,0:T(8,128)(2,1)S(1)} %collective-permute-done.6.next_ref, bf16[80,128]{1,0:T(8,128)(2,1)S(1)} %collective-permute-done.7.prev_ref, ...), custom_call_target="tpu_custom_call" | custom-call | bytes 523392 | tf_op jit(solution)/shard_map/pallas_call | solution.py:664
  71.6 0.1 collective-permute-start.8
  71.7 9.7 %all-to-all-start.2 = ((bf16[16,16,128]{2,1,0:T(8,128)(2,1)}), bf16[16,16,128]{2,1,0:T(8,128)(2,1)S(1)}, u32[]{:S(2)}, u32[]{:S(2)}) async-start(bf16[16,16,128]{2,1,0:T(8,128)(2,1)} %get-tuple-element.78), calls=%async_computation.2 | async-start | bytes 131072 | tf_op jit(solution)/shard_map/all_to_all | solution.py:785
  81.4 0.0 collective-permute-done.8
  81.4 0.6 add_bitcast_fusion
  82.0 6.7 %all-to-all-done.2 = bf16[16,16,128]{2,1,0:T(8,128)(2,1)S(1)} async-done(((bf16[16,16,128]{2,1,0:T(8,128)(2,1)}), bf16[16,16,128]{2,1,0:T(8,128)(2,1)S(1)}, u32[]{:S(2)}, u32[]{:S(2)}) %all-to-all-start.2) | async-done | bytes 65568 | tf_op jit(solution)/shard_map/all_to_all | solution.py:785
  88.8 1.1 %shard_map.149 = f32[216,256]{1,0:T(8,128)} custom-call(bf16[256,128]{1,0:T(8,128)(2,1)S(1)} %bitcast.25, bf16[512,256]{1,0:T(8,128)(2,1)S(1)} %get-tuple-element.73.bank_ref), custom_call_target="tpu_custom_call" | custom-call | bytes 548864 | tf_op jit(solution)/shard_map/pallas_call | solution.py:664
  (1 shorter events, 0.0 us)
Async XLA Ops:
  2.0 11.6 %all-to-all-start = ((bf16[8,32,256]{2,1,0:T(8,128)(2,1)}), bf16[8,32,256]{2,1,0:T(8,128)(2,1)S(1)}, u32[]{:S(2)}, u32[]{:S(2)}) async-start(bf16[8,32,256]{2,1,0:T(8,128)(2,1)} %shard_map.137), calls=%async_computation | async-start | bytes 262144 | tf_op jit(solution)/shard_map/all_to_all | solution.py:696
  14.1 8.6 %collective-permute-start.1 = (bf16[80,128]{1,0:T(8,128)(2,1)S(1)}, bf16[80,128]{1,0:T(8,128)(2,1)S(1)}, u32[]{:S(2)}, u32[]{:S(2)}) collective-permute-start(bf16[80,128]{1,0:T(8,128)(2,1)S(1)} %get-tuple-element.81), channel_id=1, source_target_pairs={{0,124},{1,125},{2,126},{3,127},{4,0},{5,1},{6,2},{7,3},{8,4},{9,5... | collective-permute-start | bytes 61448 | tf_op jit(solution)/shard_map/ppermute | solution.py:681
  21.5 6.0 %collective-permute-start = (bf16[80,128]{1,0:T(8,128)(2,1)S(1)}, bf16[80,128]{1,0:T(8,128)(2,1)S(1)}, u32[]{:S(2)}, u32[]{:S(2)}) collective-permute-start(bf16[80,128]{1,0:T(8,128)(2,1)S(1)} %get-tuple-element.82), channel_id=1, source_target_pairs={{0,4},{1,5},{2,6},{3,7},{4,8},{5,9},{6,10},{7,11},{8,12},{9,13},{1... | collective-permute-start | bytes 61448 | tf_op jit(solution)/shard_map/ppermute | solution.py:681
  22.7 11.0 %copy-start = (s32[1,216,64]{1,2,0:T(8,128)S(1)}, s32[1,216,64]{1,2,0:T(8,128)}, u32[]{:S(2)}) copy-start(s32[1,216,64]{1,2,0:T(8,128)} %param.17) | copy-start | bytes 165892
  22.7 10.9 %copy-start.1 = (s32[1,2304,4]{1,2,0:T(4,128)S(1)}, s32[1,2304,4]{1,2,0:T(4,128)}, u32[]{:S(2)}) copy-start(s32[1,2304,4]{1,2,0:T(4,128)} %param.19) | copy-start | bytes 110596
  28.8 6.8 %collective-permute-start.2 = (bf16[160,256]{1,0:T(8,128)(2,1)S(1)}, bf16[160,256]{1,0:T(8,128)(2,1)S(1)}, u32[]{:S(2)}, u32[]{:S(2)}) collective-permute-start(bf16[160,256]{1,0:T(8,128)(2,1)S(1)} %get-tuple-element.49), channel_id=1, source_target_pairs={{0,4},{1,5},{2,6},{3,7},{4,8},{5,9},{6,10},{7,11},{8,12},{9,13},{1... | collective-permute-start | bytes 245768 | tf_op jit(solution)/shard_map/ppermute | solution.py:681
  28.9 6.7 %collective-permute-start.3 = (bf16[160,256]{1,0:T(8,128)(2,1)S(1)}, bf16[160,256]{1,0:T(8,128)(2,1)S(1)}, u32[]{:S(2)}, u32[]{:S(2)}) collective-permute-start(bf16[160,256]{1,0:T(8,128)(2,1)S(1)} %get-tuple-element.50), channel_id=1, source_target_pairs={{0,124},{1,125},{2,126},{3,127},{4,0},{5,1},{6,2},{7,3},{8,4},{9,5... | collective-permute-start | bytes 245768 | tf_op jit(solution)/shard_map/ppermute | solution.py:681
  39.2 7.2 %collective-permute-start.4 = (bf16[160,256]{1,0:T(8,128)(2,1)S(1)}, bf16[160,256]{1,0:T(8,128)(2,1)S(1)}, u32[]{:S(2)}, u32[]{:S(2)}) collective-permute-start(bf16[160,256]{1,0:T(8,128)(2,1)S(1)} %get-tuple-element.55), channel_id=1, source_target_pairs={{0,4},{1,5},{2,6},{3,7},{4,8},{5,9},{6,10},{7,11},{8,12},{9,13},{1... | collective-permute-start | bytes 245768 | tf_op jit(solution)/shard_map/ppermute | solution.py:681
  39.5 6.9 %collective-permute-start.5 = (bf16[160,256]{1,0:T(8,128)(2,1)S(1)}, bf16[160,256]{1,0:T(8,128)(2,1)S(1)}, u32[]{:S(2)}, u32[]{:S(2)}) collective-permute-start(bf16[160,256]{1,0:T(8,128)(2,1)S(1)} %get-tuple-element.56), channel_id=1, source_target_pairs={{0,124},{1,125},{2,126},{3,127},{4,0},{5,1},{6,2},{7,3},{8,4},{9,5... | collective-permute-start | bytes 245768 | tf_op jit(solution)/shard_map/ppermute | solution.py:681
  46.4 9.8 %copy-start.3 = (bf16[1,16,256]{2,1,0:T(8,128)(2,1)S(1)}, bf16[1,16,256]{2,1,0:T(8,128)(2,1)}, u32[]{:S(2)}) copy-start(bf16[1,16,256]{2,1,0:T(8,128)(2,1)} %param.10) | copy-start | bytes 24580
  46.4 9.8 %copy-start.4 = (s32[256]{0:T(256)S(1)}, s32[256]{0:T(256)}, u32[]{:S(2)}) copy-start(s32[256]{0:T(256)} %param.12) | copy-start | bytes 3076
  50.1 16.1 %all-to-all-start.1 = ((bf16[32,40,128]{2,1,0:T(8,128)(2,1)}), bf16[32,40,128]{2,1,0:T(8,128)(2,1)S(1)}, u32[]{:S(2)}, u32[]{:S(2)}) async-start(bf16[32,40,128]{2,1,0:T(8,128)(2,1)} %get-tuple-element.74), calls=%async_computation.1 | async-start | bytes 655360 | tf_op jit(solution)/shard_map/all_to_all | solution.py:768
  56.3 14.3 %copy-start.2 = (bf16[1,16,256]{2,1,0:T(8,128)(2,1)S(1)}, bf16[1,16,256]{2,1,0:T(8,128)(2,1)}, u32[]{:S(2)}) copy-start(bf16[1,16,256]{2,1,0:T(8,128)(2,1)} %param.11) | copy-start | bytes 24580
  59.3 7.6 %collective-permute-start.6 = (bf16[80,128]{1,0:T(8,128)(2,1)S(1)}, bf16[80,128]{1,0:T(8,128)(2,1)S(1)}, u32[]{:S(2)}, u32[]{:S(2)}) collective-permute-start(bf16[80,128]{1,0:T(8,128)(2,1)S(1)} %get-tuple-element.70), channel_id=1, source_target_pairs={{0,124},{1,125},{2,126},{3,127},{4,0},{5,1},{6,2},{7,3},{8,4},{9,5... | collective-permute-start | bytes 61448 | tf_op jit(solution)/shard_map/ppermute | solution.py:681
  63.9 6.6 %collective-permute-start.7 = (bf16[80,128]{1,0:T(8,128)(2,1)S(1)}, bf16[80,128]{1,0:T(8,128)(2,1)S(1)}, u32[]{:S(2)}, u32[]{:S(2)}) collective-permute-start(bf16[80,128]{1,0:T(8,128)(2,1)S(1)} %get-tuple-element.71), channel_id=1, source_target_pairs={{0,4},{1,5},{2,6},{3,7},{4,8},{5,9},{6,10},{7,11},{8,12},{9,13},{1... | collective-permute-start | bytes 61448 | tf_op jit(solution)/shard_map/ppermute | solution.py:681
  71.6 9.8 %collective-permute-start.8 = (f32[8,256]{1,0:T(8,128)S(1)}, f32[8,256]{1,0:T(8,128)S(1)}, u32[]{:S(2)}, u32[]{:S(2)}) collective-permute-start(f32[8,256]{1,0:T(8,128)S(1)} %get-tuple-element.77), channel_id=1, source_target_pairs={{0,128},{128,0},{1,129},{129,1},{2,130},{130,2},{3,131},{131,3},{4... | collective-permute-start | bytes 24584 | tf_op jit(solution)/shard_map/ppermute | solution.py:792
  71.7 17.1 %all-to-all-start.2 = ((bf16[16,16,128]{2,1,0:T(8,128)(2,1)}), bf16[16,16,128]{2,1,0:T(8,128)(2,1)S(1)}, u32[]{:S(2)}, u32[]{:S(2)}) async-start(bf16[16,16,128]{2,1,0:T(8,128)(2,1)} %get-tuple-element.78), calls=%async_computation.2 | async-start | bytes 131072 | tf_op jit(solution)/shard_map/all_to_all | solution.py:785
